TPU v7x, 32 devices: a whole 2x2x4 slice. The times are simulated.
32 devices in a mesh: gz: 8 (over y, x, core), xy: 4 (over z).
Axes of the slice: x: 2, y: 2, z: 4, core: 2. Of those that a mesh axis runs over, the one named last changes fastest.
Arguments:
- east_velocity: float32 [512, 64, 512], P('xy', 'gz'), may hold values from -6 to 6
- north_velocity: float32 [512, 64, 512], P('xy', 'gz'), may hold values from -6 to 6
- upward_velocity: float32 [512, 64, 512], P('xy', 'gz'), may hold values from -5 to 5
- obstacle: int32 [512, 64, 512], P('xy', 'gz'), may hold values 0 or 1
Outputs:
- east_corrected: float32 [512, 64, 512], P('xy', 'gz')
- north_corrected: float32 [512, 64, 512], P('xy', 'gz')
- upward_corrected: float32 [512, 64, 512], P('xy', 'gz')
- pressure: float32 [512, 64, 512], P('xy', 'gz')
- residual: float32 [512, 64, 512], P('xy', 'gz')
All inputs are finite; a program needn't handle non-finite values. No bound on the sum of `obstacle` on one device may be relied on, other than what follows from the above.
Results may differ from a plain program's by a relative error of at most 0.0003.
Values sent between devices are 32-bit elements; how exact they have to be, the bound alone decides.
No kernel may reach another device: no remote copies, remote signals or barrier semaphores. Data moves between devices by JAX's collectives and lax.ppermute only.
A program may use at most 128 MiB of HBM per device.

v0:
```python
import jax
import jax.numpy as jnp
from jax import lax
from jax.sharding import PartitionSpec as P

NX = 512
NY = 512
CZ = 8


HIGH = lax.Precision.HIGHEST


def extended(block, sides, width):
    for axis, dim in sides:
        count = lax.axis_size(axis)
        forward = [(i, i + 1) for i in range(count - 1)]
        forward.append((count - 1, 0))
        backward = [(target, source) for source, target in forward]
        low = lax.ppermute(
            lax.slice_in_dim(block, block.shape[dim] - width, None, axis=dim), axis, forward
        )
        high = lax.ppermute(lax.slice_in_dim(block, 0, width, axis=dim), axis, backward)
        block = jnp.concatenate([low, block, high], axis=dim)
    return block


def hartley(length):
    index = jnp.arange(length, dtype=jnp.int32)
    product = index[:, None] * index[None, :] % length
    angle = 2.0 * jnp.pi / length * product.astype(jnp.float32)
    return jnp.cos(angle) + jnp.sin(angle)


def eigenvalues(length):
    index = jnp.arange(length, dtype=jnp.int32).astype(jnp.float32)
    return 2.0 - 2.0 * jnp.cos(2.0 * jnp.pi / length * index)


def tridiagonal(diagonal, right):
    start = jnp.zeros_like(right[0])

    def forward(carry, plane):
        ratio, value = carry
        divisor = diagonal + ratio
        ratio_new = -1.0 / divisor
        value_new = (plane + value) / divisor
        return ((ratio_new, value_new), (ratio_new, value_new))

    _, (ratios, values) = lax.scan(forward, (start, start), right)

    def backward(after, pair):
        ratio, value = pair
        solution = value - ratio * after
        return (solution, solution)

    _, solved = lax.scan(backward, start, (ratios, values), reverse=True)
    return solved


def interface_chain(bottoms, tops, couple, spread):
    start = jnp.zeros_like(bottoms[0] * couple)

    def forward(carry, pair):
        slope, offset = carry
        bottom, top = pair
        divisor = 1.0 - couple * slope
        slope_new = couple + spread * spread * slope / divisor
        offset_new = top + spread * offset + spread * slope * (bottom + couple * offset) / divisor
        return ((slope_new, offset_new), (slope, offset))

    _, (slopes, offsets) = lax.scan(forward, (start, start), (bottoms, tops))

    def backward(above, items):
        slope, offset, bottom, top = items
        lower = (bottom + couple * offset + spread * above) / (1.0 - couple * slope)
        upper = top + spread * (slope * lower + offset) + couple * above
        return (lower, (lower, upper))

    _, (lowers, uppers) = lax.scan(backward, start, (slopes, offsets, bottoms, tops), reverse=True)
    return (lowers, uppers)


def local(east_velocity, north_velocity, upward_velocity, obstacle):
    groups = lax.axis_size("xy")
    slabs = lax.axis_size("gz")
    east_rows = NX // groups
    north_rows = NY // groups
    group_index = lax.axis_index("xy")
    slab_index = lax.axis_index("gz")
    first_slab = slab_index == 0
    last_slab = slab_index == slabs - 1
    fluid = (1 - obstacle).astype(jnp.float32)
    stacked = jnp.stack([east_velocity, upward_velocity, fluid])
    framed = extended(stacked, (("gz", 2), ("xy", 1)), 1)
    inner = framed[:, :, 1:-1]
    east_next = inner[0, -1]
    fluid_west = inner[2, 0]
    fluid_east = inner[2, -1]
    column = framed[:, 1:-1]
    upward_above = jnp.where(last_slab, 0.0, column[1, :, -1])
    fluid_below = jnp.where(first_slab, 1.0, column[2, :, 0])
    fluid_above = jnp.where(last_slab, 0.0, column[2, :, -1])
    open_east = fluid * jnp.concatenate([fluid_west[None], fluid[:-1]], 0)
    open_north = fluid * jnp.roll(fluid, 1, 2)
    open_up = fluid * jnp.concatenate([fluid_below[:, None], fluid[:, :-1]], 1)
    east_masked = open_east * east_velocity
    north_masked = open_north * north_velocity
    upward_masked = open_up * upward_velocity
    east_after = jnp.concatenate([east_masked[1:], (east_next * fluid_east * fluid[-1])[None]], 0)
    upward_after = jnp.concatenate(
        [upward_masked[:, 1:], (upward_above * fluid_above * fluid[:, -1])[:, None]], 1
    )
    source = (
        east_masked
        - east_after
        + (north_masked - jnp.roll(north_masked, -1, 2))
        + (upward_masked - upward_after)
    )
    table_east = hartley(NX).reshape(groups, east_rows, NX)
    table_north = hartley(NY).reshape(groups, north_rows, NY)
    sorted_modes = jnp.einsum("xzy,gky->gxzk", source, table_north, precision=HIGH).reshape(
        groups, east_rows, CZ * north_rows
    )
    received = lax.all_to_all(sorted_modes, "xy", split_axis=0, concat_axis=0, tiled=True)
    spectrum = jnp.einsum("gxm,gxa->ma", received, table_east, precision=HIGH).reshape(
        CZ, north_rows, NX
    )
    north_modes = group_index * north_rows + jnp.arange(north_rows, dtype=jnp.int32)
    north_eigen = 2.0 - 2.0 * jnp.cos(2.0 * jnp.pi / NY * north_modes.astype(jnp.float32))
    diagonal = 2.0 + north_eigen[:, None] + eigenvalues(NX)[None, :]
    unit = jnp.broadcast_to(
        (jnp.arange(CZ) == 0).astype(jnp.float32)[:, None, None], spectrum.shape
    )
    solved = tridiagonal(diagonal, jnp.stack([spectrum, unit], 1))
    local_part = solved[:, 0]
    spike = solved[:, 1]
    couple = spike[0]
    spread = spike[-1]
    ends = jnp.stack([local_part[0], local_part[-1]])
    everything = lax.all_gather(ends[None], "gz", axis=0, tiled=True)
    lowers, uppers = interface_chain(everything[:, 0], everything[:, 1], couple, spread)
    blank = jnp.zeros_like(couple)
    below_all = jnp.concatenate([blank[None], uppers[:-1]], 0)
    above_all = jnp.concatenate([lowers[1:], blank[None]], 0)
    top_below = lax.dynamic_index_in_dim(below_all, slab_index, 0, keepdims=False)
    bottom_above = lax.dynamic_index_in_dim(above_all, slab_index, 0, keepdims=False)
    pressure_modes = local_part + spike * top_below + jnp.flip(spike, 0) * bottom_above
    back_sorted = jnp.einsum("zka,gxa->gxzk", pressure_modes, table_east, precision=HIGH).reshape(
        groups, east_rows, CZ * north_rows
    )
    returned_modes = lax.all_to_all(
        back_sorted, "xy", split_axis=0, concat_axis=0, tiled=True
    ).reshape(groups, east_rows, CZ, north_rows)
    pressure = jnp.einsum("gxzk,gky->xzy", returned_modes, table_north, precision=HIGH) * (
        1.0 / (NX * NY)
    )
    framed_pressure = extended(pressure, (("gz", 1), ("xy", 0)), 1)
    pressure_west = framed_pressure[0, 1:-1]
    pressure_east = framed_pressure[-1, 1:-1]
    pressure_below = jnp.where(first_slab, 0.0, framed_pressure[1:-1, 0])
    pressure_above = framed_pressure[1:-1, -1]
    west_full = jnp.concatenate([pressure_west[None], pressure[:-1]], 0)
    east_full = jnp.concatenate([pressure[1:], pressure_east[None]], 0)
    below_full = jnp.concatenate([pressure_below[:, None], pressure[:, :-1]], 1)
    above_full = jnp.concatenate([pressure[:, 1:], pressure_above[:, None]], 1)
    open_east_after = fluid * jnp.concatenate([fluid[1:], fluid_east[None]], 0)
    open_north_after = jnp.roll(open_north, -1, 2)
    open_up_after = fluid * jnp.concatenate([fluid[:, 1:], fluid_above[:, None]], 1)
    applied = (
        open_east * (pressure - west_full)
        + open_east_after * (pressure - east_full)
        + open_north * (pressure - jnp.roll(pressure, 1, 2))
        + open_north_after * (pressure - jnp.roll(pressure, -1, 2))
        + open_up * (pressure - below_full)
        + open_up_after * (pressure - above_full)
    )
    residual = source - applied
    east_corrected = open_east * (east_velocity - (pressure - west_full))
    north_corrected = open_north * (north_velocity - (pressure - jnp.roll(pressure, 1, 2)))
    upward_corrected = open_up * (upward_velocity - (pressure - below_full))
    return (east_corrected, north_corrected, upward_corrected, pressure, residual)


def solution(mesh):
    placed = (P("xy", "gz", None), P("xy", "gz", None), P("xy", "gz", None), P("xy", "gz", None))
    return jax.shard_map(
        local,
        mesh=mesh,
        in_specs=placed,
        out_specs=(
            P("xy", "gz", None),
            P("xy", "gz", None),
            P("xy", "gz", None),
            P("xy", "gz", None),
            P("xy", "gz", None),
        ),
        check_vma=False,
    )
```

profile of v0, /device:TPU:1, one launch (start us, length us, event | category | flops | bytes accessed | tf_op | source)
XLA Modules:
  0.0 402.1 jit_solution(10857530930627547049)
XLA Ops:
  7.2 3.0 fusion.87
  10.3 2.4 copy_bitcast_fusion
  15.2 2.6 collective-permute-start
  21.2 13.4 %collective-permute-done.1 = f32[3,128,1,512]{3,1,2,0:T(8,128)S(1)} collective-permute-done((f32[3,128,1,512]{3,1,2,0:T(8,128)}, f32[3,128,1,512]{3,1,2,0:T(8,128)S(1)}, u32[]{:S(2)}, u32[]{:S(2)}) %collective-permute-start.1) | collective-permute-done | bytes 786464 | tf_op jit(solution)/shard_map/ppermute | solution.py:23
  41.1 6.7 %copy_multiply_fusion.1 = (f32[128,8,512]{2,0,1:T(8,128)S(1)}, f32[128,8,512]{2,0,1:T(8,128)S(1)}, f32[128,8,512]{2,0,1:T(8,128)S(1)}, f32[128,8,512]{2,0,1:T(8,128)}) fusion(f32[128,8,512]{2,1,0:T(8,128)S(1)} %copy-done.9, f32[128,7,512]{2,0,1:T(8,128)S(1)} %get-tuple-element.694, f32[128,1,512]{2,0,1:T(8,128)S(1)} %fusion.68, ...), kind=kLoop, calls=%fused_computation.79 | loop fusion | flops 5767168 | bytes 23068672 | tf_op jit(solution)/shard_map/mul | solution.py:109
  50.9 9.1 %fusion.30 = f32[4,128,128,8]{2,1,3,0:T(8,128)} fusion(f32[128,8,512]{2,0,1:T(8,128)S(1)} %fusion.21, s32[4,128]{1,0:T(4,128)S(1)} %multiply_add_fusion), kind=kOutput, calls=%fused_computation.68 | convolution fusion | flops 3225157632 | bytes 4196352 | tf_op jit(solution)/shard_map/xzy,gky->gxzk/dot_general | solution.py:122
  60.0 4.4 %all-to-all-start = ((f32[4,128,1024]{1,2,0:T(8,128)}), f32[4,128,1024]{1,2,0:T(8,128)}, u32[]{:S(2)}, u32[]{:S(2)}) async-start(f32[4,128,1024]{1,2,0:T(8,128)} %bitcast.14), calls=%async_computation | async-start | bytes 4194304 | tf_op jit(solution)/shard_map/all_to_all | solution.py:125
  64.8 47.4 %all-to-all-done = f32[4,128,1024]{1,2,0:T(8,128)} async-done(((f32[4,128,1024]{1,2,0:T(8,128)}), f32[4,128,1024]{1,2,0:T(8,128)}, u32[]{:S(2)}, u32[]{:S(2)}) %all-to-all-start) | async-done | bytes 2097184 | tf_op jit(solution)/shard_map/all_to_all | solution.py:125
  112.3 9.2 %convolution_bitcast_fusion = f32[8,1,128,512]{3,2,0,1:T(8,128)S(1)} fusion(f32[8,128,4,128]{3,1,0,2:T(8,128)} %bitcast.16, s32[4,128]{1,0:T(4,128)S(1)} %multiply_add_fusion), kind=kOutput, calls=%fused_computation.83 | convolution fusion | flops 3225157632 | bytes 4196352 | tf_op jit(solution)/shard_map/gxm,gxa->ma/dot_general | solution.py:126
  121.8 2.8 pad_maximum_fusion
  124.6 2.5 broadcast.311.clone
  127.1 2.5 broadcast.311.clone.1
  129.6 20.7 %while.71 = (s32[]{:T(128)}, f32[2,128,512]{2,1,0:T(8,128)S(1)}, f32[2,128,512]{2,1,0:T(8,128)S(1)}, f32[8,2,128,512]{3,2,1,0:T(8,128)}, f32[8,2,128,512]{3,2,1,...) while((s32[]{:T(128)}, f32[2,128,512]{2,1,0:T(8,128)S(1)}, ...), condition=%wide.region_1.2_spmd.clone, body=%wide.region_0.1_spmd.clone.sunk | while | flops 851971 | bytes 4197487 | solution.py:50
  130.1 2.4 bitcast_dynamic-update-slice_fusion.12
  132.7 2.5 bitcast_dynamic-update-slice_fusion.12
  135.2 2.5 bitcast_dynamic-update-slice_fusion.12
  137.8 2.4 bitcast_dynamic-update-slice_fusion.12
  140.3 2.5 bitcast_dynamic-update-slice_fusion.12
  147.9 2.4 bitcast_dynamic-update-slice_fusion.12
  150.4 2.6 broadcast.311
  153.0 19.7 %while.72 = (s32[]{:T(128)}, f32[2,128,512]{2,1,0:T(8,128)S(1)}, f32[8,2,128,512]{3,2,1,0:T(8,128)}, f32[8,2,128,512]{3,2,1,0:T(8,128)}, f32[8,2,128,512]{3,2,1,0:T(8,128)}, /*index=5*/s32[]{:T(128)}, s32[]{:T(128)}, s32[]{:T(128)}) while((s32[]{:T(128)}, f32[2,128,512]{2,1,0:T(8,128)S(1)}, f32[8,2,128,512]{3,2,1,0:T(8,128)}, ...), condition=%wide.region_3.4_spmd.clone, body=%wide.region_2.3_spmd.clone.sunk | while | flops 393220 | bytes 2621551 | solution.py:57
  153.0 2.4 bitcast_dynamic-update-slice_fusion.13
  155.4 2.5 bitcast_dynamic-update-slice_fusion.13
  157.9 2.5 bitcast_dynamic-update-slice_fusion.13
  160.4 2.5 bitcast_dynamic-update-slice_fusion.13
  162.8 2.4 bitcast_dynamic-update-slice_fusion.13
  165.3 2.5 bitcast_dynamic-update-slice_fusion.13
  167.7 2.5 bitcast_dynamic-update-slice_fusion.13
  170.2 2.4 bitcast_dynamic-update-slice_fusion.13
  176.5 3.1 slice_bitcast_fusion.3
  179.6 33.5 %all-gather.3.cloned.1.call-done = f32[16,128,512]{2,1,0:T(8,128)} async-done(((f32[2,128,512]{2,1,0:T(8,128)}), f32[16,128,512]{2,1,0:T(8,128)}) %all-gather.3.cloned.1.call-update) | async-done | bytes 4194320 | tf_op jit(solution)/shard_map/all_gather | solution.py:141
  213.1 4.2 %slice_bitcast_fusion = (f32[8,128,512]{2,1,0:T(8,128)S(1)}, f32[8,128,512]{2,1,0:T(8,128)}) fusion(f32[8,2,128,512]{3,2,1,0:T(8,128)} %bitcast.197), kind=kLoop, calls=%fused_computation.37 | loop fusion | bytes 8388608 | tf_op jit(solution)/shard_map/squeeze | solution.py:142
  220.4 16.9 %while.73 = (s32[]{:T(128)}, f32[128,512]{1,0:T(8,128)S(1)}, f32[128,512]{1,0:T(8,128)S(1)}, f32[8,128,512]{2,1,0:T(8,128)}, f32[8,128,512]{2,1,0:T(8,128)}, /*i...) while((s32[]{:T(128)}, f32[128,512]{1,0:T(8,128)S(1)}, ...), condition=%wide.region_5.6_spmd.clone, body=%wide.region_4.5_spmd.clone.sunk | while | flops 1114115 | bytes 3408516 | solution.py:72
  240.5 22.1 %while.74 = (s32[]{:T(128)}, f32[128,512]{1,0:T(8,128)S(1)}, f32[8,128,512]{2,1,0:T(8,128)}, f32[8,128,512]{2,1,0:T(8,128)}, f32[8,128,512]{2,1,0:T(8,128)}, /*i...) while((s32[]{:T(128)}, f32[128,512]{1,0:T(8,128)S(1)}, ...), condition=%wide.region_7.8_spmd.clone, body=%wide.region_6.7_spmd.clone.sunk | while | flops 917508 | bytes 2883739 | solution.py:80
  268.9 9.3 %fusion.44 = f32[4,128,1024]{2,1,0:T(8,128)} fusion(f32[1024,512,1]{1,0,2:T(8,128)S(1)} %bitcast.198, s32[4,128]{1,0:T(4,128)S(1)} %multiply_add_fusion), kind=kOutput, calls=%fused_computation.99 | convolution fusion | flops 3225157632 | bytes 4196352 | tf_op jit(solution)/shard_map/zka,gxa->gxzk/dot_general | solution.py:149
  278.2 4.7 %all-to-all-start.1 = ((f32[4,128,1024]{2,1,0:T(8,128)}), f32[4,128,1024]{2,1,0:T(8,128)}, u32[]{:S(2)}, u32[]{:S(2)}) async-start(f32[4,128,1024]{2,1,0:T(8,128)} %fusion.44), calls=%async_computation.1 | async-start | bytes 4194304 | tf_op jit(solution)/shard_map/all_to_all | solution.py:152
  286.0 44.9 %all-to-all-done.1 = f32[4,128,1024]{2,1,0:T(8,128)} async-done(((f32[4,128,1024]{2,1,0:T(8,128)}), f32[4,128,1024]{2,1,0:T(8,128)}, u32[]{:S(2)}, u32[]{:S(2)}) %all-to-all-start.1) | async-done | bytes 2097184 | tf_op jit(solution)/shard_map/all_to_all | solution.py:152
  330.9 9.3 %bitcast_multiply_fusion.4 = f32[128,8,512]{2,0,1:T(8,128)S(1)} fusion(s32[4,128]{1,0:T(4,128)S(1)} %multiply_add_fusion, f32[4,128,1024]{2,1,0:T(8,128)} %all-to-all-done.1), kind=kOutput, calls=%fused_computation.67 | convolution fusion | flops 3225681920 | bytes 4196352 | tf_op jit(solution)/shard_map/gxzk,gky->xzy/dot_general | solution.py:155
  345.6 2.5 copy.62
  350.8 4.1 %collective-permute-done.4 = f32[128,1,512]{2,0,1:T(8,128)S(1)} collective-permute-done((f32[128,1,512]{2,0,1:T(8,128)S(1)}, f32[128,1,512]{2,0,1:T(8,128)S(1)}, u32[]{:S(2)}, u32[]{:S(2)}) %collective-permute-start.4) | collective-permute-done | bytes 262176 | tf_op jit(solution)/shard_map/ppermute | solution.py:20
  354.9 3.2 collective-permute-done.5
  358.2 3.3 collective-permute-start.7
  362.7 9.8 %subtract_multiply_fusion = (f32[128,8,512]{2,0,1:T(8,128)}, f32[128,8,512]{2,0,1:T(8,128)}, f32[128,8,512]{2,0,1:T(8,128)}) fusion(f32[128,8,512]{2,1,0:T(8,128)S(1)} %copy-done.10, f32[128,8,512]{2,0,1:T(8,128)S(1)} %bitcast_multiply_fusion.4, f32[128,7,512]{2,0,1:T(8,128)S(1)} %get-tuple-element.692, f32[128,1,512]{2,0,1:T(8,128)S(1)} %broadcast_select_fusion, ...), kind=kLoop, calls=%fused_computation.72 | loop fusion | flops 9437184 | bytes 29360128 | tf_op jit(solution)/shard_map/mul | solution.py:181
  372.5 10.6 %fusion.28 = f32[128,8,512]{2,0,1:T(8,128)} fusion(f32[128,8,512]{2,0,1:T(8,128)} %copy-done.25, f32[1,8,512]{2,0,1:T(1,128)S(1)} %slice_bitcast_fusion.8, f32[127,8,512]{2,0,1:T(8,128)} %get-tuple-element.701, f32[128,8,512]{2,0,1:T(8,128)S(1)} %bitcast_multiply_fusion.4, f32[1,8,512]{2,0,1:T(1,128)S(1)} %slice.247, f32[127,8,512]{2,0,1:T(8,128)} %get-tuple-element.699, ...), kind=kLoop, calls=%fused_computation.60 | loop fusion | flops 18350080 | bytes 33554432 | tf_op jit(solution)/shard_map/sub | solution.py:178
  383.1 4.3 %copy.63 = f32[128,8,512]{2,1,0:T(8,128)} copy(f32[128,8,512]{2,0,1:T(8,128)} %fusion.28) | data formatting | bytes 4194304
  387.4 2.5 copy.59
  389.9 2.5 copy.60
  392.5 2.5 copy.61
  (165 shorter events, 88.9 us)
Async XLA Ops:
  7.2 3.1 copy-start.11
  7.2 3.1 copy-start.8
  10.2 2.5 copy-start.14
  12.7 1.8 copy-start.16
  12.7 2.5 copy-start.18
  15.2 19.5 %collective-permute-start.1 = (f32[3,128,1,512]{3,1,2,0:T(8,128)}, f32[3,128,1,512]{3,1,2,0:T(8,128)S(1)}, u32[]{:S(2)}, u32[]{:S(2)}) collective-permute-start(f32[3,128,1,512]{3,1,2,0:T(8,128)} %get-tuple-element.680), channel_id=1, source_target_pairs={{4,0},{8,4},{12,8},{16,12},{20,16},{24,20},{28,24},{0,28},{5,1},{9... | collective-permute-start | bytes 2359304 | tf_op jit(solution)/shard_map/ppermute | solution.py:23
  15.2 19.5 %collective-permute-start = (f32[3,128,1,512]{3,1,2,0:T(8,128)}, f32[3,128,1,512]{3,1,2,0:T(8,128)}, u32[]{:S(2)}, u32[]{:S(2)}) collective-permute-start(f32[3,128,1,512]{3,1,2,0:T(8,128)} %get-tuple-element.679), channel_id=1, source_target_pairs={{0,4},{4,8},{8,12},{12,16},{16,20},{20,24},{24,28},{28,0},{1,5},{5... | collective-permute-start | bytes 2359304 | tf_op jit(solution)/shard_map/ppermute | solution.py:20
  19.5 21.6 %copy-start.5 = (f32[128,7,512]{2,0,1:T(8,128)}, f32[128,7,512]{2,0,1:T(8,128)S(1)}, u32[]{:S(2)}) copy-start(f32[128,7,512]{2,0,1:T(8,128)S(1)} %get-tuple-element.694) | copy-start | bytes 5505028
  19.5 15.2 %copy-start.15 = (f32[1,128,8,512]{3,1,2,0:T(8,128)S(1)}, f32[1,128,8,512]{3,1,2,0:T(8,128)}, u32[]{:S(2)}) copy-start(f32[1,128,8,512]{3,1,2,0:T(8,128)} %copy-done.14) | copy-start | bytes 6291460
  19.5 15.2 %copy-start.17 = (f32[1,128,8,512]{3,1,2,0:T(8,128)S(1)}, f32[1,128,8,512]{3,1,2,0:T(8,128)}, u32[]{:S(2)}) copy-start(f32[1,128,8,512]{3,1,2,0:T(8,128)} %copy-done.16) | copy-start | bytes 6291460
  19.5 15.2 %copy-start.19 = (f32[1,128,8,512]{3,1,2,0:T(8,128)S(1)}, f32[1,128,8,512]{3,1,2,0:T(8,128)}, u32[]{:S(2)}) copy-start(f32[1,128,8,512]{3,1,2,0:T(8,128)} %copy-done.18) | copy-start | bytes 6291460
  21.2 19.8 %copy-start.3 = (f32[127,8,512]{2,0,1:T(8,128)}, f32[127,8,512]{2,0,1:T(8,128)S(1)}, u32[]{:S(2)}) copy-start(f32[127,8,512]{2,0,1:T(8,128)S(1)} %get-tuple-element.702) | copy-start | bytes 6242308
  34.7 4.9 %copy-start.29 = (f32[3,128,1,512]{3,1,2,0:T(8,128)}, f32[3,128,1,512]{3,1,2,0:T(8,128)S(1)}, u32[]{:S(2)}) copy-start(f32[3,128,1,512]{3,1,2,0:T(8,128)S(1)} %collective-permute-done.1) | copy-start | bytes 2359300
  34.7 6.4 %copy-start.1 = (s32[128,8,512]{2,1,0:T(8,128)S(1)}, s32[128,8,512]{2,1,0:T(8,128)}, u32[]{:S(2)}) copy-start(s32[128,8,512]{2,1,0:T(8,128)} %param.15) | copy-start | bytes 6291460
  34.7 6.4 %copy-start.9 = (f32[128,8,512]{2,1,0:T(8,128)S(1)}, f32[128,8,512]{2,1,0:T(8,128)}, u32[]{:S(2)}) copy-start(f32[128,8,512]{2,1,0:T(8,128)} %param.14) | copy-start | bytes 6291460
  34.7 6.4 %copy-start.12 = (f32[128,8,512]{2,1,0:T(8,128)S(1)}, f32[128,8,512]{2,1,0:T(8,128)}, u32[]{:S(2)}) copy-start(f32[128,8,512]{2,1,0:T(8,128)} %param.12) | copy-start | bytes 6291460
  34.8 6.4 %copy-start.20 = (f32[128,8,512]{2,1,0:T(8,128)S(1)}, f32[128,8,512]{2,1,0:T(8,128)}, u32[]{:S(2)}) copy-start(f32[128,8,512]{2,1,0:T(8,128)} %param.13) | copy-start | bytes 6291460
  36.0 5.1 %collective-permute-start.2 = (f32[3,1,10,512]{3,1,2,0:T(1,128)S(1)}, f32[3,1,10,512]{3,1,2,0:T(1,128)S(1)}, u32[]{:S(2)}, u32[]{:S(2)}) collective-permute-start(f32[3,1,10,512]{3,1,2,0:T(1,128)S(1)} %get-tuple-element.678), channel_id=1, source_target_pairs={{0,1},{1,2},{2,3},{3,0},{4,5},{5,6},{6,7},{7,4},{8,9},{9,10},{10,1... | collective-permute-start | bytes 184328 | tf_op jit(solution)/shard_map/ppermute | solution.py:20
  37.3 11.7 %collective-permute-start.3 = (f32[3,1,10,512]{3,1,2,0:T(1,128)S(1)}, f32[3,1,10,512]{3,1,2,0:T(1,128)S(1)}, u32[]{:S(2)}, u32[]{:S(2)}) collective-permute-start(f32[3,1,10,512]{3,1,2,0:T(1,128)S(1)} %get-tuple-element.677), channel_id=1, source_target_pairs={{1,0},{2,1},{3,2},{0,3},{5,4},{6,5},{7,6},{4,7},{9,8},{10,9},{11,1... | collective-permute-start | bytes 184328 | tf_op jit(solution)/shard_map/ppermute | solution.py:23
  40.6 7.2 %copy-start.27 = (f32[128,1,512]{2,0,1:T(8,128)}, f32[128,1,512]{2,0,1:T(8,128)S(1)}, u32[]{:S(2)}) copy-start(f32[128,1,512]{2,0,1:T(8,128)S(1)} %fusion.68) | copy-start | bytes 786436
  50.9 9.1 %copy-start.25 = (f32[128,8,512]{2,0,1:T(8,128)}, f32[128,8,512]{2,0,1:T(8,128)S(1)}, u32[]{:S(2)}) copy-start(f32[128,8,512]{2,0,1:T(8,128)S(1)} %fusion.21) | copy-start | bytes 6291460
  60.0 52.3 %all-to-all-start = ((f32[4,128,1024]{1,2,0:T(8,128)}), f32[4,128,1024]{1,2,0:T(8,128)}, u32[]{:S(2)}, u32[]{:S(2)}) async-start(f32[4,128,1024]{1,2,0:T(8,128)} %bitcast.14), calls=%async_computation | async-start | bytes 4194304 | tf_op jit(solution)/shard_map/all_to_all | solution.py:125
  64.4 148.6 %all-gather.3.cloned.1.call-start = ((), (), s32[]{:S(2)}) async-start(), calls=%async_computation.2 | async-start | bytes 4718592 | tf_op jit(solution)/shard_map/all_gather | solution.py:141
  264.2 2.1 copy-start.26
  266.0 2.3 copy-start.7
  278.2 5.7 %copy-start = (f32[128,8,512]{2,0,1:T(8,128)S(1)}, f32[128,8,512]{2,0,1:T(8,128)}, u32[]{:S(2)}) copy-start(f32[128,8,512]{2,0,1:T(8,128)} %get-tuple-element.709) | copy-start | bytes 6291460
  278.2 52.7 %all-to-all-start.1 = ((f32[4,128,1024]{2,1,0:T(8,128)}), f32[4,128,1024]{2,1,0:T(8,128)}, u32[]{:S(2)}, u32[]{:S(2)}) async-start(f32[4,128,1024]{2,1,0:T(8,128)} %fusion.44), calls=%async_computation.1 | async-start | bytes 4194304 | tf_op jit(solution)/shard_map/all_to_all | solution.py:152
  344.0 18.6 %copy-start.13 = (f32[128,8,512]{2,1,0:T(8,128)S(1)}, f32[128,8,512]{2,1,0:T(8,128)}, u32[]{:S(2)}) copy-start(f32[128,8,512]{2,1,0:T(8,128)} %param.12) | copy-start | bytes 6291460
  344.0 18.6 %copy-start.21 = (f32[128,8,512]{2,1,0:T(8,128)S(1)}, f32[128,8,512]{2,1,0:T(8,128)}, u32[]{:S(2)}) copy-start(f32[128,8,512]{2,1,0:T(8,128)} %param.13) | copy-start | bytes 6291460
  345.6 17.0 %copy-start.6 = (f32[128,7,512]{2,0,1:T(8,128)S(1)}, f32[128,7,512]{2,0,1:T(8,128)}, u32[]{:S(2)}) copy-start(f32[128,7,512]{2,0,1:T(8,128)} %copy-done.5) | copy-start | bytes 5505028
  345.6 17.0 %copy-start.10 = (f32[128,8,512]{2,1,0:T(8,128)S(1)}, f32[128,8,512]{2,1,0:T(8,128)}, u32[]{:S(2)}) copy-start(f32[128,8,512]{2,1,0:T(8,128)} %param.14) | copy-start | bytes 6291460
  348.1 6.8 %collective-permute-start.4 = (f32[128,1,512]{2,0,1:T(8,128)S(1)}, f32[128,1,512]{2,0,1:T(8,128)S(1)}, u32[]{:S(2)}, u32[]{:S(2)}) collective-permute-start(f32[128,1,512]{2,0,1:T(8,128)S(1)} %get-tuple-element.704), channel_id=1, source_target_pairs={{0,4},{4,8},{8,12},{12,16},{16,20},{20,24},{24,28},{28,0},{1,5},{5... | collective-permute-start | bytes 786440 | tf_op jit(solution)/shard_map/ppermute | solution.py:20
  350.5 7.6 %collective-permute-start.5 = (f32[128,1,512]{2,0,1:T(8,128)S(1)}, f32[128,1,512]{2,0,1:T(8,128)S(1)}, u32[]{:S(2)}, u32[]{:S(2)}) collective-permute-start(f32[128,1,512]{2,0,1:T(8,128)S(1)} %get-tuple-element.705), channel_id=1, source_target_pairs={{4,0},{8,4},{12,8},{16,12},{20,16},{24,20},{28,24},{0,28},{5,1},{9... | collective-permute-start | bytes 786440 | tf_op jit(solution)/shard_map/ppermute | solution.py:23
  350.5 12.1 %copy-start.4 = (f32[127,8,512]{2,0,1:T(8,128)S(1)}, f32[127,8,512]{2,0,1:T(8,128)}, u32[]{:S(2)}) copy-start(f32[127,8,512]{2,0,1:T(8,128)} %copy-done.3) | copy-start | bytes 6242308
  350.7 11.9 %copy-start.2 = (s32[128,8,512]{2,1,0:T(8,128)S(1)}, s32[128,8,512]{2,1,0:T(8,128)}, u32[]{:S(2)}) copy-start(s32[128,8,512]{2,1,0:T(8,128)} %param.15) | copy-start | bytes 6291460
  350.7 11.9 %copy-start.28 = (f32[128,1,512]{2,0,1:T(8,128)S(1)}, f32[128,1,512]{2,0,1:T(8,128)}, u32[]{:S(2)}) copy-start(f32[128,1,512]{2,0,1:T(8,128)} %copy-done.27) | copy-start | bytes 786436
  358.1 4.5 %collective-permute-start.6 = (f32[1,10,512]{2,0,1:T(1,128)S(1)}, f32[1,10,512]{2,0,1:T(1,128)S(1)}, u32[]{:S(2)}, u32[]{:S(2)}) collective-permute-start(f32[1,10,512]{2,0,1:T(1,128)S(1)} %get-tuple-element.690), channel_id=1, source_target_pairs={{0,1},{1,2},{2,3},{3,0},{4,5},{5,6},{6,7},{7,4},{8,9},{9,10},{10,1... | collective-permute-start | bytes 61448 | tf_op jit(solution)/shard_map/ppermute | solution.py:20
  358.2 14.3 %collective-permute-start.7 = (f32[1,10,512]{2,0,1:T(1,128)S(1)}, f32[1,10,512]{2,0,1:T(1,128)S(1)}, u32[]{:S(2)}, u32[]{:S(2)}) collective-permute-start(f32[1,10,512]{2,0,1:T(1,128)S(1)} %get-tuple-element.689), channel_id=1, source_target_pairs={{1,0},{2,1},{3,2},{0,3},{5,4},{6,5},{7,6},{4,7},{9,8},{10,9},{11,1... | collective-permute-start | bytes 61448 | tf_op jit(solution)/shard_map/ppermute | solution.py:23
  383.1 4.3 %copy-start.24 = (f32[128,8,512]{2,0,1:T(8,128)S(1)}, f32[128,8,512]{2,0,1:T(8,128)}, u32[]{:S(2)}) copy-start(f32[128,8,512]{2,0,1:T(8,128)} %get-tuple-element.682) | copy-start | bytes 6291460
  387.4 2.5 copy-start.23
  389.9 2.5 copy-start.22
Sparse Core Ops, SparseCore 0:
  174.9 38.1 all-gather.2
where the time goes:
time: 409 us; the launch traced here: 402 us
  waiting for transfers between devices  148 us (36%)
  other arithmetic  116 us (28%)
  local copies, waits for them, and re-layouts  64.5 us (16%)
  matrix products  36.9 us (9%)
  starting transfers between devices  21.3 us (5%)
  between operations  14.9 us (4%)
    all_to_all x1, waiting for transfers between devices, local(): lax.all_to_all(sorted_modes, 'xy', split_axis=0, concat_axis=0, tiled=True)  47.4 us
    all_to_all x1, waiting for transfers between devices, local(): lax.all_to_all(back_sorted, 'xy', split_axis=0, concat_axis=0, tiled=True)  44.9 us
    dynamic_update_slice x16, other arithmetic, tridiagonal(): _, (ratios, values) = lax.scan(forward, (start, start), right)  39.2 us
    all_gather x1, waiting for transfers between devices, local(): everything = lax.all_gather(ends[None], 'gz', axis=0, tiled=True)  33.5 us
    dynamic_update_slice x16, other arithmetic, interface_chain(): _, (slopes, offsets) = lax.scan(forward, (start, start), (bottoms, tops))  23 us
    unnamed x65, local copies, waits for them, and re-layouts  17.7 us
    ppermute x4, waiting for transfers between devices, extended(): lax.ppermute(lax.slice_in_dim(block, 0, width, axis=dim), axis, backward)  16.7 us
    another operation x7, local copies, waits for them, and re-layouts  14 us
  transfers between devices with their start and end apart: 11, of which 8 were waited for; matrix products, arithmetic and copies ran while one was open for 8% of the time, Pallas kernels for 0%

commit v1 on v0

v1 whole, which is shorter than its diff:
```python
import functools

import jax
import jax.numpy as jnp
import ml_dtypes
import numpy as np
from jax import lax
from jax.experimental import pallas as pl
from jax.experimental.pallas import tpu as pltpu
from jax.sharding import PartitionSpec as P

F32 = jnp.float32
BF16 = jnp.bfloat16
VMEM_LIMIT = 60 * 1024 * 1024


def pair_np(table):
    high = table.astype(np.float32).astype(ml_dtypes.bfloat16)
    low = (table - high.astype(np.float64)).astype(np.float32).astype(ml_dtypes.bfloat16)
    return high, low


def north_tables(length):
    half = length // 2
    cell = np.arange(half)[:, None]
    mode = np.arange(half)[None, :]

    def cas(number):
        angle = 2.0 * np.pi * ((cell * number) % length) / length
        return (np.cos(angle) + np.sin(angle)) / np.sqrt(length)

    numbers = np.concatenate([2 * np.arange(half), 2 * np.arange(half) + 1])
    eigen = 4.0 * np.sin(np.pi * numbers / length) ** 2
    return cas(2 * mode), cas(2 * mode + 1), eigen


def east_tables(length):
    modes = np.concatenate([np.arange(0, length, 2), np.arange(1, length, 2)])
    cell = np.arange(length)
    table = np.cos(np.pi * modes[:, None] * (2 * cell[None, :] + 1) / (2 * length)) * np.sqrt(2.0 / length)
    table[0] = np.sqrt(1.0 / length)
    eigen = 4.0 * np.sin(np.pi * modes / (2 * length)) ** 2
    return table, eigen


def sine_table(length):
    index = np.arange(1, length + 1)
    table = np.sqrt(2.0 / (length + 1)) * np.sin(np.pi * np.outer(index, index) / (length + 1))
    eigen = 4.0 * np.sin(np.pi * index / (2 * (length + 1))) ** 2
    return table, eigen


def split(value):
    high = value.astype(BF16)
    return high, (value - high.astype(F32)).astype(BF16)


def dot3(left, right):
    (lh, ll), (rh, rl) = left, right
    dot = functools.partial(jnp.dot, preferred_element_type=F32)
    return dot(lh, rh) + (dot(ll, rh) + dot(lh, rl))


def chebyshev(shift, count):
    values = [jnp.ones_like(shift)]
    step = values[0]
    for n in range(count):
        step = step + shift * values[n]
        values.append(values[n] + step)
    return values


def slab_solve(shift, right):
    count = len(right)
    u = chebyshev(shift, count)
    inverse = 1.0 / u[count]
    lower = [right[0]]
    for k in range(1, count):
        lower.append(lower[-1] + u[k] * right[k])
    upper = [None] * count
    for k in range(count - 2, -1, -1):
        term = u[count - 2 - k] * right[k + 1] if k < count - 2 else right[k + 1]
        upper[k] = term if upper[k + 1] is None else upper[k + 1] + term
    out = []
    for k in range(count):
        value = u[count - 1 - k] * lower[k]
        if upper[k] is not None:
            value = value + u[k] * upper[k]
        out.append(value * inverse)
    return out


def spike_of(shift, count):
    u = chebyshev(shift, count)
    inverse = 1.0 / u[count]
    return [u[count - 1 - k] * inverse for k in range(count)]


def interface_chain(couple, spread, bottoms, tops):
    count = len(bottoms)
    slope = jnp.zeros_like(couple)
    offset = jnp.zeros_like(couple)
    slopes, offsets, inverses, bases = [], [], [], []
    for s in range(count):
        inverse = 1.0 / (1.0 - couple * slope)
        base = (bottoms[s] + couple * offset) * inverse
        slopes.append(slope)
        offsets.append(offset)
        inverses.append(inverse * spread)
        bases.append(base)
        if s < count - 1:
            weight = spread * slope
            slope, offset = (
                couple + weight * spread * inverse,
                tops[s] + spread * offset + weight * base,
            )
    above = jnp.zeros_like(couple)
    lowers, uppers = [None] * count, [None] * count
    for s in range(count - 1, -1, -1):
        lower = bases[s] + inverses[s] * above
        uppers[s] = tops[s] + spread * (slopes[s] * lower + offsets[s]) + couple * above
        lowers[s] = lower
        above = lower
    below = [jnp.zeros_like(couple)] + uppers[:-1]
    above = lowers[1:] + [jnp.zeros_like(couple)]
    return below, above


def get_lanes(ref, rows):
    return jnp.concatenate([ref[n, rows, :] for n in range(ref.shape[0])], 1)


def put_lanes(ref, rows, value, start):
    for n in range(value.shape[1] // 128):
        ref[start + n, rows, :] = value[:, n * 128 : (n + 1) * 128]


def first_rows(nz, obs, up, ftop, fbot, gbot):
    rows = ftop.shape[0]
    ftop[...] = (1 - obs[pl.ds(nz - 1, rows, stride=nz), :]).astype(F32)
    low = (1 - obs[pl.ds(0, rows, stride=nz), :]).astype(F32)
    fbot[...] = low
    gbot[...] = low * up[pl.ds(0, rows, stride=nz), :]


def north_roll(value, shift):
    return pltpu.roll(value, shift % value.shape[1], 1)


def put_row(value, row, index):
    where = lax.broadcasted_iota(jnp.int32, value.shape, 0) == index
    return jnp.where(where, jnp.broadcast_to(row, value.shape), value)


def below_of(value, row):
    return put_row(pltpu.roll(value, 1, 0), row, 0)


def above_of(value, row):
    return put_row(pltpu.roll(value, value.shape[0] - 1, 0), row, value.shape[0] - 1)


def fluid_of(block):
    return (1 - block).astype(F32)


def forward_kernel(
    nz, slabs,
    obs, obs_prev, obs_next, east, east_next, north, up,
    f_west, f_east, g_east, f_below, g_above,
    te_h, te_l, to_h, to_l, c_h, c_l, lam_a, lam_b, c0,
    modes, out,
    src, half, bottom, top, acc,
):
    step = pl.program_id(0)
    steps = pl.num_programs(0)
    chunk = src.shape[0] // nz
    ny = src.shape[1]
    nx = chunk * steps
    first_slab = lax.axis_index("gz") == 0
    lift = jnp.where(first_slab, 1.0, 0.0).astype(F32)

    fluid_prev = jnp.where(step == 0, f_west[...], fluid_of(obs_prev[...]))
    last = step == steps - 1
    after_fluid = fluid_of(obs_next[...])
    flux_after = jnp.where(last, g_east[...], after_fluid * east_next[...])

    def row(i, carry):
        fluid, masked = carry
        at = pl.multiple_of(i * nz, nz)
        nxt = pl.multiple_of(jnp.minimum(i + 1, chunk - 1) * nz, nz)
        end = i == chunk - 1
        fluid_next = fluid_of(obs[pl.ds(nxt, nz), :])
        flux = jnp.where(end, flux_after, fluid_next * east[pl.ds(nxt, nz), :])
        masked_next = fluid * flux
        north_masked = fluid * north_roll(fluid, 1) * north[pl.ds(at, nz), :]
        below = below_of(fluid, f_below[pl.ds(i, 1), :] + lift)
        up_masked = fluid * below * up[pl.ds(at, nz), :]
        up_after = above_of(up_masked, fluid[nz - 1 : nz, :] * g_above[pl.ds(i, 1), :])
        src[pl.ds(at, nz), :] = (
            (masked - masked_next) + (north_masked - north_roll(north_masked, -1)) + (up_masked - up_after)
        )
        return fluid_next, masked_next

    start = fluid_of(obs[0:nz, :])
    lax.fori_loop(0, chunk, row, (start, start * fluid_prev * east[0:nz, :]), unroll=2)

    hy = ny // 2
    low, high = src[:, :hy], src[:, hy:]
    rows = pl.ds(pl.multiple_of(step * chunk * nz, chunk * nz), chunk * nz)
    put_lanes(half, rows, dot3(split(low + high), (te_h[...], te_l[...])), 0)
    put_lanes(half, rows, dot3(split(low - high), (to_h[...], to_l[...])), hy // 128)

    @pl.when(last)
    def _():
        left = (c_h[...], c_l[...])
        for k in range(nz):
            modes[k] = dot3(left, split(get_lanes(half, pl.ds(k, nx, stride=nz))))
        acc[...] = jnp.zeros_like(acc)
        blocks = nx // 8

        def solve(n, carry):
            at = pl.ds(pl.multiple_of(n * 8, 8), 8)
            parity = n // (blocks // 2)
            for lane in range(0, ny, 128):
                lanes = slice(lane, lane + 128)
                shift = lam_a[at, :] + lam_b[:, lanes]
                local = slab_solve(shift, [modes[k, at, lanes] for k in range(nz)])
                bottom[at, lanes] = local[0]
                top[at, lanes] = local[nz - 1]
                weight = c0[at, :]
                for k in range(nz):
                    acc[parity, k, :, lanes] += weight * local[k]
            return carry

        lax.fori_loop(0, blocks, solve, 0)
        even = [jnp.sum(acc[0, k], axis=0, keepdims=True) for k in range(nz)]
        odd = [jnp.sum(acc[1, k], axis=0, keepdims=True) for k in range(nz)]
        west = jnp.concatenate([e + o for e, o in zip(even, odd)], 0)
        east_end = jnp.concatenate([e - o for e, o in zip(even, odd)], 0)
        width = ny // slabs
        for j in range(slabs):
            lanes = slice(j * width, (j + 1) * width)
            out[j, 0:nx, :] = jnp.concatenate([bottom[:, lanes], top[:, lanes]], 1)
            out[j, nx : nx + nz, :] = jnp.concatenate([west[:, lanes], east_end[:, lanes]], 1)


def ends_kernel(nz, ends, lam_a, lam_b, c0, sum_h, sum_l, sine_h, sine_l, out, acc):
    slabs, width = ends.shape[0], ends.shape[2] // 2
    nx = ends.shape[1] - nz
    blocks = nx // 8
    row_b = lam_b[lax.axis_index("gz")]
    acc[...] = jnp.zeros_like(acc)

    def block(n, carry):
        at = pl.ds(pl.multiple_of(n * 8, 8), 8)
        parity = n // (blocks // 2)
        shift = lam_a[at, :width] + row_b
        spike = spike_of(shift, nz)
        pairs = [ends[s, at, :] for s in range(slabs)]
        below, above = interface_chain(
            spike[0], spike[nz - 1], [p[:, :width] for p in pairs], [p[:, width:] for p in pairs]
        )
        weight = c0[at, :width]
        spike = [weight * g for g in spike]
        for s in range(slabs):
            for k in range(nz):
                rows = pl.ds((s * nz + k) * 8, 8)
                acc[parity, rows, :] += spike[k] * below[s] + spike[nz - 1 - k] * above[s]
        return carry

    lax.fori_loop(0, blocks, block, 0)
    even, odd = acc[0], acc[1]
    sums = jnp.concatenate([even + odd, even - odd], 1)
    rows = jnp.concatenate([ends[s, nx : nx + nz, :] for s in range(slabs)], 0)
    out[...] = dot3((sum_h[...], sum_l[...]), split(sums)) + dot3((sine_h[...], sine_l[...]), split(rows))


def power(value, count):
    result = None
    while count:
        if count & 1:
            result = value if result is None else result * value
        count >>= 1
        if count:
            value = value * value
    return result


def correct_kernel(nz, groups, ends, found, lam_a, lam_b, mu, c0, sine_h, sine_l, out, jump):
    slabs, width = ends.shape[0], ends.shape[2] // 2
    nx = ends.shape[1] - nz
    total = slabs * nz
    blocks = nx // 8
    row_b = lam_b[lax.axis_index("gz")]
    shift = mu[:, :width] + row_b[0:1, :]
    cosh = 1.0 + 0.5 * shift
    sinh = jnp.sqrt(shift + 0.25 * shift * shift)
    grow = cosh + sinh
    decay = 1.0 / grow
    far = power(decay, nx)
    far2 = far * far
    scale = 1.0 / (sinh * (1.0 - far2))
    self2 = ((1.0 + far2) + (decay + far2 * grow)) * scale
    cross2 = 2.0 * (1.0 + cosh) * far * scale
    inverse = {}
    for f in range(groups):
        key = min(f, groups - f)
        if key not in inverse:
            inverse[key] = 1.0 / (1.0 + self2 - float(np.cos(2 * np.pi * f / groups)) * cross2)
    kernel = {}
    for n in range(groups // 2 + 1):
        value = None
        for f in range(groups):
            factor = float(np.cos(2 * np.pi * f * n / groups)) / groups
            term = factor * inverse[min(f, groups - f)]
            value = term if value is None else value + term
        kernel[n] = value
    jumps_east, jumps_west = None, None
    for n in range(groups):
        nxt = (n + 1) % groups
        t = found[n * total : (n + 1) * total, width:] - found[nxt * total : (nxt + 1) * total, :width]
        east_term = kernel[min(n, groups - n)] * t
        west_term = kernel[min(nxt, groups - nxt)] * t
        jumps_east = east_term if jumps_east is None else jumps_east + east_term
        jumps_west = west_term if jumps_west is None else jumps_west + west_term
    both = dot3((sine_h[...], sine_l[...]), split(jnp.concatenate([jumps_west, jumps_east], 1)))
    west, east = both[:, :width], both[:, width:]
    jump[0] = west - east
    jump[1] = west + east
    for s in range(slabs):
        out[s, nx : nx + nz, :] = both[s * nz : (s + 1) * nz, :]

    def block(n, carry):
        at = pl.ds(pl.multiple_of(n * 8, 8), 8)
        parity = n // (blocks // 2)
        shift = lam_a[at, :width] + row_b
        spike = spike_of(shift, nz)
        weight = c0[at, :width]
        loads = [weight * g for g in spike]
        bottoms, tops = [], []
        for s in range(slabs):
            pair = ends[s, at, :]
            low, high = pair[:, :width], pair[:, width:]
            for k in range(nz):
                q = jnp.broadcast_to(jump[parity, pl.ds(s * nz + k, 1), :], low.shape)
                low = low + loads[k] * q
                high = high + loads[nz - 1 - k] * q
            bottoms.append(low)
            tops.append(high)
        below, above = interface_chain(spike[0], spike[nz - 1], bottoms, tops)
        for s in range(slabs):
            out[s, at, :] = jnp.concatenate([below[s], above[s]], 1)
        return carry

    lax.fori_loop(0, blocks, block, 0)


def backward_kernel(
    nz, slabs,
    modes, solved,
    obs, obs_prev, obs_next, east, east_next, north, up,
    f_west, f_east, g_east, f_below, g_above, f_above,
    te_h, te_l, ti_h, ti_l, ct_h, ct_l, lam_a, lam_b, c0,
    out_east, out_north, out_up, out_p, out_r,
    below, above, found, half, press, p_below, p_above,
):
    step = pl.program_id(0)
    steps = pl.num_programs(0)
    chunk = obs.shape[0] // nz
    ny = obs.shape[1]
    hy = ny // 2
    nx = chunk * steps
    first_slab = lax.axis_index("gz") == 0
    lift = jnp.where(first_slab, 1.0, 0.0).astype(F32)
    last = step == steps - 1

    @pl.when(step == 0)
    def _():
        width = ny // slabs
        west, east_end = [], []
        for j in range(slabs):
            lanes = slice(j * width, (j + 1) * width)
            below[:, lanes] = solved[j, 0:nx, :width]
            above[:, lanes] = solved[j, 0:nx, width:]
            west.append(solved[j, nx : nx + nz, :width])
            east_end.append(solved[j, nx : nx + nz, width:])
        west = jnp.concatenate(west, 1)
        east_end = jnp.concatenate(east_end, 1)
        found[2] = west
        found[3] = east_end
        found[0] = west - east_end
        found[1] = west + east_end
        blocks = nx // 8

        def solve(n, carry):
            at = pl.ds(pl.multiple_of(n * 8, 8), 8)
            parity = n // (blocks // 2)
            for lane in range(0, ny, 128):
                lanes = slice(lane, lane + 128)
                shift = lam_a[at, :] + lam_b[:, lanes]
                weight = c0[at, :]
                right = []
                for k in range(nz):
                    q = jnp.broadcast_to(found[parity, pl.ds(k, 1), lanes], weight.shape)
                    right.append(modes[k, at, lanes] + weight * q)
                right[0] = right[0] + below[at, lanes]
                right[nz - 1] = right[nz - 1] + above[at, lanes]
                local = slab_solve(shift, right)
                for k in range(nz):
                    modes[k, at, lanes] = local[k]
            return carry

        lax.fori_loop(0, blocks, solve, 0)
        left = (ct_h[...], ct_l[...])
        for k in range(nz):
            put_lanes(half, pl.ds(nz + k, nx, stride=nz), dot3(left, split(modes[k])), 0)
        first, final = slice(nz, 2 * nz), slice(nx * nz, (nx + 1) * nz)
        put_lanes(half, slice(0, nz), get_lanes(half, first) + found[2], 0)
        put_lanes(half, slice((nx + 1) * nz, (nx + 2) * nz), get_lanes(half, final) - found[3], 0)

        def north_back(value):
            even = dot3(split(value[:, :hy]), (te_h[...], te_l[...]))
            odd = dot3(split(value[:, hy:]), (ti_h[...], ti_l[...]))
            return even + odd, even - odd

        p_below[:, :hy], p_below[:, hy:] = north_back(dot3(left, split(below[...])))
        p_above[:, :hy], p_above[:, hy:] = north_back(dot3(left, split(above[...])))
        size = 16 * nz

        def back(n, carry):
            at = pl.ds(pl.multiple_of(n * size, size), size)
            press[at, :hy], press[at, hy:] = north_back(get_lanes(half, at))
            return carry

        lax.fori_loop(0, nx * nz // size, back, 0)
        at = slice(nx * nz, (nx + 2) * nz)
        press[at, :hy], press[at, hy:] = north_back(get_lanes(half, at))

    fluid_prev = jnp.where(step == 0, f_west[...], fluid_of(obs_prev[...]))
    after_fluid = jnp.where(last, f_east[...], fluid_of(obs_next[...]))
    flux_after = jnp.where(last, g_east[...], fluid_of(obs_next[...]) * east_next[...])
    base = step * chunk

    def rows_of(i):
        return pl.ds(pl.multiple_of((base + i + 1) * nz, nz), nz)

    def row(i, carry):
        fluid, p, east_done = carry
        at = pl.ds(pl.multiple_of(i * nz, nz), nz)
        nxt = pl.ds(pl.multiple_of(jnp.minimum(i + 1, chunk - 1) * nz, nz), nz)
        end = i == chunk - 1
        fluid_next = jnp.where(end, after_fluid, fluid_of(obs[nxt, :]))
        flux = jnp.where(end, flux_after, fluid_next * east[nxt, :])
        p_next = press[rows_of(i + 1), :]
        east_next_done = fluid * (flux - fluid_next * (p_next - p))
        north_done = fluid * north_roll(fluid, 1) * (north[at, :] - (p - north_roll(p, 1)))
        line = pl.ds(base + i, 1)
        chunk_line = pl.ds(i, 1)
        fluid_below = below_of(fluid, f_below[chunk_line, :] + lift)
        up_done = fluid * fluid_below * (up[at, :] - (p - below_of(p, p_below[line, :])))
        edge = fluid[nz - 1 : nz, :] * (
            g_above[chunk_line, :] - f_above[chunk_line, :] * (p_above[line, :] - p[nz - 1 : nz, :])
        )
        out_east[at, :] = east_done
        out_north[at, :] = north_done
        out_up[at, :] = up_done
        out_p[at, :] = p
        out_r[at, :] = (
            (east_done - east_next_done)
            + (north_done - north_roll(north_done, -1))
            + (up_done - above_of(up_done, edge))
        )
        return fluid_next, p_next, east_next_done

    start = fluid_of(obs[0:nz, :])
    p_first = press[rows_of(0), :]
    done = start * fluid_prev * (east[0:nz, :] - (p_first - press[rows_of(-1), :]))
    lax.fori_loop(0, chunk, row, (start, p_first, done), unroll=2)


def local(groups, slabs, east_velocity, north_velocity, upward_velocity, obstacle):
    nx, nz, ny = east_velocity.shape
    total = slabs * nz
    width = ny // slabs
    flat = [a.reshape(nx * nz, ny) for a in (obstacle, east_velocity, north_velocity, upward_velocity)]
    obs, east, north, up = flat

    even_np, odd_np, lam_b_np = north_tables(ny)
    block_np, lam_a_np = east_tables(nx)
    sine_np, mu_np = sine_table(total)
    te_h, te_l = pair_np(even_np)
    to_h, to_l = pair_np(odd_np)
    ti_h, ti_l = pair_np(odd_np.T.copy())
    c_h, c_l = pair_np(block_np)
    ct_h, ct_l = pair_np(block_np.T.copy())
    sine_h, sine_l = pair_np(sine_np)
    sum_h, sum_l = (np.repeat(t, 8, axis=1) for t in (sine_h, sine_l))
    lam_a = np.repeat(lam_a_np[:, None], 128, 1).astype(np.float32)
    c0 = np.repeat(block_np[:, :1], 128, 1).astype(np.float32)
    lam_b = np.repeat(lam_b_np[None], 8, 0).astype(np.float32)
    lam_b_part = np.repeat(lam_b_np.reshape(slabs, 1, width), 8, 1).astype(np.float32)
    mu = np.repeat(mu_np[:, None], 128, 1).astype(np.float32)

    chunk = 16
    steps = nx // chunk
    params = pltpu.CompilerParams(vmem_limit_bytes=VMEM_LIMIT, dimension_semantics=("arbitrary",))
    single = pltpu.CompilerParams(vmem_limit_bytes=VMEM_LIMIT)
    big = pl.BlockSpec((chunk * nz, ny), lambda i: (i, 0))
    line = pl.BlockSpec((chunk, ny), lambda i: (i, 0))
    before = pl.BlockSpec((nz, ny), lambda i: (jnp.maximum(i * chunk - 1, 0), 0))
    after = pl.BlockSpec((nz, ny), lambda i: (jnp.minimum(i * chunk + chunk, nx - 1), 0))

    def whole(a):
        return pl.BlockSpec(a.shape, lambda *_: (0,) * len(a.shape))

    plane = jax.ShapeDtypeStruct((nx, ny), F32)
    f_top, f_bot, g_bot = pl.pallas_call(
        functools.partial(first_rows, nz),
        grid=(ny // 128,),
        in_specs=[pl.BlockSpec((nx * nz, 128), lambda i: (0, i))] * 2,
        out_specs=[pl.BlockSpec((nx, 128), lambda i: (0, i))] * 3,
        out_shape=[plane] * 3,
        compiler_params=params,
        name="planes",
    )(obs, up)

    rising = [(i, i + 1) for i in range(slabs - 1)]
    falling = [(i + 1, i) for i in range(slabs - 1)]
    to_east = [(i, (i + 1) % groups) for i in range(groups)]
    to_west = [((i + 1) % groups, i) for i in range(groups)]
    f_below = lax.ppermute(f_top, "gz", rising)
    g_above = lax.ppermute(g_bot, "gz", falling)
    f_first = (1 - obs[:nz]).astype(F32)
    f_west = lax.ppermute((1 - obs[(nx - 1) * nz :]).astype(F32), "xy", to_east)
    side = lax.ppermute(jnp.concatenate([f_first, f_first * east[:nz]], 0), "xy", to_west)
    f_east, g_east = side[:nz], side[nz:]
    f_above = lax.ppermute(f_bot, "gz", falling)

    tables = (te_h, te_l, to_h, to_l, c_h, c_l, lam_a, lam_b, c0)
    ends_shape = jax.ShapeDtypeStruct((slabs, nx + nz, 2 * width), F32)
    modes, ends = pl.pallas_call(
        functools.partial(forward_kernel, nz, slabs),
        grid=(steps,),
        in_specs=[big, before, after, big, after, big, big]
        + [whole(f_west)] * 3 + [line, line]
        + [whole(t) for t in tables],
        out_specs=[
            pl.BlockSpec((nz, nx, ny), lambda i: (0, 0, 0)),
            pl.BlockSpec(ends_shape.shape, lambda i: (0, 0, 0)),
        ],
        out_shape=[jax.ShapeDtypeStruct((nz, nx, ny), F32), ends_shape],
        scratch_shapes=[
            pltpu.VMEM((chunk * nz, ny), F32),
            pltpu.VMEM((ny // 128, nx * nz, 128), F32),
            pltpu.VMEM((nx, ny), F32),
            pltpu.VMEM((nx, ny), F32),
            pltpu.VMEM((2, nz, 8, ny), F32),
        ],
        compiler_params=params,
        name="forward",
    )(obs, obs, obs, east, east, north, up, f_west, f_east, g_east, f_below, g_above, *tables)

    ends = lax.all_to_all(ends, "gz", split_axis=0, concat_axis=0, tiled=True)
    own = pl.pallas_call(
        functools.partial(ends_kernel, nz),
        out_shape=jax.ShapeDtypeStruct((total, 2 * width), F32),
        scratch_shapes=[pltpu.VMEM((2, total * 8, width), F32)],
        compiler_params=single,
        name="ends",
    )(ends, lam_a, lam_b_part, c0, sum_h, sum_l, sine_h, sine_l)
    found = [own]
    for shift in range(1, groups):
        found.append(lax.ppermute(own, "xy", [((i + shift) % groups, i) for i in range(groups)]))
    solved = pl.pallas_call(
        functools.partial(correct_kernel, nz, groups),
        out_shape=ends_shape,
        scratch_shapes=[pltpu.VMEM((2, total, width), F32)],
        compiler_params=single,
        name="correct",
    )(ends, jnp.concatenate(found, 0), lam_a, lam_b_part, mu, c0, sine_h, sine_l)
    solved = lax.all_to_all(solved, "gz", split_axis=0, concat_axis=0, tiled=True)

    tables = (te_h, te_l, ti_h, ti_l, ct_h, ct_l, lam_a, lam_b, c0)
    field = jax.ShapeDtypeStruct((nx * nz, ny), F32)
    outs = pl.pallas_call(
        functools.partial(backward_kernel, nz, slabs),
        grid=(steps,),
        in_specs=[
            pl.BlockSpec((nz, nx, ny), lambda i: (0, 0, 0)),
            pl.BlockSpec(ends_shape.shape, lambda i: (0, 0, 0)),
        ]
        + [big, before, after, big, after, big, big]
        + [whole(f_west)] * 3 + [line, line, line]
        + [whole(t) for t in tables],
        out_specs=[big] * 5,
        out_shape=[field] * 5,
        scratch_shapes=[
            pltpu.VMEM((nx, ny), F32),
            pltpu.VMEM((nx, ny), F32),
            pltpu.VMEM((4, nz, ny), F32),
            pltpu.VMEM((ny // 128, (nx + 2) * nz, 128), F32),
            pltpu.VMEM(((nx + 2) * nz, ny), F32),
            pltpu.VMEM((nx, ny), F32),
            pltpu.VMEM((nx, ny), F32),
        ],
        compiler_params=params,
        name="backward",
    )(modes, solved, obs, obs, obs, east, east, north, up,
      f_west, f_east, g_east, f_below, g_above, f_above, *tables)
    return tuple(o.reshape(nx, nz, ny) for o in outs)


def solution(mesh):
    placed = P("xy", "gz", None)
    return jax.shard_map(
        functools.partial(local, mesh.shape["xy"], mesh.shape["gz"]),
        mesh=mesh,
        in_specs=(placed,) * 4,
        out_specs=(placed,) * 5,
        check_vma=False,
    )
```

time: 409 us -> 144 us (0.35); the launches traced: 402 us -> 143 us
  waiting for transfers between devices: 148 us -> 15.3 us
  other arithmetic: 116 us -> 2.91 us
  Pallas kernels: 0 us -> 86.1 us
  local copies, waits for them, and re-layouts: 64.5 us -> 2.29 us
  matrix products: 36.9 us -> 0 us
  blocking collectives: 0 us -> 15.4 us
  between operations: 14.9 us -> 0.69 us
    all_to_all x2 -> x1, waiting for transfers between devices: 92.3 us -> 0.01 us  [local(): lax.all_to_all(solved, 'gz', split_axis=0, concat_axis=0, tiled=True)]
    pallas_call x0 -> x5, Pallas kernels: none -> 86.1 us  [the longest x1 21.4 us: local(): pl.pallas_call(functools.partial(correct_kernel, nz, groups), out_shape=e...]
    dynamic_update_slice x32 -> x0, other arithmetic: 62.3 us -> none  [the longest x16 39.2 us: tridiagonal(): _, (ratios, values) = lax.scan(forward, (start, start), right)]
    dot_general x4 -> x0, matrix products: 36.9 us -> none  [the longest x1 9.32 us: local(): jnp.einsum('zka,gxa->gxzk', pressure_modes, table_east, precision=HIGH)]
    all_gather x1 -> x0, waiting for transfers between devices: 33.5 us -> none  [local(): everything = lax.all_gather(ends[None], 'gz', axis=0, tiled=True)]
    mul x6 -> x1, other arithmetic: 18.3 us -> 0.74 us  [local(): f_first * east[:nz]]
    another operation x10 -> x0, local copies, waits for them, and re-layouts: 16.7 us -> none
    unnamed x65 -> x12, local copies, waits for them, and re-layouts: 17.7 us -> 1.68 us
  transfers between devices with their start and end apart: 11 -> 9, of which waited for: 8 -> 5; matrix products, arithmetic and copies ran while one was open for 8% -> 1% of each run, Pallas kernels for 0% -> 0%
where the time goes in v1:
time: 144 us; the launch traced here: 143 us
  Pallas kernels  86.1 us (60%)
  starting transfers between devices  20.1 us (14%)
  blocking collectives  15.4 us (11%)
  waiting for transfers between devices  15.3 us (11%)
  other arithmetic  2.91 us (2%)
  local copies, waits for them, and re-layouts  2.29 us (2%)
    pallas_call x1, Pallas kernels, local(): pl.pallas_call(functools.partial(correct_kernel, nz, groups), out_shape=e...  21.4 us
    pallas_call x1, Pallas kernels, local(): pl.pallas_call(functools.partial(ends_kernel, nz), out_shape=jax.ShapeDty...  21.3 us
    pallas_call x1, Pallas kernels, local(): pl.pallas_call(functools.partial(backward_kernel, nz, slabs), grid=(steps...  21 us
    pallas_call x1, Pallas kernels, local(): pl.pallas_call(functools.partial(forward_kernel, nz, slabs), grid=(steps,...  18.5 us
    all_to_all x1, blocking collectives, local(): ends = lax.all_to_all(ends, 'gz', split_axis=0, concat_axis=0, tiled=True)  15.4 us
    ppermute x1, waiting for transfers between devices, local(): f_above = lax.ppermute(f_bot, 'gz', falling)  9.27 us
    all_to_all x1, starting transfers between devices, local(): lax.all_to_all(solved, 'gz', split_axis=0, concat_axis=0, tiled=True)  5.05 us
    ppermute x1, starting transfers between devices, local(): f_below = lax.ppermute(f_top, 'gz', rising)  4.49 us
  transfers between devices with their start and end apart: 9, of which 5 were waited for; matrix products, arithmetic and copies ran while one was open for 1% of the time, Pallas kernels for 0%

profile of v1, /device:TPU:1, one launch (start us, length us, event | category | flops | bytes accessed | tf_op | source)
XLA Modules:
  0.0 142.8 jit_solution(4150279751469616543)
XLA Ops:
  0.6 3.9 %planes.1 = (f32[128,512]{1,0:T(8,128)}, f32[128,512]{1,0:T(8,128)}, f32[128,512]{1,0:T(8,128)}) custom-call(s32[1024,512]{1,0:T(8,128)} %bitcast.17, f32[1024,512]{1,0:T(8,128)} %bitcast.28), custom_call_target="tpu_custom_call" | custom-call | tf_op jit(solution)/shard_map/planes/pallas_call | solution.py:518
  4.6 4.5 %collective-permute-start.2 = (f32[128,512]{1,0:T(8,128)}, f32[128,512]{1,0:T(8,128)S(1)}, u32[]{:S(2)}, u32[]{:S(2)}) collective-permute-start(f32[128,512]{1,0:T(8,128)} %get-tuple-element.15), channel_id=1, source_target_pairs={{0,4},{4,8},{8,12},{12,16},{16,20},{20,24},{24,28},{1,5},{5,9},{9,... | collective-permute-start | bytes 786440 | tf_op jit(solution)/shard_map/ppermute | solution.py:532
  9.1 1.9 %collective-permute-start.3 = (f32[128,512]{1,0:T(8,128)}, f32[128,512]{1,0:T(8,128)S(1)}, u32[]{:S(2)}, u32[]{:S(2)}) collective-permute-start(f32[128,512]{1,0:T(8,128)} %get-tuple-element.16), channel_id=1, source_target_pairs={{4,0},{8,4},{12,8},{16,12},{20,16},{24,20},{28,24},{5,1},{9,5},{13... | collective-permute-start | bytes 786440 | tf_op jit(solution)/shard_map/ppermute | solution.py:533
  11.0 0.7 convert_bitcast_fusion
  11.7 0.7 bitcast_multiply_fusion
  12.5 3.4 %collective-permute-start.1 = (f32[16,512]{1,0:T(8,128)S(1)}, f32[16,512]{1,0:T(8,128)S(1)}, u32[]{:S(2)}, u32[]{:S(2)}) collective-permute-start(f32[16,512]{1,0:T(8,128)S(1)} %pad_maximum_fusion.1), channel_id=1, source_target_pairs={{1,0},{2,1},{3,2},{0,3},{5,4},{6,5},{7,6},{4,7},{9,8},{10,9},{11,1... | collective-permute-start | bytes 98312 | tf_op jit(solution)/shard_map/ppermute | solution.py:536
  15.9 0.0 collective-permute-start
  15.9 1.0 collective-permute-done.1
  16.9 0.6 fusion
  17.5 2.8 %collective-permute-done.f_west = f32[8,512]{1,0:T(8,128)S(1)} collective-permute-done((f32[8,512]{1,0:T(8,128)S(1)}, f32[8,512]{1,0:T(8,128)S(1)}, u32[]{:S(2)}, u32[]{:S(2)}) %collective-permute-start) | collective-permute-done | bytes 16416 | tf_op jit(solution)/shard_map/ppermute | solution.py:535
  20.2 0.0 copy-start.4
  20.2 0.0 collective-permute-done.2.f_below
  20.2 0.0 copy-start.1
  20.2 0.0 collective-permute-done.3.g_above
  20.3 0.0 copy-start.2
  20.3 0.6 copy-done.4
  20.8 0.1 copy-done.1
  21.0 0.1 copy-done.2
  21.1 18.5 %forward.1 = (f32[8,128,512]{2,1,0:T(8,128)}, f32[8,136,128]{2,1,0:T(8,128)}) custom-call(s32[1024,512]{1,0:T(8,128)} %bitcast.18, s32[1024,512]{1,0:T(8,128)} %bitcast.19, s32[1024,512]{1,0:T(8,128)} %bitcast.20, f32[1024,512]{1,0:T(8,128)} %bitcast.24, f32[1024,512]{1,0:T(8,128)} %bitcast.25, f32[1024,512]{1,0:T(8,128)} %bitcast.31, f32[1024,512]{1,0:T(8,128)} %bitcast.29, ...), custom_call_target="tpu_custom_call" | custom-call | tf_op jit(solution)/shard_map/forward/pallas_call | solution.py:542
  39.5 15.4 %all_to_all.10.ends = f32[8,136,128]{2,1,0:T(8,128)} all-to-all(f32[8,136,128]{2,1,0:T(8,128)} %get-tuple-element.18), channel_id=1, replica_groups=mesh['gz'=8,'xy'=4] {'gz'}, dimensions={0} | all-to-all | bytes 1114112 | tf_op jit(solution)/shard_map/all_to_all | solution.py:564
  54.9 0.0 copy-start.5
  54.9 21.3 %ends.1 = f32[64,128]{1,0:T(8,128)} custom-call(f32[8,136,128]{2,1,0:T(8,128)} %all_to_all.10.ends, f32[128,128]{1,0:T(8,128)} %constant.46.clone.lam_a, f32[8,8,64]{2,1,0:T(8,128)} %constant.49.clone.lam_b, f32[128,128]{1,0:T(8,128)} %constant.48.clone.c0, bf16[64,512]{1,0:T(8,128)(2,1)} %constant.50.clone.sum_h, bf16[64,512]{1,0:T(8,128)(2,1)} %constant.51.clone.sum_l, ...), custom_call_target="tpu_custom_call" | custom-call | tf_op jit(solution)/shard_map/ends/pallas_call | solution.py:565
  76.3 0.0 collective-permute-start.6
  76.3 0.8 collective-permute-start.5
  77.1 2.5 %collective-permute-start.4 = (f32[64,128]{1,0:T(8,128)}, f32[64,128]{1,0:T(8,128)S(1)}, u32[]{:S(2)}, u32[]{:S(2)}) collective-permute-start(f32[64,128]{1,0:T(8,128)} %ends.1), channel_id=1, source_target_pairs={{1,0},{2,1},{3,2},{0,3},{5,4},{6,5},{7,6},{4,7},{9,8},{10,9},{11,1... | collective-permute-start | bytes 98312 | tf_op jit(solution)/shard_map/ppermute | solution.py:574
  79.5 1.5 %collective-permute-done.6 = f32[64,128]{1,0:T(8,128)S(1)} collective-permute-done((f32[64,128]{1,0:T(8,128)}, f32[64,128]{1,0:T(8,128)S(1)}, u32[]{:S(2)}, u32[]{:S(2)}) %collective-permute-start.6) | collective-permute-done | bytes 32800 | tf_op jit(solution)/shard_map/ppermute | solution.py:574
  81.1 0.0 collective-permute-done.5
  81.1 0.7 collective-permute-done.4
  81.8 1.4 pad_maximum_fusion.found
  83.2 21.4 %correct.1 = f32[8,136,128]{2,1,0:T(8,128)} custom-call(f32[8,136,128]{2,1,0:T(8,128)} %all_to_all.10.ends, f32[256,128]{1,0:T(8,128)} %pad_maximum_fusion.found, f32[128,128]{1,0:T(8,128)} %constant.46.clone.lam_a, f32[8,8,64]{2,1,0:T(8,128)} %constant.49.clone.lam_b, f32[64,128]{1,0:T(8,128)} %constant.54.clone.mu, f32[128,128]{1,0:T(8,128)} %constant.48.clone.c0, ...), custom_call_target="tpu_custom_call" | custom-call | tf_op jit(solution)/shard_map/correct/pallas_call | solution.py:575
  104.6 5.1 %all-to-all-start.1 = ((f32[8,136,128]{2,1,0:T(8,128)}), f32[8,136,128]{2,1,0:T(8,128)S(1)}, u32[]{:S(2)}, u32[]{:S(2)}) async-start(f32[8,136,128]{2,1,0:T(8,128)} %correct.1), calls=%async_computation.1 | async-start | bytes 1114112 | tf_op jit(solution)/shard_map/all_to_all | solution.py:582
  109.6 0.0 copy-done.5
  109.6 2.0 %collective-permute-start.7 = (f32[128,512]{1,0:T(8,128)S(1)}, f32[128,512]{1,0:T(8,128)S(1)}, u32[]{:S(2)}, u32[]{:S(2)}) collective-permute-start(f32[128,512]{1,0:T(8,128)S(1)} %copy-done.5), channel_id=1, source_target_pairs={{4,0},{8,4},{12,8},{16,12},{20,16},{24,20},{28,24},{5,1},{9,5},{13... | collective-permute-start | bytes 786440 | tf_op jit(solution)/shard_map/ppermute | solution.py:538
  111.7 9.3 %collective-permute-done.7.f_above = f32[128,512]{1,0:T(8,128)S(1)} collective-permute-done((f32[128,512]{1,0:T(8,128)S(1)}, f32[128,512]{1,0:T(8,128)S(1)}, u32[]{:S(2)}, u32[]{:S(2)}) %collective-permute-start.7) | collective-permute-done | bytes 262176 | tf_op jit(solution)/shard_map/ppermute | solution.py:538
  120.9 0.0 copy-start.3
  120.9 0.0 all-to-all-done.1.solved
  121.0 0.0 copy-start
  121.0 0.7 copy-done.3
  121.6 0.2 copy-done
  121.8 21.0 %backward.1 = (f32[1024,512]{1,0:T(8,128)}, f32[1024,512]{1,0:T(8,128)}, f32[1024,512]{1,0:T(8,128)}, f32[1024,512]{1,0:T(8,128)}, f32[1024,512]{1,0:T(8,128)}) custom-call(f32[8,128,512]{2,1,0:T(8,128)} %get-tuple-element.17.modes, f32[8,136,128]{2,1,0:T(8,128)} %copy-done, s32[1024,512]{1,0:T(8,128)} %bitcast.21, s32[1024,512]{1,0:T(8,128)} %bitcast.22, ...), custom_call_target="tpu_custom_call" | custom-call | tf_op jit(solution)/shard_map/backward/pallas_call | solution.py:586
  (1 shorter events, 0.0 us)
Async XLA Ops:
  4.6 15.7 %collective-permute-start.2 = (f32[128,512]{1,0:T(8,128)}, f32[128,512]{1,0:T(8,128)S(1)}, u32[]{:S(2)}, u32[]{:S(2)}) collective-permute-start(f32[128,512]{1,0:T(8,128)} %get-tuple-element.15), channel_id=1, source_target_pairs={{0,4},{4,8},{8,12},{12,16},{16,20},{20,24},{24,28},{1,5},{5,9},{9,... | collective-permute-start | bytes 786440 | tf_op jit(solution)/shard_map/ppermute | solution.py:532
  9.1 11.2 %collective-permute-start.3 = (f32[128,512]{1,0:T(8,128)}, f32[128,512]{1,0:T(8,128)S(1)}, u32[]{:S(2)}, u32[]{:S(2)}) collective-permute-start(f32[128,512]{1,0:T(8,128)} %get-tuple-element.16), channel_id=1, source_target_pairs={{4,0},{8,4},{12,8},{16,12},{20,16},{24,20},{28,24},{5,1},{9,5},{13... | collective-permute-start | bytes 786440 | tf_op jit(solution)/shard_map/ppermute | solution.py:533
  12.5 4.4 %collective-permute-start.1 = (f32[16,512]{1,0:T(8,128)S(1)}, f32[16,512]{1,0:T(8,128)S(1)}, u32[]{:S(2)}, u32[]{:S(2)}) collective-permute-start(f32[16,512]{1,0:T(8,128)S(1)} %pad_maximum_fusion.1), channel_id=1, source_target_pairs={{1,0},{2,1},{3,2},{0,3},{5,4},{6,5},{7,6},{4,7},{9,8},{10,9},{11,1... | collective-permute-start | bytes 98312 | tf_op jit(solution)/shard_map/ppermute | solution.py:536
  15.9 4.4 %collective-permute-start = (f32[8,512]{1,0:T(8,128)S(1)}, f32[8,512]{1,0:T(8,128)S(1)}, u32[]{:S(2)}, u32[]{:S(2)}) collective-permute-start(f32[8,512]{1,0:T(8,128)S(1)} %get-tuple-element.26), channel_id=1, source_target_pairs={{0,1},{1,2},{2,3},{3,0},{4,5},{5,6},{6,7},{7,4},{8,9},{9,10},{10,1... | collective-permute-start | bytes 49160 | tf_op jit(solution)/shard_map/ppermute | solution.py:535
  20.2 0.6 copy-start.4
  20.2 0.7 copy-start.1
  20.3 0.8 copy-start.2
  54.9 54.7 %copy-start.5 = (f32[128,512]{1,0:T(8,128)S(1)}, f32[128,512]{1,0:T(8,128)}, u32[]{:S(2)}) copy-start(f32[128,512]{1,0:T(8,128)} %get-tuple-element.19) | copy-start | bytes 786436
  76.3 4.8 %collective-permute-start.6 = (f32[64,128]{1,0:T(8,128)}, f32[64,128]{1,0:T(8,128)S(1)}, u32[]{:S(2)}, u32[]{:S(2)}) collective-permute-start(f32[64,128]{1,0:T(8,128)} %ends.1), channel_id=1, source_target_pairs={{3,0},{0,1},{1,2},{2,3},{7,4},{4,5},{5,6},{6,7},{11,8},{8,9},{9,10... | collective-permute-start | bytes 98312 | tf_op jit(solution)/shard_map/ppermute | solution.py:574
  76.3 4.8 %collective-permute-start.5 = (f32[64,128]{1,0:T(8,128)}, f32[64,128]{1,0:T(8,128)S(1)}, u32[]{:S(2)}, u32[]{:S(2)}) collective-permute-start(f32[64,128]{1,0:T(8,128)} %ends.1), channel_id=1, source_target_pairs={{2,0},{3,1},{0,2},{1,3},{6,4},{7,5},{4,6},{5,7},{10,8},{11,9},{8,1... | collective-permute-start | bytes 98312 | tf_op jit(solution)/shard_map/ppermute | solution.py:574
  77.1 4.7 %collective-permute-start.4 = (f32[64,128]{1,0:T(8,128)}, f32[64,128]{1,0:T(8,128)S(1)}, u32[]{:S(2)}, u32[]{:S(2)}) collective-permute-start(f32[64,128]{1,0:T(8,128)} %ends.1), channel_id=1, source_target_pairs={{1,0},{2,1},{3,2},{0,3},{5,4},{6,5},{7,6},{4,7},{9,8},{10,9},{11,1... | collective-permute-start | bytes 98312 | tf_op jit(solution)/shard_map/ppermute | solution.py:574
  104.6 16.4 %all-to-all-start.1 = ((f32[8,136,128]{2,1,0:T(8,128)}), f32[8,136,128]{2,1,0:T(8,128)S(1)}, u32[]{:S(2)}, u32[]{:S(2)}) async-start(f32[8,136,128]{2,1,0:T(8,128)} %correct.1), calls=%async_computation.1 | async-start | bytes 1114112 | tf_op jit(solution)/shard_map/all_to_all | solution.py:582
  109.6 11.3 %collective-permute-start.7 = (f32[128,512]{1,0:T(8,128)S(1)}, f32[128,512]{1,0:T(8,128)S(1)}, u32[]{:S(2)}, u32[]{:S(2)}) collective-permute-start(f32[128,512]{1,0:T(8,128)S(1)} %copy-done.5), channel_id=1, source_target_pairs={{4,0},{8,4},{12,8},{16,12},{20,16},{24,20},{28,24},{5,1},{9,5},{13... | collective-permute-start | bytes 786440 | tf_op jit(solution)/shard_map/ppermute | solution.py:538
  120.9 0.7 copy-start.3
  121.0 0.9 copy-start

commit v2 on v1

--- a/solution.py
+++ b/solution.py
@@ -241,39 +241,45 @@
         width = ny // slabs
         for j in range(slabs):
             lanes = slice(j * width, (j + 1) * width)
-            out[j, 0:nx, :] = jnp.concatenate([bottom[:, lanes], top[:, lanes]], 1)
+            hx = nx // 2
+            out[j, 0:hx, :] = jnp.concatenate([bottom[:hx, lanes], bottom[hx:, lanes]], 1)
+            out[j, hx:nx, :] = jnp.concatenate([top[:hx, lanes], top[hx:, lanes]], 1)
             out[j, nx : nx + nz, :] = jnp.concatenate([west[:, lanes], east_end[:, lanes]], 1)
 
 
+def swap_halves(value):
+    width = value.shape[1] // 2
+    return jnp.concatenate([value[:, width:], value[:, :width]], 1)
+
+
+def in_first_half(value):
+    return lax.broadcasted_iota(jnp.int32, value.shape, 1) < value.shape[1] // 2
+
+
 def ends_kernel(nz, ends, lam_a, lam_b, c0, sum_h, sum_l, sine_h, sine_l, out, acc):
-    slabs, width = ends.shape[0], ends.shape[2] // 2
+    slabs = ends.shape[0]
     nx = ends.shape[1] - nz
-    blocks = nx // 8
-    row_b = lam_b[lax.axis_index("gz")]
-    acc[...] = jnp.zeros_like(acc)
-
-    def block(n, carry):
-        at = pl.ds(pl.multiple_of(n * 8, 8), 8)
-        parity = n // (blocks // 2)
-        shift = lam_a[at, :width] + row_b
-        spike = spike_of(shift, nz)
-        pairs = [ends[s, at, :] for s in range(slabs)]
-        below, above = interface_chain(
-            spike[0], spike[nz - 1], [p[:, :width] for p in pairs], [p[:, width:] for p in pairs]
-        )
-        weight = c0[at, :width]
-        spike = [weight * g for g in spike]
-        for s in range(slabs):
-            for k in range(nz):
-                rows = pl.ds((s * nz + k) * 8, 8)
-                acc[parity, rows, :] += spike[k] * below[s] + spike[nz - 1 - k] * above[s]
-        return carry
-
-    lax.fori_loop(0, blocks, block, 0)
-    even, odd = acc[0], acc[1]
-    sums = jnp.concatenate([even + odd, even - odd], 1)
+    hx = nx // 2
+    shift = lam_a[...] + lam_b[lax.axis_index("gz")][0:1, :]
+    spike = spike_of(shift, nz)
+    below, above = interface_chain(
+        spike[0],
+        spike[nz - 1],
+        [ends[s, 0:hx, :] for s in range(slabs)],
+        [ends[s, hx:nx, :] for s in range(slabs)],
+    )
+    weight = c0[...]
+    spike = [weight * g for g in spike]
+    for s in range(slabs):
+        for k in range(nz):
+            term = spike[k] * below[s] + spike[nz - 1 - k] * above[s]
+            row = (s * nz + k) * 8
+            acc[row : row + 8, :] = jnp.sum(term.reshape(hx // 8, 8, term.shape[1]), axis=0)
+    both = dot3((sum_h[...], sum_l[...]), split(acc[...]))
+    other = swap_halves(both)
+    both = jnp.where(in_first_half(both), both + other, other - both)
     rows = jnp.concatenate([ends[s, nx : nx + nz, :] for s in range(slabs)], 0)
-    out[...] = dot3((sum_h[...], sum_l[...]), split(sums)) + dot3((sine_h[...], sine_l[...]), split(rows))
+    out[...] = both + dot3((sine_h[...], sine_l[...]), split(rows))
 
 
 def power(value, count):
@@ -287,13 +293,14 @@
     return result
 
 
-def correct_kernel(nz, groups, ends, found, lam_a, lam_b, mu, c0, sine_h, sine_l, out, jump):
+def correct_kernel(nz, groups, ends, *rest):
+    found = rest[:groups]
+    lam_a, lam_b, mu, c0, sine_h, sine_l, out, jump = rest[groups:]
     slabs, width = ends.shape[0], ends.shape[2] // 2
     nx = ends.shape[1] - nz
-    total = slabs * nz
-    blocks = nx // 8
-    row_b = lam_b[lax.axis_index("gz")]
-    shift = mu[:, :width] + row_b[0:1, :]
+    hx = nx // 2
+    row_b = lam_b[lax.axis_index("gz")][0:1, :]
+    shift = mu[:, :width] + row_b[:, :width]
     cosh = 1.0 + 0.5 * shift
     sinh = jnp.sqrt(shift + 0.25 * shift * shift)
     grow = cosh + sinh
@@ -319,41 +326,32 @@
     jumps_east, jumps_west = None, None
     for n in range(groups):
         nxt = (n + 1) % groups
-        t = found[n * total : (n + 1) * total, width:] - found[nxt * total : (nxt + 1) * total, :width]
+        t = found[n][:, width:] - found[nxt][:, :width]
         east_term = kernel[min(n, groups - n)] * t
         west_term = kernel[min(nxt, groups - nxt)] * t
         jumps_east = east_term if jumps_east is None else jumps_east + east_term
         jumps_west = west_term if jumps_west is None else jumps_west + west_term
     both = dot3((sine_h[...], sine_l[...]), split(jnp.concatenate([jumps_west, jumps_east], 1)))
-    west, east = both[:, :width], both[:, width:]
-    jump[0] = west - east
-    jump[1] = west + east
+    other = swap_halves(both)
+    jump[...] = jnp.where(in_first_half(both), both - other, both + other)
+    shift = lam_a[...] + row_b
+    spike = spike_of(shift, nz)
+    weight = c0[...]
+    loads = [weight * g for g in spike]
+    bottoms, tops = [], []
     for s in range(slabs):
+        low, high = ends[s, 0:hx, :], ends[s, hx:nx, :]
+        for k in range(nz):
+            q = jump[s * nz + k : s * nz + k + 1, :]
+            low = low + loads[k] * q
+            high = high + loads[nz - 1 - k] * q
+        bottoms.append(low)
+        tops.append(high)
+    below, above = interface_chain(spike[0], spike[nz - 1], bottoms, tops)
+    for s in range(slabs):
+        out[s, 0:hx, :] = below[s]
+        out[s, hx:nx, :] = above[s]
         out[s, nx : nx + nz, :] = both[s * nz : (s + 1) * nz, :]
-
-    def block(n, carry):
-        at = pl.ds(pl.multiple_of(n * 8, 8), 8)
-        parity = n // (blocks // 2)
-        shift = lam_a[at, :width] + row_b
-        spike = spike_of(shift, nz)
-        weight = c0[at, :width]
-        loads = [weight * g for g in spike]
-        bottoms, tops = [], []
-        for s in range(slabs):
-            pair = ends[s, at, :]
-            low, high = pair[:, :width], pair[:, width:]
-            for k in range(nz):
-                q = jnp.broadcast_to(jump[parity, pl.ds(s * nz + k, 1), :], low.shape)
-                low = low + loads[k] * q
-                high = high + loads[nz - 1 - k] * q
-            bottoms.append(low)
-            tops.append(high)
-        below, above = interface_chain(spike[0], spike[nz - 1], bottoms, tops)
-        for s in range(slabs):
-            out[s, at, :] = jnp.concatenate([below[s], above[s]], 1)
-        return carry
-
-    lax.fori_loop(0, blocks, block, 0)
 
 
 def backward_kernel(
@@ -381,8 +379,11 @@
         west, east_end = [], []
         for j in range(slabs):
             lanes = slice(j * width, (j + 1) * width)
-            below[:, lanes] = solved[j, 0:nx, :width]
-            above[:, lanes] = solved[j, 0:nx, width:]
+            hx = nx // 2
+            below[:hx, lanes] = solved[j, 0:hx, :width]
+            below[hx:, lanes] = solved[j, 0:hx, width:]
+            above[:hx, lanes] = solved[j, hx:nx, :width]
+            above[hx:, lanes] = solved[j, hx:nx, width:]
             west.append(solved[j, nx : nx + nz, :width])
             east_end.append(solved[j, nx : nx + nz, width:])
         west = jnp.concatenate(west, 1)
@@ -499,7 +500,12 @@
     lam_a = np.repeat(lam_a_np[:, None], 128, 1).astype(np.float32)
     c0 = np.repeat(block_np[:, :1], 128, 1).astype(np.float32)
     lam_b = np.repeat(lam_b_np[None], 8, 0).astype(np.float32)
-    lam_b_part = np.repeat(lam_b_np.reshape(slabs, 1, width), 8, 1).astype(np.float32)
+    part = np.tile(lam_b_np.reshape(slabs, 1, width), (1, 8, 2)).astype(np.float32)
+
+    def paired(column):
+        return np.repeat(column.reshape(2, nx // 2).T, width, 1).astype(np.float32)
+
+    lam_pair, c0_pair = paired(lam_a_np), paired(block_np[:, 0])
     mu = np.repeat(mu_np[:, None], 128, 1).astype(np.float32)
 
     chunk = 16
@@ -565,20 +571,20 @@
     own = pl.pallas_call(
         functools.partial(ends_kernel, nz),
         out_shape=jax.ShapeDtypeStruct((total, 2 * width), F32),
-        scratch_shapes=[pltpu.VMEM((2, total * 8, width), F32)],
+        scratch_shapes=[pltpu.VMEM((total * 8, 2 * width), F32)],
         compiler_params=single,
         name="ends",
-    )(ends, lam_a, lam_b_part, c0, sum_h, sum_l, sine_h, sine_l)
+    )(ends, lam_pair, part, c0_pair, sum_h, sum_l, sine_h, sine_l)
     found = [own]
     for shift in range(1, groups):
         found.append(lax.ppermute(own, "xy", [((i + shift) % groups, i) for i in range(groups)]))
     solved = pl.pallas_call(
         functools.partial(correct_kernel, nz, groups),
         out_shape=ends_shape,
-        scratch_shapes=[pltpu.VMEM((2, total, width), F32)],
+        scratch_shapes=[pltpu.VMEM((total, 2 * width), F32)],
         compiler_params=single,
         name="correct",
-    )(ends, jnp.concatenate(found, 0), lam_a, lam_b_part, mu, c0, sine_h, sine_l)
+    )(ends, *found, lam_pair, part, mu, c0_pair, sine_h, sine_l)
     solved = lax.all_to_all(solved, "gz", split_axis=0, concat_axis=0, tiled=True)
 
     tables = (te_h, te_l, ti_h, ti_l, ct_h, ct_l, lam_a, lam_b, c0)

time: 144 us -> 106 us (0.74)
  Pallas kernels: 86.1 us -> 48.8 us
    pallas_call x1, Pallas kernels: 21.3 us -> 2.56 us  [local(): pl.pallas_call(functools.partial(ends_kernel, nz), out_shape=jax.ShapeDty...]
    pallas_call x1, Pallas kernels: 21.4 us -> 2.88 us  [local(): pl.pallas_call(functools.partial(correct_kernel, nz, groups), out_shape=e...]
  transfers between devices with their start and end apart: 9 -> 9, of which waited for: 5 -> 5; matrix products, arithmetic and copies ran while one was open for 1% -> 2% of each run, Pallas kernels for 0% -> 0%
where the time goes in v2:
time: 106 us; the launch traced here: 105 us
  Pallas kernels  48.8 us (46%)
  starting transfers between devices  20.2 us (19%)
  blocking collectives  15.5 us (15%)
  waiting for transfers between devices  15.3 us (14%)
  local copies, waits for them, and re-layouts  2.9 us (3%)
  other arithmetic  1.49 us (1%)
    pallas_call x1, Pallas kernels, local(): pl.pallas_call(functools.partial(backward_kernel, nz, slabs), grid=(steps...  21 us
    pallas_call x1, Pallas kernels, local(): pl.pallas_call(functools.partial(forward_kernel, nz, slabs), grid=(steps,...  18.5 us
    all_to_all x1, blocking collectives, local(): ends = lax.all_to_all(ends, 'gz', split_axis=0, concat_axis=0, tiled=True)  15.5 us
    ppermute x1, waiting for transfers between devices, local(): f_above = lax.ppermute(f_bot, 'gz', falling)  9.27 us
    all_to_all x1, starting transfers between devices, local(): lax.all_to_all(solved, 'gz', split_axis=0, concat_axis=0, tiled=True)  5.09 us
    ppermute x1, starting transfers between devices, local(): f_below = lax.ppermute(f_top, 'gz', rising)  4.49 us
    pallas_call x1, Pallas kernels, local(): pl.pallas_call(functools.partial(first_rows, nz), grid=(ny // 128,), in_s...  3.94 us
    ppermute x1, starting transfers between devices, local(): lax.ppermute(jnp.concatenate([f_first, f_first * east[:nz]], 0), 'xy', to...  3.37 us
  transfers between devices with their start and end apart: 9, of which 5 were waited for; matrix products, arithmetic and copies ran while one was open for 2% of the time, Pallas kernels for 0%

profile of v2, /device:TPU:1, one launch (start us, length us, event | category | flops | bytes accessed | tf_op | source)
XLA Modules:
  0.0 104.9 jit_solution(12767815646961208422)
XLA Ops:
  0.6 3.9 %planes.1 = (f32[128,512]{1,0:T(8,128)}, f32[128,512]{1,0:T(8,128)}, f32[128,512]{1,0:T(8,128)}) custom-call(s32[1024,512]{1,0:T(8,128)} %bitcast.17, f32[1024,512]{1,0:T(8,128)} %bitcast.28), custom_call_target="tpu_custom_call" | custom-call | tf_op jit(solution)/shard_map/planes/pallas_call | solution.py:524
  4.6 4.5 %collective-permute-start.2 = (f32[128,512]{1,0:T(8,128)}, f32[128,512]{1,0:T(8,128)S(1)}, u32[]{:S(2)}, u32[]{:S(2)}) collective-permute-start(f32[128,512]{1,0:T(8,128)} %get-tuple-element.15), channel_id=1, source_target_pairs={{0,4},{4,8},{8,12},{12,16},{16,20},{20,24},{24,28},{1,5},{5,9},{9,... | collective-permute-start | bytes 786440 | tf_op jit(solution)/shard_map/ppermute | solution.py:538
  9.1 1.9 %collective-permute-start.3 = (f32[128,512]{1,0:T(8,128)}, f32[128,512]{1,0:T(8,128)S(1)}, u32[]{:S(2)}, u32[]{:S(2)}) collective-permute-start(f32[128,512]{1,0:T(8,128)} %get-tuple-element.16), channel_id=1, source_target_pairs={{4,0},{8,4},{12,8},{16,12},{20,16},{24,20},{28,24},{5,1},{9,5},{13... | collective-permute-start | bytes 786440 | tf_op jit(solution)/shard_map/ppermute | solution.py:539
  11.0 0.7 convert_bitcast_fusion
  11.7 0.7 bitcast_multiply_fusion
  12.5 3.4 %collective-permute-start.1 = (f32[16,512]{1,0:T(8,128)S(1)}, f32[16,512]{1,0:T(8,128)S(1)}, u32[]{:S(2)}, u32[]{:S(2)}) collective-permute-start(f32[16,512]{1,0:T(8,128)S(1)} %pad_maximum_fusion), channel_id=1, source_target_pairs={{1,0},{2,1},{3,2},{0,3},{5,4},{6,5},{7,6},{4,7},{9,8},{10,9},{11,1... | collective-permute-start | bytes 98312 | tf_op jit(solution)/shard_map/ppermute | solution.py:542
  15.9 0.0 collective-permute-start
  15.9 1.0 collective-permute-done.1
  16.9 0.6 fusion
  17.5 2.8 %collective-permute-done.f_west = f32[8,512]{1,0:T(8,128)S(1)} collective-permute-done((f32[8,512]{1,0:T(8,128)S(1)}, f32[8,512]{1,0:T(8,128)S(1)}, u32[]{:S(2)}, u32[]{:S(2)}) %collective-permute-start) | collective-permute-done | bytes 16416 | tf_op jit(solution)/shard_map/ppermute | solution.py:541
  20.2 0.0 copy-start.4
  20.2 0.0 collective-permute-done.2.f_below
  20.2 0.0 copy-start.1
  20.2 0.0 collective-permute-done.3.g_above
  20.3 0.0 copy-start.2
  20.3 0.6 copy-done.4
  20.8 0.1 copy-done.1
  21.0 0.1 copy-done.2
  21.0 18.5 %forward.1 = (f32[8,128,512]{2,1,0:T(8,128)}, f32[8,136,128]{2,1,0:T(8,128)}) custom-call(s32[1024,512]{1,0:T(8,128)} %bitcast.18, s32[1024,512]{1,0:T(8,128)} %bitcast.19, s32[1024,512]{1,0:T(8,128)} %bitcast.20, f32[1024,512]{1,0:T(8,128)} %bitcast.24, f32[1024,512]{1,0:T(8,128)} %bitcast.25, f32[1024,512]{1,0:T(8,128)} %bitcast.31, f32[1024,512]{1,0:T(8,128)} %bitcast.29, ...), custom_call_target="tpu_custom_call" | custom-call | tf_op jit(solution)/shard_map/forward/pallas_call | solution.py:548
  39.5 0.0 copy-start.8
  39.5 15.5 %all_to_all.10.ends = f32[8,136,128]{2,1,0:T(8,128)} all-to-all(f32[8,136,128]{2,1,0:T(8,128)} %get-tuple-element.18), channel_id=1, replica_groups=mesh['gz'=8,'xy'=4] {'gz'}, dimensions={0} | all-to-all | bytes 1114112 | tf_op jit(solution)/shard_map/all_to_all | solution.py:570
  55.1 2.6 %ends.1.rest_0_ = f32[64,128]{1,0:T(8,128)} custom-call(f32[8,136,128]{2,1,0:T(8,128)} %all_to_all.10.ends, f32[64,128]{1,0:T(8,128)} %constant.53.clone.lam_a.rest_4_, f32[8,8,128]{2,1,0:T(8,128)} %constant.54.clone.lam_b.rest_5_, f32[64,128]{1,0:T(8,128)} %constant.55.clone.c0.rest_7_, bf16[64,512]{1,0:T(8,128)(2,1)} %constant.56.clone.sum_h, ...), custom_call_target="tpu_custom_call" | custom-call | tf_op jit(solution)/shard_map/ends/pallas_call | solution.py:571
  57.6 0.0 collective-permute-start.6
  57.6 0.8 collective-permute-start.5
  58.4 2.5 %collective-permute-start.4 = (f32[64,128]{1,0:T(8,128)}, f32[64,128]{1,0:T(8,128)S(1)}, u32[]{:S(2)}, u32[]{:S(2)}) collective-permute-start(f32[64,128]{1,0:T(8,128)} %ends.1.rest_0_), channel_id=1, source_target_pairs={{1,0},{2,1},{3,2},{0,3},{5,4},{6,5},{7,6},{4,7},{9,8},{10,9},{11,1... | collective-permute-start | bytes 98312 | tf_op jit(solution)/shard_map/ppermute | solution.py:580
  60.9 1.5 %collective-permute-done.6.rest_3_ = f32[64,128]{1,0:T(8,128)S(1)} collective-permute-done((f32[64,128]{1,0:T(8,128)}, f32[64,128]{1,0:T(8,128)S(1)}, u32[]{:S(2)}, u32[]{:S(2)}) %collective-permute-start.6) | collective-permute-done | bytes 32800 | tf_op jit(solution)/shard_map/ppermute | solution.py:580
  62.4 0.0 copy-start.5
  62.4 0.0 collective-permute-done.5.rest_2_
  62.4 0.0 copy-start.6
  62.4 0.7 collective-permute-done.4.rest_1_
  63.1 0.0 copy-done.5
  63.1 0.0 copy-done.6
  63.1 0.0 copy-start.7
  63.1 0.6 copy-done.7
  63.7 2.9 %correct.1 = f32[8,136,128]{2,1,0:T(8,128)} custom-call(f32[8,136,128]{2,1,0:T(8,128)} %all_to_all.10.ends, f32[64,128]{1,0:T(8,128)} %ends.1.rest_0_, f32[64,128]{1,0:T(8,128)} %copy-done.7, f32[64,128]{1,0:T(8,128)} %copy-done.6, f32[64,128]{1,0:T(8,128)} %copy-done.5, f32[64,128]{1,0:T(8,128)} %constant.53.clone.lam_a.rest_4_, ...), custom_call_target="tpu_custom_call" | custom-call | tf_op jit(solution)/shard_map/correct/pallas_call | solution.py:581
  66.6 5.1 %all-to-all-start.1 = ((f32[8,136,128]{2,1,0:T(8,128)}), f32[8,136,128]{2,1,0:T(8,128)S(1)}, u32[]{:S(2)}, u32[]{:S(2)}) async-start(f32[8,136,128]{2,1,0:T(8,128)} %correct.1), calls=%async_computation.1 | async-start | bytes 1114112 | tf_op jit(solution)/shard_map/all_to_all | solution.py:588
  71.7 0.0 copy-done.8
  71.7 2.0 %collective-permute-start.7 = (f32[128,512]{1,0:T(8,128)S(1)}, f32[128,512]{1,0:T(8,128)S(1)}, u32[]{:S(2)}, u32[]{:S(2)}) collective-permute-start(f32[128,512]{1,0:T(8,128)S(1)} %copy-done.8), channel_id=1, source_target_pairs={{4,0},{8,4},{12,8},{16,12},{20,16},{24,20},{28,24},{5,1},{9,5},{13... | collective-permute-start | bytes 786440 | tf_op jit(solution)/shard_map/ppermute | solution.py:544
  73.7 9.3 %collective-permute-done.7.f_above = f32[128,512]{1,0:T(8,128)S(1)} collective-permute-done((f32[128,512]{1,0:T(8,128)S(1)}, f32[128,512]{1,0:T(8,128)S(1)}, u32[]{:S(2)}, u32[]{:S(2)}) %collective-permute-start.7) | collective-permute-done | bytes 262176 | tf_op jit(solution)/shard_map/ppermute | solution.py:544
  83.0 0.0 copy-start.3
  83.0 0.0 all-to-all-done.1.solved
  83.0 0.0 copy-start
  83.0 0.7 copy-done.3
  83.7 0.2 copy-done
  83.9 21.0 %backward.1 = (f32[1024,512]{1,0:T(8,128)}, f32[1024,512]{1,0:T(8,128)}, f32[1024,512]{1,0:T(8,128)}, f32[1024,512]{1,0:T(8,128)}, f32[1024,512]{1,0:T(8,128)}) custom-call(f32[8,128,512]{2,1,0:T(8,128)} %get-tuple-element.17.modes, f32[8,136,128]{2,1,0:T(8,128)} %copy-done, s32[1024,512]{1,0:T(8,128)} %bitcast.21, s32[1024,512]{1,0:T(8,128)} %bitcast.22, ...), custom_call_target="tpu_custom_call" | custom-call | tf_op jit(solution)/shard_map/backward/pallas_call | solution.py:592
  (1 shorter events, 0.0 us)
Async XLA Ops:
  4.6 15.7 %collective-permute-start.2 = (f32[128,512]{1,0:T(8,128)}, f32[128,512]{1,0:T(8,128)S(1)}, u32[]{:S(2)}, u32[]{:S(2)}) collective-permute-start(f32[128,512]{1,0:T(8,128)} %get-tuple-element.15), channel_id=1, source_target_pairs={{0,4},{4,8},{8,12},{12,16},{16,20},{20,24},{24,28},{1,5},{5,9},{9,... | collective-permute-start | bytes 786440 | tf_op jit(solution)/shard_map/ppermute | solution.py:538
  9.1 11.2 %collective-permute-start.3 = (f32[128,512]{1,0:T(8,128)}, f32[128,512]{1,0:T(8,128)S(1)}, u32[]{:S(2)}, u32[]{:S(2)}) collective-permute-start(f32[128,512]{1,0:T(8,128)} %get-tuple-element.16), channel_id=1, source_target_pairs={{4,0},{8,4},{12,8},{16,12},{20,16},{24,20},{28,24},{5,1},{9,5},{13... | collective-permute-start | bytes 786440 | tf_op jit(solution)/shard_map/ppermute | solution.py:539
  12.5 4.4 %collective-permute-start.1 = (f32[16,512]{1,0:T(8,128)S(1)}, f32[16,512]{1,0:T(8,128)S(1)}, u32[]{:S(2)}, u32[]{:S(2)}) collective-permute-start(f32[16,512]{1,0:T(8,128)S(1)} %pad_maximum_fusion), channel_id=1, source_target_pairs={{1,0},{2,1},{3,2},{0,3},{5,4},{6,5},{7,6},{4,7},{9,8},{10,9},{11,1... | collective-permute-start | bytes 98312 | tf_op jit(solution)/shard_map/ppermute | solution.py:542
  15.9 4.4 %collective-permute-start = (f32[8,512]{1,0:T(8,128)S(1)}, f32[8,512]{1,0:T(8,128)S(1)}, u32[]{:S(2)}, u32[]{:S(2)}) collective-permute-start(f32[8,512]{1,0:T(8,128)S(1)} %get-tuple-element.26), channel_id=1, source_target_pairs={{0,1},{1,2},{2,3},{3,0},{4,5},{5,6},{6,7},{7,4},{8,9},{9,10},{10,1... | collective-permute-start | bytes 49160 | tf_op jit(solution)/shard_map/ppermute | solution.py:541
  20.2 0.6 copy-start.4
  20.2 0.7 copy-start.1
  20.3 0.8 copy-start.2
  39.5 32.2 %copy-start.8 = (f32[128,512]{1,0:T(8,128)S(1)}, f32[128,512]{1,0:T(8,128)}, u32[]{:S(2)}) copy-start(f32[128,512]{1,0:T(8,128)} %get-tuple-element.19) | copy-start | bytes 786436
  57.6 4.8 %collective-permute-start.6 = (f32[64,128]{1,0:T(8,128)}, f32[64,128]{1,0:T(8,128)S(1)}, u32[]{:S(2)}, u32[]{:S(2)}) collective-permute-start(f32[64,128]{1,0:T(8,128)} %ends.1.rest_0_), channel_id=1, source_target_pairs={{3,0},{0,1},{1,2},{2,3},{7,4},{4,5},{5,6},{6,7},{11,8},{8,9},{9,10... | collective-permute-start | bytes 98312 | tf_op jit(solution)/shard_map/ppermute | solution.py:580
  57.6 4.8 %collective-permute-start.5 = (f32[64,128]{1,0:T(8,128)}, f32[64,128]{1,0:T(8,128)S(1)}, u32[]{:S(2)}, u32[]{:S(2)}) collective-permute-start(f32[64,128]{1,0:T(8,128)} %ends.1.rest_0_), channel_id=1, source_target_pairs={{2,0},{3,1},{0,2},{1,3},{6,4},{7,5},{4,6},{5,7},{10,8},{11,9},{8,1... | collective-permute-start | bytes 98312 | tf_op jit(solution)/shard_map/ppermute | solution.py:580
  58.4 4.7 %collective-permute-start.4 = (f32[64,128]{1,0:T(8,128)}, f32[64,128]{1,0:T(8,128)S(1)}, u32[]{:S(2)}, u32[]{:S(2)}) collective-permute-start(f32[64,128]{1,0:T(8,128)} %ends.1.rest_0_), channel_id=1, source_target_pairs={{1,0},{2,1},{3,2},{0,3},{5,4},{6,5},{7,6},{4,7},{9,8},{10,9},{11,1... | collective-permute-start | bytes 98312 | tf_op jit(solution)/shard_map/ppermute | solution.py:580
  62.4 0.7 copy-start.5
  62.4 0.7 copy-start.6
  63.1 0.6 copy-start.7
  66.6 16.4 %all-to-all-start.1 = ((f32[8,136,128]{2,1,0:T(8,128)}), f32[8,136,128]{2,1,0:T(8,128)S(1)}, u32[]{:S(2)}, u32[]{:S(2)}) async-start(f32[8,136,128]{2,1,0:T(8,128)} %correct.1), calls=%async_computation.1 | async-start | bytes 1114112 | tf_op jit(solution)/shard_map/all_to_all | solution.py:588
  71.7 11.3 %collective-permute-start.7 = (f32[128,512]{1,0:T(8,128)S(1)}, f32[128,512]{1,0:T(8,128)S(1)}, u32[]{:S(2)}, u32[]{:S(2)}) collective-permute-start(f32[128,512]{1,0:T(8,128)S(1)} %copy-done.8), channel_id=1, source_target_pairs={{4,0},{8,4},{12,8},{16,12},{20,16},{24,20},{28,24},{5,1},{9,5},{13... | collective-permute-start | bytes 786440 | tf_op jit(solution)/shard_map/ppermute | solution.py:544
  83.0 0.7 copy-start.3
  83.0 0.9 copy-start

commit v3 on v2

--- a/solution.py
+++ b/solution.py
@@ -11,7 +11,7 @@
 
 F32 = jnp.float32
 BF16 = jnp.bfloat16
-VMEM_LIMIT = 60 * 1024 * 1024
+VMEM_LIMIT = 24 * 1024 * 1024
 
 
 def pair_np(table):
@@ -135,12 +135,12 @@
         ref[start + n, rows, :] = value[:, n * 128 : (n + 1) * 128]
 
 
-def first_rows(nz, obs, up, ftop, fbot, gbot):
-    rows = ftop.shape[0]
-    ftop[...] = (1 - obs[pl.ds(nz - 1, rows, stride=nz), :]).astype(F32)
-    low = (1 - obs[pl.ds(0, rows, stride=nz), :]).astype(F32)
-    fbot[...] = low
-    gbot[...] = low * up[pl.ds(0, rows, stride=nz), :]
+def planes_kernel(nz, obs, up, high, low):
+    rows = high.shape[0]
+    high[...] = (1 - obs[pl.ds(nz - 1, rows, stride=nz), :]).astype(F32)
+    fluid = (1 - obs[pl.ds(0, rows, stride=nz), :]).astype(F32)
+    low[0] = fluid
+    low[1] = fluid * up[pl.ds(0, rows, stride=nz), :]
 
 
 def north_roll(value, shift):
@@ -164,87 +164,130 @@
     return (1 - block).astype(F32)
 
 
-def forward_kernel(
-    nz, slabs,
+def stack_left(table):
+    high, low = pair_np(table)
+    return np.concatenate([high, low], 1), high
+
+
+def east_dot(left, value):
+    high, low = split(value)
+    dot = functools.partial(jnp.dot, preferred_element_type=F32)
+    return dot(left[0], jnp.concatenate([high, high], 0)) + dot(left[1], low)
+
+
+def north_forward(value, even, odd):
+    half = value.shape[1] // 2
+    low, high = value[:, :half], value[:, half:]
+    return dot3(split(low + high), even), dot3(split(low - high), odd)
+
+
+def interior_kernel(
+    nz,
     obs, obs_prev, obs_next, east, east_next, north, up,
-    f_west, f_east, g_east, f_below, g_above,
-    te_h, te_l, to_h, to_l, c_h, c_l, lam_a, lam_b, c0,
-    modes, out,
-    src, half, bottom, top, acc,
+    te_h, te_l, to_h, to_l, c_hl, c_h,
+    modes,
+    src, half,
 ):
     step = pl.program_id(0)
-    steps = pl.num_programs(0)
+    last = step == pl.num_programs(0) - 1
     chunk = src.shape[0] // nz
     ny = src.shape[1]
-    nx = chunk * steps
-    first_slab = lax.axis_index("gz") == 0
-    lift = jnp.where(first_slab, 1.0, 0.0).astype(F32)
-
-    fluid_prev = jnp.where(step == 0, f_west[...], fluid_of(obs_prev[...]))
-    last = step == steps - 1
-    after_fluid = fluid_of(obs_next[...])
-    flux_after = jnp.where(last, g_east[...], after_fluid * east_next[...])
-
-    def row(i, carry):
-        fluid, masked = carry
-        at = pl.multiple_of(i * nz, nz)
-        nxt = pl.multiple_of(jnp.minimum(i + 1, chunk - 1) * nz, nz)
-        end = i == chunk - 1
-        fluid_next = fluid_of(obs[pl.ds(nxt, nz), :])
-        flux = jnp.where(end, flux_after, fluid_next * east[pl.ds(nxt, nz), :])
+    nx = chunk * pl.num_programs(0)
+
+    fluid_prev = jnp.where(step == 0, 0.0, fluid_of(obs_prev[...]))
+    flux_after = jnp.where(last, 0.0, fluid_of(obs_next[...]) * east_next[...])
+    none = jnp.zeros((1, ny), F32)
+    fluid = fluid_of(obs[0:nz, :])
+    masked = fluid * fluid_prev * east[0:nz, :]
+    for i in range(chunk):
+        at = slice(i * nz, (i + 1) * nz)
+        if i < chunk - 1:
+            nxt = slice((i + 1) * nz, (i + 2) * nz)
+            fluid_next = fluid_of(obs[nxt, :])
+            flux = fluid_next * east[nxt, :]
+        else:
+            fluid_next, flux = None, flux_after
         masked_next = fluid * flux
-        north_masked = fluid * north_roll(fluid, 1) * north[pl.ds(at, nz), :]
-        below = below_of(fluid, f_below[pl.ds(i, 1), :] + lift)
-        up_masked = fluid * below * up[pl.ds(at, nz), :]
-        up_after = above_of(up_masked, fluid[nz - 1 : nz, :] * g_above[pl.ds(i, 1), :])
-        src[pl.ds(at, nz), :] = (
-            (masked - masked_next) + (north_masked - north_roll(north_masked, -1)) + (up_masked - up_after)
+        north_masked = fluid * north_roll(fluid, 1) * north[at, :]
+        up_masked = fluid * below_of(fluid, none) * up[at, :]
+        src[at, :] = (
+            (masked - masked_next)
+            + (north_masked - north_roll(north_masked, -1))
+            + (up_masked - above_of(up_masked, none))
         )
-        return fluid_next, masked_next
-
-    start = fluid_of(obs[0:nz, :])
-    lax.fori_loop(0, chunk, row, (start, start * fluid_prev * east[0:nz, :]), unroll=2)
-
-    hy = ny // 2
-    low, high = src[:, :hy], src[:, hy:]
+        fluid, masked = fluid_next, masked_next
+
     rows = pl.ds(pl.multiple_of(step * chunk * nz, chunk * nz), chunk * nz)
-    put_lanes(half, rows, dot3(split(low + high), (te_h[...], te_l[...])), 0)
-    put_lanes(half, rows, dot3(split(low - high), (to_h[...], to_l[...])), hy // 128)
+    even, odd = north_forward(src[...], (te_h[...], te_l[...]), (to_h[...], to_l[...]))
+    put_lanes(half, rows, even, 0)
+    put_lanes(half, rows, odd, ny // 256)
 
     @pl.when(last)
     def _():
-        left = (c_h[...], c_l[...])
+        left = (c_hl[...], c_h[...])
         for k in range(nz):
-            modes[k] = dot3(left, split(get_lanes(half, pl.ds(k, nx, stride=nz))))
-        acc[...] = jnp.zeros_like(acc)
-        blocks = nx // 8
-
-        def solve(n, carry):
-            at = pl.ds(pl.multiple_of(n * 8, 8), 8)
-            parity = n // (blocks // 2)
-            for lane in range(0, ny, 128):
-                lanes = slice(lane, lane + 128)
-                shift = lam_a[at, :] + lam_b[:, lanes]
-                local = slab_solve(shift, [modes[k, at, lanes] for k in range(nz)])
-                bottom[at, lanes] = local[0]
-                top[at, lanes] = local[nz - 1]
-                weight = c0[at, :]
-                for k in range(nz):
-                    acc[parity, k, :, lanes] += weight * local[k]
-            return carry
-
-        lax.fori_loop(0, blocks, solve, 0)
-        even = [jnp.sum(acc[0, k], axis=0, keepdims=True) for k in range(nz)]
-        odd = [jnp.sum(acc[1, k], axis=0, keepdims=True) for k in range(nz)]
-        west = jnp.concatenate([e + o for e, o in zip(even, odd)], 0)
-        east_end = jnp.concatenate([e - o for e, o in zip(even, odd)], 0)
-        width = ny // slabs
-        for j in range(slabs):
-            lanes = slice(j * width, (j + 1) * width)
-            hx = nx // 2
-            out[j, 0:hx, :] = jnp.concatenate([bottom[:hx, lanes], bottom[hx:, lanes]], 1)
-            out[j, hx:nx, :] = jnp.concatenate([top[:hx, lanes], top[hx:, lanes]], 1)
-            out[j, nx : nx + nz, :] = jnp.concatenate([west[:, lanes], east_end[:, lanes]], 1)
+            modes[k] = east_dot(left, get_lanes(half, pl.ds(k, nx, stride=nz)))
+
+
+def joined_kernel(
+    nz, slabs,
+    modes_in, high, low, f_below, low_above, first, side_west, side_east,
+    te_h, te_l, to_h, to_l, c_hl, c_h, lam_a, lam_b, c0,
+    modes, out,
+    bottom, top, acc, edge,
+):
+    nx, ny = high.shape
+    lift = jnp.where(lax.axis_index("gz") == 0, 1.0, 0.0).astype(F32)
+    even_table, odd_table = (te_h[...], te_l[...]), (to_h[...], to_l[...])
+    lower = low[1] * (f_below[...] + lift)
+    upper = -(high[...] * low_above[1])
+    west = first[nz : 2 * nz, :] * side_west[...]
+    east_end = -(first[2 * nz :, :] * side_east[nz:, :])
+    stacked = jnp.concatenate([lower, upper, west, east_end], 0)
+    stacked = jnp.concatenate(north_forward(stacked, even_table, odd_table), 1)
+    left = (c_hl[...], c_h[...])
+    bottom[...] = east_dot(left, stacked[:nx])
+    top[...] = east_dot(left, stacked[nx : 2 * nx])
+    west, east_end = stacked[2 * nx : 2 * nx + nz], stacked[2 * nx + nz :]
+    edge[0] = west + east_end
+    edge[1] = west - east_end
+    acc[...] = jnp.zeros_like(acc)
+    blocks = nx // 8
+
+    def solve(n, carry):
+        at = pl.ds(pl.multiple_of(n * 8, 8), 8)
+        parity = n // (blocks // 2)
+        for lane in range(0, ny, 128):
+            lanes = slice(lane, lane + 128)
+            shift = lam_a[at, :] + lam_b[:, lanes]
+            weight = c0[at, :]
+            right = []
+            for k in range(nz):
+                q = jnp.broadcast_to(edge[parity, pl.ds(k, 1), lanes], weight.shape)
+                right.append(modes_in[k, at, lanes] + weight * q)
+            right[0] = right[0] + bottom[at, lanes]
+            right[nz - 1] = right[nz - 1] + top[at, lanes]
+            for k in range(nz):
+                modes[k, at, lanes] = right[k]
+            local = slab_solve(shift, right)
+            bottom[at, lanes] = local[0]
+            top[at, lanes] = local[nz - 1]
+            for k in range(nz):
+                acc[parity, k, :, lanes] += weight * local[k]
+        return carry
+
+    lax.fori_loop(0, blocks, solve, 0)
+    even = [jnp.sum(acc[0, k], axis=0, keepdims=True) for k in range(nz)]
+    odd = [jnp.sum(acc[1, k], axis=0, keepdims=True) for k in range(nz)]
+    west = jnp.concatenate([e + o for e, o in zip(even, odd)], 0)
+    east_end = jnp.concatenate([e - o for e, o in zip(even, odd)], 0)
+    width = ny // slabs
+    hx = nx // 2
+    for j in range(slabs):
+        lanes = slice(j * width, (j + 1) * width)
+        out[j, 0:hx, :] = jnp.concatenate([bottom[:hx, lanes], bottom[hx:, lanes]], 1)
+        out[j, hx:nx, :] = jnp.concatenate([top[:hx, lanes], top[hx:, lanes]], 1)
+        out[j, nx : nx + nz, :] = jnp.concatenate([west[:, lanes], east_end[:, lanes]], 1)
 
 
 def swap_halves(value):
@@ -355,31 +398,28 @@
 
 
 def backward_kernel(
-    nz, slabs,
+    nz, slabs, chunk,
     modes, solved,
-    obs, obs_prev, obs_next, east, east_next, north, up,
-    f_west, f_east, g_east, f_below, g_above, f_above,
-    te_h, te_l, ti_h, ti_l, ct_h, ct_l, lam_a, lam_b, c0,
+    obs, east, north, up,
+    side_west, side_east, f_below, low_above,
+    te_h, te_l, ti_h, ti_l, ct_hl, ct_h, lam_a, lam_b, c0,
     out_east, out_north, out_up, out_p, out_r,
     below, above, found, half, press, p_below, p_above,
 ):
     step = pl.program_id(0)
-    steps = pl.num_programs(0)
-    chunk = obs.shape[0] // nz
+    last = step == pl.num_programs(0) - 1
     ny = obs.shape[1]
     hy = ny // 2
-    nx = chunk * steps
-    first_slab = lax.axis_index("gz") == 0
-    lift = jnp.where(first_slab, 1.0, 0.0).astype(F32)
-    last = step == steps - 1
+    nx = chunk * pl.num_programs(0)
+    lift = jnp.where(lax.axis_index("gz") == 0, 1.0, 0.0).astype(F32)
 
     @pl.when(step == 0)
     def _():
         width = ny // slabs
         west, east_end = [], []
+        hx = nx // 2
         for j in range(slabs):
             lanes = slice(j * width, (j + 1) * width)
-            hx = nx // 2
             below[:hx, lanes] = solved[j, 0:hx, :width]
             below[hx:, lanes] = solved[j, 0:hx, width:]
             above[:hx, lanes] = solved[j, hx:nx, :width]
@@ -413,9 +453,9 @@
             return carry
 
         lax.fori_loop(0, blocks, solve, 0)
-        left = (ct_h[...], ct_l[...])
+        left = (ct_hl[...], ct_h[...])
         for k in range(nz):
-            put_lanes(half, pl.ds(nz + k, nx, stride=nz), dot3(left, split(modes[k])), 0)
+            put_lanes(half, pl.ds(nz + k, nx, stride=nz), east_dot(left, modes[k]), 0)
         first, final = slice(nz, 2 * nz), slice(nx * nz, (nx + 1) * nz)
         put_lanes(half, slice(0, nz), get_lanes(half, first) + found[2], 0)
         put_lanes(half, slice((nx + 1) * nz, (nx + 2) * nz), get_lanes(half, final) - found[3], 0)
@@ -425,9 +465,11 @@
             odd = dot3(split(value[:, hy:]), (ti_h[...], ti_l[...]))
             return even + odd, even - odd
 
-        p_below[:, :hy], p_below[:, hy:] = north_back(dot3(left, split(below[...])))
-        p_above[:, :hy], p_above[:, hy:] = north_back(dot3(left, split(above[...])))
-        size = 16 * nz
+        both = jnp.concatenate([east_dot(left, below[...]), east_dot(left, above[...])], 0)
+        both = jnp.concatenate(north_back(both), 1)
+        p_below[...] = both[:nx]
+        p_above[...] = both[nx:]
+        size = 32 * nz
 
         def back(n, carry):
             at = pl.ds(pl.multiple_of(n * size, size), size)
@@ -438,30 +480,36 @@
         at = slice(nx * nz, (nx + 2) * nz)
         press[at, :hy], press[at, hy:] = north_back(get_lanes(half, at))
 
-    fluid_prev = jnp.where(step == 0, f_west[...], fluid_of(obs_prev[...]))
-    after_fluid = jnp.where(last, f_east[...], fluid_of(obs_next[...]))
-    flux_after = jnp.where(last, g_east[...], fluid_of(obs_next[...]) * east_next[...])
     base = step * chunk
 
-    def rows_of(i):
-        return pl.ds(pl.multiple_of((base + i + 1) * nz, nz), nz)
-
-    def row(i, carry):
-        fluid, p, east_done = carry
-        at = pl.ds(pl.multiple_of(i * nz, nz), nz)
-        nxt = pl.ds(pl.multiple_of(jnp.minimum(i + 1, chunk - 1) * nz, nz), nz)
-        end = i == chunk - 1
-        fluid_next = jnp.where(end, after_fluid, fluid_of(obs[nxt, :]))
-        flux = jnp.where(end, flux_after, fluid_next * east[nxt, :])
-        p_next = press[rows_of(i + 1), :]
+    def cells(x):
+        return pl.ds(pl.multiple_of(x * nz, nz), nz)
+
+    fluid_prev = jnp.where(step == 0, side_west[...], fluid_of(obs[cells(jnp.maximum(base - 1, 0)), :]))
+    after = cells(jnp.minimum(base + chunk, nx - 1))
+    after_fluid = jnp.where(last, side_east[0:nz, :], fluid_of(obs[after, :]))
+    after_flux = jnp.where(last, side_east[nz:, :], fluid_of(obs[after, :]) * east[after, :])
+
+    fluid = fluid_of(obs[cells(base), :])
+    p = press[cells(base + 1), :]
+    east_done = fluid * fluid_prev * (east[cells(base), :] - (p - press[cells(base), :]))
+    for i in range(chunk):
+        at = slice(i * nz, (i + 1) * nz)
+        own = cells(base + i)
+        line = pl.ds(base + i, 1)
+        if i < chunk - 1:
+            nxt = cells(base + i + 1)
+            fluid_next = fluid_of(obs[nxt, :])
+            flux = fluid_next * east[nxt, :]
+        else:
+            fluid_next, flux = after_fluid, after_flux
+        p_next = press[cells(base + i + 2), :]
         east_next_done = fluid * (flux - fluid_next * (p_next - p))
-        north_done = fluid * north_roll(fluid, 1) * (north[at, :] - (p - north_roll(p, 1)))
-        line = pl.ds(base + i, 1)
-        chunk_line = pl.ds(i, 1)
-        fluid_below = below_of(fluid, f_below[chunk_line, :] + lift)
-        up_done = fluid * fluid_below * (up[at, :] - (p - below_of(p, p_below[line, :])))
+        north_done = fluid * north_roll(fluid, 1) * (north[own, :] - (p - north_roll(p, 1)))
+        fluid_below = below_of(fluid, f_below[line, :] + lift)
+        up_done = fluid * fluid_below * (up[own, :] - (p - below_of(p, p_below[line, :])))
         edge = fluid[nz - 1 : nz, :] * (
-            g_above[chunk_line, :] - f_above[chunk_line, :] * (p_above[line, :] - p[nz - 1 : nz, :])
+            low_above[1, line, :] - low_above[0, line, :] * (p_above[line, :] - p[nz - 1 : nz, :])
         )
         out_east[at, :] = east_done
         out_north[at, :] = north_done
@@ -472,12 +520,7 @@
             + (north_done - north_roll(north_done, -1))
             + (up_done - above_of(up_done, edge))
         )
-        return fluid_next, p_next, east_next_done
-
-    start = fluid_of(obs[0:nz, :])
-    p_first = press[rows_of(0), :]
-    done = start * fluid_prev * (east[0:nz, :] - (p_first - press[rows_of(-1), :]))
-    lax.fori_loop(0, chunk, row, (start, p_first, done), unroll=2)
+        fluid, p, east_done = fluid_next, p_next, east_next_done
 
 
 def local(groups, slabs, east_velocity, north_velocity, upward_velocity, obstacle):
@@ -493,8 +536,8 @@
     te_h, te_l = pair_np(even_np)
     to_h, to_l = pair_np(odd_np)
     ti_h, ti_l = pair_np(odd_np.T.copy())
-    c_h, c_l = pair_np(block_np)
-    ct_h, ct_l = pair_np(block_np.T.copy())
+    c_hl, c_h = stack_left(block_np)
+    ct_hl, ct_h = stack_left(block_np.T.copy())
     sine_h, sine_l = pair_np(sine_np)
     sum_h, sum_l = (np.repeat(t, 8, axis=1) for t in (sine_h, sine_l))
     lam_a = np.repeat(lam_a_np[:, None], 128, 1).astype(np.float32)
@@ -513,20 +556,21 @@
     params = pltpu.CompilerParams(vmem_limit_bytes=VMEM_LIMIT, dimension_semantics=("arbitrary",))
     single = pltpu.CompilerParams(vmem_limit_bytes=VMEM_LIMIT)
     big = pl.BlockSpec((chunk * nz, ny), lambda i: (i, 0))
-    line = pl.BlockSpec((chunk, ny), lambda i: (i, 0))
     before = pl.BlockSpec((nz, ny), lambda i: (jnp.maximum(i * chunk - 1, 0), 0))
     after = pl.BlockSpec((nz, ny), lambda i: (jnp.minimum(i * chunk + chunk, nx - 1), 0))
-
-    def whole(a):
-        return pl.BlockSpec(a.shape, lambda *_: (0,) * len(a.shape))
-
-    plane = jax.ShapeDtypeStruct((nx, ny), F32)
-    f_top, f_bot, g_bot = pl.pallas_call(
-        functools.partial(first_rows, nz),
+    kept = pl.BlockSpec(memory_space=pltpu.VMEM)
+    modes_shape = jax.ShapeDtypeStruct((nz, nx, ny), F32)
+    cells = nx * nz * ny
+
+    high, low = pl.pallas_call(
+        functools.partial(planes_kernel, nz),
         grid=(ny // 128,),
         in_specs=[pl.BlockSpec((nx * nz, 128), lambda i: (0, i))] * 2,
-        out_specs=[pl.BlockSpec((nx, 128), lambda i: (0, i))] * 3,
-        out_shape=[plane] * 3,
+        out_specs=[
+            pl.BlockSpec((nx, 128), lambda i: (0, i)),
+            pl.BlockSpec((2, nx, 128), lambda i: (0, 0, i)),
+        ],
+        out_shape=[jax.ShapeDtypeStruct((nx, ny), F32), jax.ShapeDtypeStruct((2, nx, ny), F32)],
         compiler_params=params,
         name="planes",
     )(obs, up)
@@ -535,37 +579,45 @@
     falling = [(i + 1, i) for i in range(slabs - 1)]
     to_east = [(i, (i + 1) % groups) for i in range(groups)]
     to_west = [((i + 1) % groups, i) for i in range(groups)]
-    f_below = lax.ppermute(f_top, "gz", rising)
-    g_above = lax.ppermute(g_bot, "gz", falling)
     f_first = (1 - obs[:nz]).astype(F32)
-    f_west = lax.ppermute((1 - obs[(nx - 1) * nz :]).astype(F32), "xy", to_east)
-    side = lax.ppermute(jnp.concatenate([f_first, f_first * east[:nz]], 0), "xy", to_west)
-    f_east, g_east = side[:nz], side[nz:]
-    f_above = lax.ppermute(f_bot, "gz", falling)
-
-    tables = (te_h, te_l, to_h, to_l, c_h, c_l, lam_a, lam_b, c0)
-    ends_shape = jax.ShapeDtypeStruct((slabs, nx + nz, 2 * width), F32)
-    modes, ends = pl.pallas_call(
-        functools.partial(forward_kernel, nz, slabs),
+    f_final = (1 - obs[(nx - 1) * nz :]).astype(F32)
+    first = jnp.concatenate([f_first, f_first * east[:nz], f_final], 0)
+    side_west = lax.ppermute(first[2 * nz :], "xy", to_east)
+    side_east = lax.ppermute(first[: 2 * nz], "xy", to_west)
+    f_below = lax.ppermute(high, "gz", rising)
+    low_above = lax.ppermute(low, "gz", falling)
+
+    tables = (te_h, te_l, to_h, to_l, c_hl, c_h)
+    modes = pl.pallas_call(
+        functools.partial(interior_kernel, nz),
         grid=(steps,),
-        in_specs=[big, before, after, big, after, big, big]
-        + [whole(f_west)] * 3 + [line, line]
-        + [whole(t) for t in tables],
-        out_specs=[
-            pl.BlockSpec((nz, nx, ny), lambda i: (0, 0, 0)),
-            pl.BlockSpec(ends_shape.shape, lambda i: (0, 0, 0)),
-        ],
-        out_shape=[jax.ShapeDtypeStruct((nz, nx, ny), F32), ends_shape],
+        in_specs=[big, before, after, big, after, big, big] + [kept] * 6,
+        out_specs=kept,
+        out_shape=modes_shape,
         scratch_shapes=[
             pltpu.VMEM((chunk * nz, ny), F32),
             pltpu.VMEM((ny // 128, nx * nz, 128), F32),
+        ],
+        compiler_params=params,
+        cost_estimate=pl.CostEstimate(flops=cells * 2 * 3 * (ny // 2 + nx), bytes_accessed=20 * cells, transcendentals=0),
+        name="interior",
+    )(obs, obs, obs, east, east, north, up, *tables)
+    ends_shape = jax.ShapeDtypeStruct((slabs, nx + nz, 2 * width), F32)
+    modes, ends = pl.pallas_call(
+        functools.partial(joined_kernel, nz, slabs),
+        in_specs=[kept] * 17,
+        out_specs=[kept] * 2,
+        out_shape=[modes_shape, ends_shape],
+        scratch_shapes=[
             pltpu.VMEM((nx, ny), F32),
             pltpu.VMEM((nx, ny), F32),
             pltpu.VMEM((2, nz, 8, ny), F32),
+            pltpu.VMEM((2, nz, ny), F32),
         ],
-        compiler_params=params,
-        name="forward",
-    )(obs, obs, obs, east, east, north, up, f_west, f_east, g_east, f_below, g_above, *tables)
+        input_output_aliases={0: 0},
+        compiler_params=single,
+        name="joined",
+    )(modes, high, low, f_below, low_above, first, side_west, side_east, *tables, lam_a, lam_b, c0)
 
     ends = lax.all_to_all(ends, "gz", split_axis=0, concat_axis=0, tiled=True)
     own = pl.pallas_call(
@@ -587,18 +639,12 @@
     )(ends, *found, lam_pair, part, mu, c0_pair, sine_h, sine_l)
     solved = lax.all_to_all(solved, "gz", split_axis=0, concat_axis=0, tiled=True)
 
-    tables = (te_h, te_l, ti_h, ti_l, ct_h, ct_l, lam_a, lam_b, c0)
+    tables = (te_h, te_l, ti_h, ti_l, ct_hl, ct_h, lam_a, lam_b, c0)
     field = jax.ShapeDtypeStruct((nx * nz, ny), F32)
     outs = pl.pallas_call(
-        functools.partial(backward_kernel, nz, slabs),
+        functools.partial(backward_kernel, nz, slabs, chunk),
         grid=(steps,),
-        in_specs=[
-            pl.BlockSpec((nz, nx, ny), lambda i: (0, 0, 0)),
-            pl.BlockSpec(ends_shape.shape, lambda i: (0, 0, 0)),
-        ]
-        + [big, before, after, big, after, big, big]
-        + [whole(f_west)] * 3 + [line, line, line]
-        + [whole(t) for t in tables],
+        in_specs=[kept] * (10 + len(tables)),
         out_specs=[big] * 5,
         out_shape=[field] * 5,
         scratch_shapes=[
@@ -612,8 +658,7 @@
         ],
         compiler_params=params,
         name="backward",
-    )(modes, solved, obs, obs, obs, east, east, north, up,
-      f_west, f_east, g_east, f_below, g_above, f_above, *tables)
+    )(modes, solved, obs, east, north, up, side_west, side_east, f_below, low_above, *tables)
     return tuple(o.reshape(nx, nz, ny) for o in outs)
 
 

time: 106 us -> 73.1 us (0.69)
  Pallas kernels: 48.8 us -> 21.2 us
  waiting for transfers between devices: 15.3 us -> 2 us
  blocking collectives: 15.5 us -> 27.7 us
  starting transfers between devices: 20.2 us -> 13.5 us
  local copies, waits for them, and re-layouts: 2.9 us -> 6.03 us
    pallas_call x3 -> x4, Pallas kernels: 43.4 us -> 19.3 us  [the longest x1 11.6 us: local(): pl.pallas_call(functools.partial(backward_kernel, nz, slabs, chunk), grid...]
    all_to_all x0 -> x1, blocking collectives: none -> 13.5 us  [local(): lax.all_to_all(solved, 'gz', split_axis=0, concat_axis=0, tiled=True)]
    ppermute x5 -> x4, waiting for transfers between devices: 13 us -> 0.01 us  [the longest x1 0.01 us: local(): side_west = lax.ppermute(first[2 * nz:], 'xy', to_east)]
    all_to_all x1 -> x0, starting transfers between devices: 5.09 us -> none  [local(): lax.all_to_all(solved, 'gz', split_axis=0, concat_axis=0, tiled=True)]
    unnamed x18 -> x58, local copies, waits for them, and re-layouts: 2.29 us -> 6.03 us
    pallas_call x1, Pallas kernels: 2.88 us -> 1.06 us  [local(): pl.pallas_call(functools.partial(correct_kernel, nz, groups), out_shape=e...]
    pallas_call x1, Pallas kernels: 2.56 us -> 0.81 us  [local(): pl.pallas_call(functools.partial(ends_kernel, nz), out_shape=jax.ShapeDty...]
    ppermute x5 -> x4, starting transfers between devices: 11.8 us -> 10.1 us  [the longest x1 4.09 us: local(): f_below = lax.ppermute(high, 'gz', rising)]
  transfers between devices with their start and end apart: 9 -> 7, of which waited for: 5 -> 2; matrix products, arithmetic and copies ran while one was open for 2% -> 0% of each run, Pallas kernels for 0% -> 8%
where the time goes in v3:
time: 73.1 us; the launch traced here: 72.1 us
  blocking collectives  27.7 us (38%)
  Pallas kernels  21.2 us (29%)
  starting transfers between devices  13.5 us (18%)
  local copies, waits for them, and re-layouts  6.03 us (8%)
  waiting for transfers between devices  2 us (3%)
  between operations  1.03 us (1%)
  other arithmetic  0.76 us (1%)
    all_to_all x1, blocking collectives, local(): ends = lax.all_to_all(ends, 'gz', split_axis=0, concat_axis=0, tiled=True)  14.2 us
    all_to_all x1, blocking collectives, local(): lax.all_to_all(solved, 'gz', split_axis=0, concat_axis=0, tiled=True)  13.5 us
    pallas_call x1, Pallas kernels, local(): pl.pallas_call(functools.partial(backward_kernel, nz, slabs, chunk), grid...  11.6 us
    unnamed x58, local copies, waits for them, and re-layouts  6.03 us
    pallas_call x1, Pallas kernels, local(): pl.pallas_call(functools.partial(interior_kernel, nz), grid=(steps,), in_...  4.64 us
    ppermute x1, starting transfers between devices, local(): f_below = lax.ppermute(high, 'gz', rising)  4.09 us
    ppermute x3, starting transfers between devices, local(): lax.ppermute(own, 'xy', [((i + shift) % groups, i) for i in range(groups)])  3.31 us
    pallas_call x1, Pallas kernels, local(): pl.pallas_call(functools.partial(joined_kernel, nz, slabs), in_specs=[kep...  2.12 us
  transfers between devices with their start and end apart: 7, of which 2 were waited for; matrix products, arithmetic and copies ran while one was open for 0% of the time, Pallas kernels for 8%

profile of v3, /device:TPU:1, one launch (start us, length us, event | category | flops | bytes accessed | tf_op | source)
XLA Modules:
  0.0 72.1 jit_solution(12969047738565903051)
XLA Ops:
  0.6 0.0 copy-start.17
  0.6 0.7 %convert_bitcast_fusion.1 = (f32[8,512]{1,0:T(8,128)S(1)}, f32[8,512]{1,0:T(8,128)S(1)}) fusion(s32[128,8,512]{2,1,0:T(8,128)} %param.28), kind=kLoop, calls=%fused_computation.4 | loop fusion | flops 16384 | bytes 65536 | tf_op jit(solution)/shard_map/convert_element_type | solution.py:582
  1.4 2.1 %collective-permute-start.2 = (f32[8,512]{1,0:T(8,128)S(1)}, f32[8,512]{1,0:T(8,128)S(1)}, u32[]{:S(2)}, u32[]{:S(2)}) collective-permute-start(f32[8,512]{1,0:T(8,128)S(1)} %get-tuple-element.24), channel_id=1, source_target_pairs={{0,1},{1,2},{2,3},{3,0},{4,5},{5,6},{6,7},{7,4},{8,9},{9,10},{10,1... | collective-permute-start | bytes 49160 | tf_op jit(solution)/shard_map/ppermute | solution.py:585
  3.5 1.6 %copy-done = s32[128,8,512]{2,1,0:T(8,128)S(1)} copy-done((s32[128,8,512]{2,1,0:T(8,128)S(1)}, s32[128,8,512]{2,1,0:T(8,128)}, u32[]{:S(2)}) %copy-start) | copy-done | bytes 2097176
  5.1 1.6 %copy-done.3 = f32[128,8,512]{2,1,0:T(8,128)S(1)} copy-done((f32[128,8,512]{2,1,0:T(8,128)S(1)}, f32[128,8,512]{2,1,0:T(8,128)}, u32[]{:S(2)}) %copy-start.3) | copy-done | bytes 2097176
  6.7 0.9 %planes.1 = (f32[128,512]{1,0:T(8,128)S(1)}, f32[2,128,512]{2,1,0:T(8,128)S(1)}) custom-call(s32[1024,512]{1,0:T(8,128)S(1)} %bitcast.17, f32[1024,512]{1,0:T(8,128)S(1)} %bitcast.25), custom_call_target="tpu_custom_call" | custom-call | tf_op jit(solution)/shard_map/planes/pallas_call | solution.py:565
  7.6 4.1 %collective-permute-start = (f32[128,512]{1,0:T(8,128)S(1)}, f32[128,512]{1,0:T(8,128)S(1)}, u32[]{:S(2)}, u32[]{:S(2)}) collective-permute-start(f32[128,512]{1,0:T(8,128)S(1)} %get-tuple-element.14.high), channel_id=1, source_target_pairs={{0,4},{4,8},{8,12},{12,16},{16,20},{20,24},{24,28},{1,5},{5,9},{9,... | collective-permute-start | bytes 786440 | tf_op jit(solution)/shard_map/ppermute | solution.py:587
  11.7 1.9 %collective-permute-start.1 = (f32[2,128,512]{2,1,0:T(8,128)S(1)}, f32[2,128,512]{2,1,0:T(8,128)S(1)}, u32[]{:S(2)}, u32[]{:S(2)}) collective-permute-start(f32[2,128,512]{2,1,0:T(8,128)S(1)} %get-tuple-element.15.low), channel_id=1, source_target_pairs={{4,0},{8,4},{12,8},{16,12},{20,16},{24,20},{28,24},{5,1},{9,5},{13... | collective-permute-start | bytes 1572872 | tf_op jit(solution)/shard_map/ppermute | solution.py:588
  13.6 0.0 copy-done.2
  13.7 2.0 %collective-permute-start.3 = (f32[16,512]{1,0:T(8,128)S(1)}, f32[16,512]{1,0:T(8,128)S(1)}, u32[]{:S(2)}, u32[]{:S(2)}) collective-permute-start(f32[16,512]{1,0:T(8,128)S(1)} %pad_maximum_fusion.1), channel_id=1, source_target_pairs={{1,0},{2,1},{3,2},{0,3},{5,4},{6,5},{7,6},{4,7},{9,8},{10,9},{11,1... | collective-permute-start | bytes 98312 | tf_op jit(solution)/shard_map/ppermute | solution.py:586
  15.7 0.0 copy-done.17
  15.7 0.0 copy-start.7
  15.7 0.9 %copy-done.7 = bf16[256,256]{1,0:T(8,128)(2,1)S(1)} copy-done((bf16[256,256]{1,0:T(8,128)(2,1)S(1)}, bf16[256,256]{1,0:T(8,128)(2,1)}, u32[]{:S(2)}) %copy-start.7) | copy-done | bytes 131096
  16.6 0.9 %copy-done.9 = bf16[256,256]{1,0:T(8,128)(2,1)S(1)} copy-done((bf16[256,256]{1,0:T(8,128)(2,1)S(1)}, bf16[256,256]{1,0:T(8,128)(2,1)}, u32[]{:S(2)}) %copy-start.9) | copy-done | bytes 131096
  17.5 0.9 %copy-done.10 = bf16[256,256]{1,0:T(8,128)(2,1)S(1)} copy-done((bf16[256,256]{1,0:T(8,128)(2,1)S(1)}, bf16[256,256]{1,0:T(8,128)(2,1)}, u32[]{:S(2)}) %copy-start.10) | copy-done | bytes 131096
  18.5 0.0 copy-start.22
  18.5 4.6 %interior.1.modes_in = f32[8,128,512]{2,1,0:T(8,128)S(1)} custom-call(s32[1024,512]{1,0:T(8,128)S(1)} %bitcast.18, s32[1024,512]{1,0:T(8,128)S(1)} %bitcast.19, s32[1024,512]{1,0:T(8,128)S(1)} %bitcast.20, f32[1024,512]{1,0:T(8,128)S(1)} %bitcast.22, f32[1024,512]{1,0:T(8,128)S(1)} %bitcast.23, f32[1024,512]{1,0:T(8,128)S(1)} %bitcast.28, ...), custom_call_target="tpu_custom_call" | custom-call | flops 1207959552 | bytes 10485760 | tf_op jit(solution)/shard_map/interior/pallas_call | solution.py:591
  23.1 0.0 copy-start.18
  23.1 0.0 copy-start.19
  23.1 0.0 copy-start.20
  23.2 0.0 copy-start.23
  23.2 0.0 copy-start.24
  23.2 0.0 copy-start.25
  23.2 0.0 copy-start.26
  23.2 0.0 copy-start.28
  23.2 0.0 collective-permute-done.2.side_west
  23.2 0.0 collective-permute-done.3.side_east
  23.2 0.0 collective-permute-done.f_below
  23.2 0.0 collective-permute-done.1.low_above
  23.3 0.0 copy-start.21
  23.3 2.1 %joined.1 = (f32[8,128,512]{2,1,0:T(8,128)S(1)}, f32[8,136,128]{2,1,0:T(8,128)S(1)}) custom-call(f32[8,128,512]{2,1,0:T(8,128)S(1)} %interior.1.modes_in, f32[128,512]{1,0:T(8,128)S(1)} %get-tuple-element.14.high, f32[2,128,512]{2,1,0:T(8,128)S(1)} %get-tuple-element.15.low, ...), custom_call_target="tpu_custom_call", output_to_operand_aliasing={{0}: (0, {})} | custom-call | tf_op jit(solution)/shard_map/joined/pallas_call | solution.py:606
  25.4 0.0 copy-start.1
  25.5 0.0 copy-start.4
  25.5 0.0 copy-start.15
  25.5 0.0 copy-start.16
  25.5 0.0 copy-start.27
  25.5 14.2 %all_to_all.10.ends = f32[8,136,128]{2,1,0:T(8,128)S(1)} all-to-all(f32[8,136,128]{2,1,0:T(8,128)S(1)} %get-tuple-element.17), channel_id=1, replica_groups=mesh['gz'=8,'xy'=4] {'gz'}, dimensions={0} | all-to-all | bytes 1114112 | tf_op jit(solution)/shard_map/all_to_all | solution.py:622
  39.7 0.0 copy-done.19
  39.7 0.8 %ends.1.rest_0_ = f32[64,128]{1,0:T(8,128)S(1)} custom-call(f32[8,136,128]{2,1,0:T(8,128)S(1)} %all_to_all.10.ends, f32[64,128]{1,0:T(8,128)S(1)} %copy-done.20, f32[8,8,128]{2,1,0:T(8,128)S(1)} %copy-done.19, f32[64,128]{1,0:T(8,128)S(1)} %copy-done.18, bf16[64,512]{1,0:T(8,128)(2,1)S(1)} %copy-done.26, bf16[64,512]{1,0:T(8,128)(2,1)S(1)} %copy-done.25, ...), custom_call_target="tpu_custom_call" | custom-call | tf_op jit(solution)/shard_map/ends/pallas_call | solution.py:623
  40.6 0.1 collective-permute-start.6
  40.6 1.8 %collective-permute-start.5 = (f32[64,128]{1,0:T(8,128)S(1)}, f32[64,128]{1,0:T(8,128)S(1)}, u32[]{:S(2)}, u32[]{:S(2)}) collective-permute-start(f32[64,128]{1,0:T(8,128)S(1)} %ends.1.rest_0_), channel_id=1, source_target_pairs={{2,0},{3,1},{0,2},{1,3},{6,4},{7,5},{4,6},{5,7},{10,8},{11,9},{8,1... | collective-permute-start | bytes 98312 | tf_op jit(solution)/shard_map/ppermute | solution.py:632
  42.4 1.5 %collective-permute-start.4 = (f32[64,128]{1,0:T(8,128)S(1)}, f32[64,128]{1,0:T(8,128)S(1)}, u32[]{:S(2)}, u32[]{:S(2)}) collective-permute-start(f32[64,128]{1,0:T(8,128)S(1)} %ends.1.rest_0_), channel_id=1, source_target_pairs={{1,0},{2,1},{3,2},{0,3},{5,4},{6,5},{7,6},{4,7},{9,8},{10,9},{11,1... | collective-permute-start | bytes 98312 | tf_op jit(solution)/shard_map/ppermute | solution.py:632
  43.9 1.3 %collective-permute-done.6.rest_3_ = f32[64,128]{1,0:T(8,128)S(1)} collective-permute-done((f32[64,128]{1,0:T(8,128)S(1)}, f32[64,128]{1,0:T(8,128)S(1)}, u32[]{:S(2)}, u32[]{:S(2)}) %collective-permute-start.6) | collective-permute-done | bytes 32800 | tf_op jit(solution)/shard_map/ppermute | solution.py:632
  45.2 0.0 collective-permute-done.5.rest_2_
  45.2 0.7 collective-permute-done.4.rest_1_
  45.9 1.1 %correct.1 = f32[8,136,128]{2,1,0:T(8,128)S(1)} custom-call(f32[8,136,128]{2,1,0:T(8,128)S(1)} %all_to_all.10.ends, f32[64,128]{1,0:T(8,128)S(1)} %ends.1.rest_0_, f32[64,128]{1,0:T(8,128)S(1)} %collective-permute-done.4.rest_1_, f32[64,128]{1,0:T(8,128)S(1)} %collective-permute-done.5.rest_2_, f32[64,128]{1,0:T(8,128)S(1)} %collective-permute-done.6.rest_3_, ...), custom_call_target="tpu_custom_call" | custom-call | tf_op jit(solution)/shard_map/correct/pallas_call | solution.py:633
  46.9 13.5 %all_to_all.11.solved = f32[8,136,128]{2,1,0:T(8,128)S(1)} all-to-all(f32[8,136,128]{2,1,0:T(8,128)S(1)} %correct.1), channel_id=1, replica_groups=mesh['gz'=8,'xy'=4] {'gz'}, dimensions={0} | all-to-all | bytes 1114112 | tf_op jit(solution)/shard_map/all_to_all | solution.py:640
  60.5 11.6 %backward.1 = (f32[1024,512]{1,0:T(8,128)}, f32[1024,512]{1,0:T(8,128)}, f32[1024,512]{1,0:T(8,128)}, f32[1024,512]{1,0:T(8,128)}, f32[1024,512]{1,0:T(8,128)}) custom-call(f32[8,128,512]{2,1,0:T(8,128)S(1)} %get-tuple-element.16.modes, f32[8,136,128]{2,1,0:T(8,128)S(1)} %all_to_all.11.solved, s32[1024,512]{1,0:T(8,128)S(1)} %bitcast.21, ...), custom_call_target="tpu_custom_call" | custom-call | tf_op jit(solution)/shard_map/backward/pallas_call | solution.py:644
  (36 shorter events, 0.1 us)
Async XLA Ops:
  0.6 15.1 %copy-start.17 = (bf16[128,128]{1,0:T(8,128)(2,1)S(1)}, bf16[128,128]{1,0:T(8,128)(2,1)}, u32[]{:S(2)}) copy-start(bf16[128,128]{1,0:T(8,128)(2,1)} %constant.49.clone.c_h) | copy-start | bytes 98308
  1.4 21.8 %collective-permute-start.2 = (f32[8,512]{1,0:T(8,128)S(1)}, f32[8,512]{1,0:T(8,128)S(1)}, u32[]{:S(2)}, u32[]{:S(2)}) collective-permute-start(f32[8,512]{1,0:T(8,128)S(1)} %get-tuple-element.24), channel_id=1, source_target_pairs={{0,1},{1,2},{2,3},{3,0},{4,5},{5,6},{6,7},{7,4},{8,9},{9,10},{10,1... | collective-permute-start | bytes 49160 | tf_op jit(solution)/shard_map/ppermute | solution.py:585
  3.5 1.6 %copy-start = (s32[128,8,512]{2,1,0:T(8,128)S(1)}, s32[128,8,512]{2,1,0:T(8,128)}, u32[]{:S(2)}) copy-start(s32[128,8,512]{2,1,0:T(8,128)} %param.28) | copy-start | bytes 6291460
  5.1 1.6 %copy-start.3 = (f32[128,8,512]{2,1,0:T(8,128)S(1)}, f32[128,8,512]{2,1,0:T(8,128)}, u32[]{:S(2)}) copy-start(f32[128,8,512]{2,1,0:T(8,128)} %param.27) | copy-start | bytes 6291460
  6.7 6.9 %copy-start.2 = (f32[128,8,512]{2,1,0:T(8,128)S(1)}, f32[128,8,512]{2,1,0:T(8,128)}, u32[]{:S(2)}) copy-start(f32[128,8,512]{2,1,0:T(8,128)} %param.25) | copy-start | bytes 6291460
  6.7 9.0 %copy-start.5 = (f32[128,8,512]{2,1,0:T(8,128)S(1)}, f32[128,8,512]{2,1,0:T(8,128)}, u32[]{:S(2)}) copy-start(f32[128,8,512]{2,1,0:T(8,128)} %param.26) | copy-start | bytes 6291460
  6.7 9.0 %copy-start.6 = (bf16[256,256]{1,0:T(8,128)(2,1)S(1)}, bf16[256,256]{1,0:T(8,128)(2,1)}, u32[]{:S(2)}) copy-start(bf16[256,256]{1,0:T(8,128)(2,1)} %constant.45.clone.te_l) | copy-start | bytes 393220
  6.7 9.0 %copy-start.14 = (bf16[128,256]{1,0:T(8,128)(2,1)S(1)}, bf16[128,256]{1,0:T(8,128)(2,1)}, u32[]{:S(2)}) copy-start(bf16[128,256]{1,0:T(8,128)(2,1)} %constant.48.clone.c_hl) | copy-start | bytes 196612
  7.6 15.6 %collective-permute-start = (f32[128,512]{1,0:T(8,128)S(1)}, f32[128,512]{1,0:T(8,128)S(1)}, u32[]{:S(2)}, u32[]{:S(2)}) collective-permute-start(f32[128,512]{1,0:T(8,128)S(1)} %get-tuple-element.14.high), channel_id=1, source_target_pairs={{0,4},{4,8},{8,12},{12,16},{16,20},{20,24},{24,28},{1,5},{5,9},{9,... | collective-permute-start | bytes 786440 | tf_op jit(solution)/shard_map/ppermute | solution.py:587
  11.7 11.5 %collective-permute-start.1 = (f32[2,128,512]{2,1,0:T(8,128)S(1)}, f32[2,128,512]{2,1,0:T(8,128)S(1)}, u32[]{:S(2)}, u32[]{:S(2)}) collective-permute-start(f32[2,128,512]{2,1,0:T(8,128)S(1)} %get-tuple-element.15.low), channel_id=1, source_target_pairs={{4,0},{8,4},{12,8},{16,12},{20,16},{24,20},{28,24},{5,1},{9,5},{13... | collective-permute-start | bytes 1572872 | tf_op jit(solution)/shard_map/ppermute | solution.py:588
  13.7 9.6 %collective-permute-start.3 = (f32[16,512]{1,0:T(8,128)S(1)}, f32[16,512]{1,0:T(8,128)S(1)}, u32[]{:S(2)}, u32[]{:S(2)}) collective-permute-start(f32[16,512]{1,0:T(8,128)S(1)} %pad_maximum_fusion.1), channel_id=1, source_target_pairs={{1,0},{2,1},{3,2},{0,3},{5,4},{6,5},{7,6},{4,7},{9,8},{10,9},{11,1... | collective-permute-start | bytes 98312 | tf_op jit(solution)/shard_map/ppermute | solution.py:586
  15.7 0.9 %copy-start.7 = (bf16[256,256]{1,0:T(8,128)(2,1)S(1)}, bf16[256,256]{1,0:T(8,128)(2,1)}, u32[]{:S(2)}) copy-start(bf16[256,256]{1,0:T(8,128)(2,1)} %constant.44.clone.te_h) | copy-start | bytes 393220
  16.6 0.9 %copy-start.9 = (bf16[256,256]{1,0:T(8,128)(2,1)S(1)}, bf16[256,256]{1,0:T(8,128)(2,1)}, u32[]{:S(2)}) copy-start(bf16[256,256]{1,0:T(8,128)(2,1)} %constant.47.clone.to_l) | copy-start | bytes 393220
  17.5 0.9 %copy-start.10 = (bf16[256,256]{1,0:T(8,128)(2,1)S(1)}, bf16[256,256]{1,0:T(8,128)(2,1)}, u32[]{:S(2)}) copy-start(bf16[256,256]{1,0:T(8,128)(2,1)} %constant.46.clone.to_h) | copy-start | bytes 393220
  18.4 4.8 %copy-start.8 = (bf16[256,256]{1,0:T(8,128)(2,1)S(1)}, bf16[256,256]{1,0:T(8,128)(2,1)}, u32[]{:S(2)}) copy-start(bf16[256,256]{1,0:T(8,128)(2,1)} %constant.44.clone.te_h) | copy-start | bytes 393220
  18.4 4.8 %copy-start.11 = (bf16[256,256]{1,0:T(8,128)(2,1)S(1)}, bf16[256,256]{1,0:T(8,128)(2,1)}, u32[]{:S(2)}) copy-start(bf16[256,256]{1,0:T(8,128)(2,1)} %constant.46.clone.to_h) | copy-start | bytes 393220
  18.4 4.8 %copy-start.12 = (f32[128,128]{1,0:T(8,128)S(1)}, f32[128,128]{1,0:T(8,128)}, u32[]{:S(2)}) copy-start(f32[128,128]{1,0:T(8,128)} %constant.52.clone.c0) | copy-start | bytes 196612
  18.4 4.8 %copy-start.13 = (f32[128,128]{1,0:T(8,128)S(1)}, f32[128,128]{1,0:T(8,128)}, u32[]{:S(2)}) copy-start(f32[128,128]{1,0:T(8,128)} %constant.50.clone.lam_a) | copy-start | bytes 196612
  18.5 4.8 %copy-start.22 = (f32[8,512]{1,0:T(8,128)S(1)}, f32[8,512]{1,0:T(8,128)}, u32[]{:S(2)}) copy-start(f32[8,512]{1,0:T(8,128)} %constant.51.clone.lam_b) | copy-start | bytes 49156
  23.1 16.6 %copy-start.18 = (f32[64,128]{1,0:T(8,128)S(1)}, f32[64,128]{1,0:T(8,128)}, u32[]{:S(2)}) copy-start(f32[64,128]{1,0:T(8,128)} %constant.55.clone.c0.rest_7_) | copy-start | bytes 98308
  23.1 16.6 %copy-start.19 = (f32[8,8,128]{2,1,0:T(8,128)S(1)}, f32[8,8,128]{2,1,0:T(8,128)}, u32[]{:S(2)}) copy-start(f32[8,8,128]{2,1,0:T(8,128)} %constant.54.clone.lam_b.rest_5_) | copy-start | bytes 98308
  23.1 16.6 %copy-start.20 = (f32[64,128]{1,0:T(8,128)S(1)}, f32[64,128]{1,0:T(8,128)}, u32[]{:S(2)}) copy-start(f32[64,128]{1,0:T(8,128)} %constant.53.clone.lam_a.rest_4_) | copy-start | bytes 98308
  23.2 16.6 %copy-start.23 = (bf16[64,64]{1,0:T(8,128)(2,1)S(1)}, bf16[64,64]{1,0:T(8,128)(2,1)}, u32[]{:S(2)}) copy-start(bf16[64,64]{1,0:T(8,128)(2,1)} %constant.59.clone.sine_l.rest_9_) | copy-start | bytes 24580
  23.2 16.6 %copy-start.24 = (bf16[64,64]{1,0:T(8,128)(2,1)S(1)}, bf16[64,64]{1,0:T(8,128)(2,1)}, u32[]{:S(2)}) copy-start(bf16[64,64]{1,0:T(8,128)(2,1)} %constant.58.clone.sine_h.rest_8_) | copy-start | bytes 24580
  23.2 16.6 %copy-start.25 = (bf16[64,512]{1,0:T(8,128)(2,1)S(1)}, bf16[64,512]{1,0:T(8,128)(2,1)}, u32[]{:S(2)}) copy-start(bf16[64,512]{1,0:T(8,128)(2,1)} %constant.57.clone.sum_l) | copy-start | bytes 196612
  23.2 16.5 %copy-start.26 = (bf16[64,512]{1,0:T(8,128)(2,1)S(1)}, bf16[64,512]{1,0:T(8,128)(2,1)}, u32[]{:S(2)}) copy-start(bf16[64,512]{1,0:T(8,128)(2,1)} %constant.56.clone.sum_h) | copy-start | bytes 196612
  23.2 22.7 %copy-start.28 = (f32[64,128]{1,0:T(8,128)S(1)}, f32[64,128]{1,0:T(8,128)}, u32[]{:S(2)}) copy-start(f32[64,128]{1,0:T(8,128)} %constant.60.clone.rest_6_) | copy-start | bytes 98308
  23.3 37.1 %copy-start.21 = (bf16[128,256]{1,0:T(8,128)(2,1)S(1)}, bf16[128,256]{1,0:T(8,128)(2,1)}, u32[]{:S(2)}) copy-start(bf16[128,256]{1,0:T(8,128)(2,1)} %constant.63.clone.ct_hl) | copy-start | bytes 196612
  25.4 35.0 %copy-start.1 = (s32[128,8,512]{2,1,0:T(8,128)S(1)}, s32[128,8,512]{2,1,0:T(8,128)}, u32[]{:S(2)}) copy-start(s32[128,8,512]{2,1,0:T(8,128)} %param.28) | copy-start | bytes 6291460
  25.5 35.0 %copy-start.4 = (f32[128,8,512]{2,1,0:T(8,128)S(1)}, f32[128,8,512]{2,1,0:T(8,128)}, u32[]{:S(2)}) copy-start(f32[128,8,512]{2,1,0:T(8,128)} %param.27) | copy-start | bytes 6291460
  25.5 35.0 %copy-start.15 = (bf16[256,256]{1,0:T(8,128)(2,1)S(1)}, bf16[256,256]{1,0:T(8,128)(2,1)}, u32[]{:S(2)}) copy-start(bf16[256,256]{1,0:T(8,128)(2,1)} %constant.62.clone.ti_l) | copy-start | bytes 393220
  25.5 35.0 %copy-start.16 = (bf16[256,256]{1,0:T(8,128)(2,1)S(1)}, bf16[256,256]{1,0:T(8,128)(2,1)}, u32[]{:S(2)}) copy-start(bf16[256,256]{1,0:T(8,128)(2,1)} %constant.61.clone.ti_h) | copy-start | bytes 393220
  25.5 35.0 %copy-start.27 = (bf16[128,128]{1,0:T(8,128)(2,1)S(1)}, bf16[128,128]{1,0:T(8,128)(2,1)}, u32[]{:S(2)}) copy-start(bf16[128,128]{1,0:T(8,128)(2,1)} %constant.64.clone.ct_h) | copy-start | bytes 98308
  40.6 4.6 %collective-permute-start.6 = (f32[64,128]{1,0:T(8,128)S(1)}, f32[64,128]{1,0:T(8,128)S(1)}, u32[]{:S(2)}, u32[]{:S(2)}) collective-permute-start(f32[64,128]{1,0:T(8,128)S(1)} %ends.1.rest_0_), channel_id=1, source_target_pairs={{3,0},{0,1},{1,2},{2,3},{7,4},{4,5},{5,6},{6,7},{11,8},{8,9},{9,10... | collective-permute-start | bytes 98312 | tf_op jit(solution)/shard_map/ppermute | solution.py:632
  40.6 4.6 %collective-permute-start.5 = (f32[64,128]{1,0:T(8,128)S(1)}, f32[64,128]{1,0:T(8,128)S(1)}, u32[]{:S(2)}, u32[]{:S(2)}) collective-permute-start(f32[64,128]{1,0:T(8,128)S(1)} %ends.1.rest_0_), channel_id=1, source_target_pairs={{2,0},{3,1},{0,2},{1,3},{6,4},{7,5},{4,6},{5,7},{10,8},{11,9},{8,1... | collective-permute-start | bytes 98312 | tf_op jit(solution)/shard_map/ppermute | solution.py:632
  42.4 3.4 %collective-permute-start.4 = (f32[64,128]{1,0:T(8,128)S(1)}, f32[64,128]{1,0:T(8,128)S(1)}, u32[]{:S(2)}, u32[]{:S(2)}) collective-permute-start(f32[64,128]{1,0:T(8,128)S(1)} %ends.1.rest_0_), channel_id=1, source_target_pairs={{1,0},{2,1},{3,2},{0,3},{5,4},{6,5},{7,6},{4,7},{9,8},{10,9},{11,1... | collective-permute-start | bytes 98312 | tf_op jit(solution)/shard_map/ppermute | solution.py:632

commit v4 on v3

v4 whole, which is shorter than its diff:
```python
import functools

import jax
import jax.numpy as jnp
import ml_dtypes
import numpy as np
from jax import lax
from jax.experimental import pallas as pl
from jax.experimental.pallas import tpu as pltpu
from jax.sharding import PartitionSpec as P

F32 = jnp.float32
BF16 = jnp.bfloat16
VMEM_LIMIT = 24 * 1024 * 1024
LOAD_LIMIT = 48 * 1024 * 1024


def pair_np(table):
    high = table.astype(np.float32).astype(ml_dtypes.bfloat16)
    low = (table - high.astype(np.float64)).astype(np.float32).astype(ml_dtypes.bfloat16)
    return high, low


def north_tables(length):
    half = length // 2
    cell = np.arange(half)[:, None]
    mode = np.arange(half)[None, :]

    def cas(number):
        angle = 2.0 * np.pi * ((cell * number) % length) / length
        return (np.cos(angle) + np.sin(angle)) / np.sqrt(length)

    numbers = np.concatenate([2 * np.arange(half), 2 * np.arange(half) + 1])
    eigen = 4.0 * np.sin(np.pi * numbers / length) ** 2
    return cas(2 * mode), cas(2 * mode + 1), eigen


def east_tables(length):
    modes = np.concatenate([np.arange(0, length, 2), np.arange(1, length, 2)])
    cell = np.arange(length)
    table = np.cos(np.pi * modes[:, None] * (2 * cell[None, :] + 1) / (2 * length)) * np.sqrt(2.0 / length)
    table[0] = np.sqrt(1.0 / length)
    eigen = 4.0 * np.sin(np.pi * modes / (2 * length)) ** 2
    return table, eigen


def sine_table(length):
    index = np.arange(1, length + 1)
    table = np.sqrt(2.0 / (length + 1)) * np.sin(np.pi * np.outer(index, index) / (length + 1))
    eigen = 4.0 * np.sin(np.pi * index / (2 * (length + 1))) ** 2
    return table, eigen


def split(value):
    high = value.astype(BF16)
    return high, (value - high.astype(F32)).astype(BF16)


def dot3(left, right):
    (lh, ll), (rh, rl) = left, right
    dot = functools.partial(jnp.dot, preferred_element_type=F32)
    return dot(lh, rh) + (dot(ll, rh) + dot(lh, rl))


def chebyshev(shift, count):
    values = [jnp.ones_like(shift)]
    step = values[0]
    for n in range(count):
        step = step + shift * values[n]
        values.append(values[n] + step)
    return values


def slab_solve(shift, right):
    count = len(right)
    u = chebyshev(shift, count)
    inverse = 1.0 / u[count]
    lower = [right[0]]
    for k in range(1, count):
        lower.append(lower[-1] + u[k] * right[k])
    upper = [None] * count
    for k in range(count - 2, -1, -1):
        term = u[count - 2 - k] * right[k + 1] if k < count - 2 else right[k + 1]
        upper[k] = term if upper[k + 1] is None else upper[k + 1] + term
    out = []
    for k in range(count):
        value = u[count - 1 - k] * lower[k]
        if upper[k] is not None:
            value = value + u[k] * upper[k]
        out.append(value * inverse)
    return out


def spike_of(shift, count):
    u = chebyshev(shift, count)
    inverse = 1.0 / u[count]
    return [u[count - 1 - k] * inverse for k in range(count)]


def interface_chain(couple, spread, bottoms, tops):
    count = len(bottoms)
    slope = jnp.zeros_like(couple)
    offset = jnp.zeros_like(couple)
    slopes, offsets, inverses, bases = [], [], [], []
    for s in range(count):
        inverse = 1.0 / (1.0 - couple * slope)
        base = (bottoms[s] + couple * offset) * inverse
        slopes.append(slope)
        offsets.append(offset)
        inverses.append(inverse * spread)
        bases.append(base)
        if s < count - 1:
            weight = spread * slope
            slope, offset = (
                couple + weight * spread * inverse,
                tops[s] + spread * offset + weight * base,
            )
    above = jnp.zeros_like(couple)
    lowers, uppers = [None] * count, [None] * count
    for s in range(count - 1, -1, -1):
        lower = bases[s] + inverses[s] * above
        uppers[s] = tops[s] + spread * (slopes[s] * lower + offsets[s]) + couple * above
        lowers[s] = lower
        above = lower
    below = [jnp.zeros_like(couple)] + uppers[:-1]
    above = lowers[1:] + [jnp.zeros_like(couple)]
    return below, above


def get_lanes(ref, rows):
    return jnp.concatenate([ref[n, rows, :] for n in range(ref.shape[0])], 1)


def put_lanes(ref, rows, value, start):
    for n in range(value.shape[1] // 128):
        ref[start + n, rows, :] = value[:, n * 128 : (n + 1) * 128]


def load_kernel(nz, obs, up_in, east, fluid, up, high, low, side, final, raw, line, sems):
    parts = raw.shape[0]
    rows = high.shape[0]
    copies = []
    for n in range(parts):
        lanes = slice(n * 128, (n + 1) * 128)
        copies.append(
            (
                pltpu.make_async_copy(obs.at[:, lanes], raw.at[n], sems.at[n]),
                pltpu.make_async_copy(up_in.at[:, lanes], up.at[n], sems.at[parts + n]),
            )
        )
        for copy in copies[-1]:
            copy.start()
    edge = pltpu.make_async_copy(east.at[0:nz, :], line, sems.at[2 * parts])
    edge.start()
    edge.wait()
    for n, (flags, speed) in enumerate(copies):
        lanes = slice(n * 128, (n + 1) * 128)
        flags.wait()
        fluid[n] = fluid_of(raw[n])
        high[:, lanes] = fluid[n, pl.ds(nz - 1, rows, stride=nz), :]
        bottom = fluid[n, pl.ds(0, rows, stride=nz), :]
        low[0, :, lanes] = bottom
        first = fluid[n, 0:nz, :]
        side[0:nz, lanes] = first
        side[nz : 2 * nz, lanes] = first * line[:, lanes]
        final[:, lanes] = fluid[n, (rows - 1) * nz : rows * nz, :]
        speed.wait()
        low[1, :, lanes] = bottom * up[n, pl.ds(0, rows, stride=nz), :]


def north_roll(value, shift):
    return pltpu.roll(value, shift % value.shape[1], 1)


def put_row(value, row, index):
    where = lax.broadcasted_iota(jnp.int32, value.shape, 0) == index
    return jnp.where(where, jnp.broadcast_to(row, value.shape), value)


def below_of(value, row):
    return put_row(pltpu.roll(value, 1, 0), row, 0)


def above_of(value, row):
    return put_row(pltpu.roll(value, value.shape[0] - 1, 0), row, value.shape[0] - 1)


def fluid_of(block):
    return (1 - block).astype(F32)


def east_left(table):
    return table, table[:, : table.shape[0]]


def north_pair(tables, index):
    size = tables.shape[1]
    return tables[2 * index * size : (2 * index + 1) * size, :], tables[(2 * index + 1) * size : (2 * index + 2) * size, :]


def east_dot(left, value):
    high, low = split(value)
    dot = functools.partial(jnp.dot, preferred_element_type=F32)
    return dot(left[0], jnp.concatenate([high, high], 0)) + dot(left[1], low)


def north_forward(value, even, odd):
    half = value.shape[1] // 2
    low, high = value[:, :half], value[:, half:]
    return dot3(split(low + high), even), dot3(split(low - high), odd)


def interior_kernel(nz, chunk, fluid, up, east, north, tables, east_table, modes, src, ready, half):
    ny = src.shape[1]
    nx = modes.shape[1]
    count = nx // chunk
    lift = jnp.where(lax.axis_index("gz") == 0, 1.0, 0.0).astype(F32)
    floor = jnp.broadcast_to(lift, (1, ny))
    none = jnp.zeros((1, ny), F32)

    def cells(x):
        return pl.ds(pl.multiple_of(x * nz, nz), nz)

    def stencil(step):
        base = step * chunk
        inside = jnp.where(step > 0, 1.0, 0.0).astype(F32)
        more = jnp.where(step < count - 1, 1.0, 0.0).astype(F32)
        here = get_lanes(fluid, cells(base))
        before = get_lanes(fluid, cells(jnp.maximum(base - 1, 0)))
        masked = here * (before * inside) * east[cells(base), :]
        for i in range(chunk):
            own = cells(base + i)
            nxt = cells(base + i + 1) if i < chunk - 1 else cells(jnp.minimum(base + chunk, nx - 1))
            after = get_lanes(fluid, nxt)
            flux = after * east[nxt, :]
            if i == chunk - 1:
                flux = flux * more
            masked_next = here * flux
            north_masked = here * north_roll(here, 1) * north[own, :]
            up_masked = here * below_of(here, floor) * get_lanes(up, own)
            src[i * nz : (i + 1) * nz, :] = (
                (masked - masked_next)
                + (north_masked - north_roll(north_masked, -1))
                + (up_masked - above_of(up_masked, none))
            )
            here, masked = after, masked_next

    def transform(step):
        rows = pl.ds(pl.multiple_of(step * chunk * nz, chunk * nz), chunk * nz)
        even, odd = north_forward(ready[...], north_pair(tables, 0), north_pair(tables, 1))
        put_lanes(half, rows, even, 0)
        put_lanes(half, rows, odd, ny // 256)

    stencil(0)
    ready[...] = src[...]

    def body(step, carry):
        transform(step - 1)
        stencil(step)
        ready[...] = src[...]
        return carry

    lax.fori_loop(1, count, body, 0)
    transform(count - 1)
    left = east_left(east_table[0])
    for k in range(nz):
        modes[k] = east_dot(left, get_lanes(half, pl.ds(k, nx, stride=nz)))


def joined_kernel(
    nz, slabs,
    modes_in, high, low_above, final, side_east,
    tables, east_table, east_values, lam_b,
    crown, out,
    bottom, top, acc,
):
    nx, ny = high.shape
    leaving = final[...] * side_east[nz:, :]
    stacked = jnp.concatenate([high[...] * low_above[1], leaving], 0)
    stacked = jnp.concatenate(north_forward(stacked, north_pair(tables, 0), north_pair(tables, 1)), 1)
    top[...] = east_dot(east_left(east_table[0]), stacked[:nx])
    leaving = stacked[nx:]
    acc[...] = jnp.zeros_like(acc)
    blocks = nx // 8

    def solve(n, carry):
        at = pl.ds(pl.multiple_of(n * 8, 8), 8)
        parity = n // (blocks // 2)
        for lane in range(0, ny, 128):
            lanes = slice(lane, lane + 128)
            shift = east_values[0, at, :] + lam_b[:, lanes]
            weight = east_values[1, at, :]
            rising = top[at, lanes]
            right = [modes_in[k, at, lanes] for k in range(nz)]
            right[nz - 1] = right[nz - 1] - rising
            crown[at, lanes] = right[nz - 1]
            local = slab_solve(shift, right)
            bottom[at, lanes] = local[0]
            top[at, lanes] = local[nz - 1] + rising
            for k in range(nz):
                acc[parity, k, :, lanes] += weight * local[k]
        return carry

    lax.fori_loop(0, blocks, solve, 0)
    even = [jnp.sum(acc[0, k], axis=0, keepdims=True) for k in range(nz)]
    odd = [jnp.sum(acc[1, k], axis=0, keepdims=True) for k in range(nz)]
    west = jnp.concatenate([e + o for e, o in zip(even, odd)], 0)
    east_end = jnp.concatenate([e - o for e, o in zip(even, odd)], 0) + leaving
    width = ny // slabs
    hx = nx // 2
    for j in range(slabs):
        lanes = slice(j * width, (j + 1) * width)
        out[j, 0:hx, :] = jnp.concatenate([bottom[:hx, lanes], bottom[hx:, lanes]], 1)
        out[j, hx:nx, :] = jnp.concatenate([top[:hx, lanes], top[hx:, lanes]], 1)
        out[j, nx : nx + nz, :] = jnp.concatenate([west[:, lanes], east_end[:, lanes]], 1)


def swap_halves(value):
    width = value.shape[1] // 2
    return jnp.concatenate([value[:, width:], value[:, :width]], 1)


def in_first_half(value):
    return lax.broadcasted_iota(jnp.int32, value.shape, 1) < value.shape[1] // 2


def ends_kernel(nz, ends, final, pairs, lam_b, sums, sines, out, out_more, acc):
    slabs = ends.shape[0]
    nx = ends.shape[1] - nz
    hx = nx // 2
    total = slabs * nz
    shift = pairs[0:hx, :] + lam_b[lax.axis_index("gz")][0:1, :]
    spike = spike_of(shift, nz)
    below, above = interface_chain(
        spike[0],
        spike[nz - 1],
        [ends[s, 0:hx, :] for s in range(slabs)],
        [ends[s, hx:nx, :] for s in range(slabs)],
    )
    weight = pairs[hx:nx, :]
    spike = [weight * g for g in spike]
    for s in range(slabs):
        for k in range(nz):
            term = spike[k] * below[s] + spike[nz - 1 - k] * above[s]
            row = (s * nz + k) * 8
            acc[row : row + 8, :] = jnp.sum(term.reshape(hx // 8, 8, term.shape[1]), axis=0)
    both = dot3((sums[:total, :], sums[total:, :]), split(acc[...]))
    other = swap_halves(both)
    both = jnp.where(in_first_half(both), both + other, other - both)
    rows = jnp.concatenate([ends[s, nx : nx + nz, :] for s in range(slabs)], 0)
    both = both + dot3((sines[:total, :], sines[total:, :]), split(rows))
    out[...] = both
    out_more[:total, :] = both
    lanes = both.shape[1]
    for n in range(final.shape[1] // lanes):
        out_more[total + n * nz : total + (n + 1) * nz, :] = final[:, n * lanes : (n + 1) * lanes]


def power(value, count):
    result = None
    while count:
        if count & 1:
            result = value if result is None else result * value
        count >>= 1
        if count:
            value = value * value
    return result


def correct_kernel(nz, groups, ends, *rest):
    found = rest[:groups]
    pairs, lam_b, sines, out, jump = rest[groups:]
    slabs, width = ends.shape[0], ends.shape[2] // 2
    nx = ends.shape[1] - nz
    hx = nx // 2
    total = slabs * nz
    row_b = lam_b[lax.axis_index("gz")][0:1, :]
    shift = pairs[nx:, :width] + row_b[:, :width]
    cosh = 1.0 + 0.5 * shift
    sinh = jnp.sqrt(shift + 0.25 * shift * shift)
    grow = cosh + sinh
    decay = 1.0 / grow
    far = power(decay, nx)
    far2 = far * far
    scale = 1.0 / (sinh * (1.0 - far2))
    self2 = ((1.0 + far2) + (decay + far2 * grow)) * scale
    cross2 = 2.0 * (1.0 + cosh) * far * scale
    inverse = {}
    for f in range(groups):
        key = min(f, groups - f)
        if key not in inverse:
            inverse[key] = 1.0 / (1.0 + self2 - float(np.cos(2 * np.pi * f / groups)) * cross2)
    kernel = {}
    for n in range(groups // 2 + 1):
        value = None
        for f in range(groups):
            factor = float(np.cos(2 * np.pi * f * n / groups)) / groups
            term = factor * inverse[min(f, groups - f)]
            value = term if value is None else value + term
        kernel[n] = value
    jumps_east, jumps_west = None, None
    for n in range(groups):
        nxt = (n + 1) % groups
        t = found[n][:total, width:] - found[nxt][:total, :width]
        east_term = kernel[min(n, groups - n)] * t
        west_term = kernel[min(nxt, groups - nxt)] * t
        jumps_east = east_term if jumps_east is None else jumps_east + east_term
        jumps_west = west_term if jumps_west is None else jumps_west + west_term
    both = dot3((sines[:total, :], sines[total:, :]), split(jnp.concatenate([jumps_west, jumps_east], 1)))
    other = swap_halves(both)
    jump[...] = jnp.where(in_first_half(both), both - other, both + other)
    shift = pairs[0:hx, :] + row_b
    spike = spike_of(shift, nz)
    weight = pairs[hx:nx, :]
    loads = [weight * g for g in spike]
    bottoms, tops = [], []
    for s in range(slabs):
        low, high = ends[s, 0:hx, :], ends[s, hx:nx, :]
        for k in range(nz):
            q = jump[s * nz + k : s * nz + k + 1, :]
            low = low + loads[k] * q
            high = high + loads[nz - 1 - k] * q
        bottoms.append(low)
        tops.append(high)
    below, above = interface_chain(spike[0], spike[nz - 1], bottoms, tops)
    for s in range(slabs):
        out[s, 0:hx, :] = below[s]
        out[s, hx:nx, :] = above[s]
        out[s, nx : nx + nz, :] = both[s * nz : (s + 1) * nz, :]


def backward_kernel(
    nz, slabs, chunk,
    modes, crown, solved,
    obs, up, east, north,
    from_west, side_east, f_below, low, low_above,
    tables, east_table, east_values, lam_b,
    out_east, out_north, out_up, out_p, out_r,
    work, below, above, found, half, press, coming, p_below, p_above,
):
    step = pl.program_id(0)
    last = step == pl.num_programs(0) - 1
    ny = east.shape[1]
    hy = ny // 2
    nx = chunk * pl.num_programs(0)
    size = chunk * nz
    lift = jnp.where(lax.axis_index("gz") == 0, 1.0, 0.0).astype(F32)

    def north_back(value):
        even = dot3(split(value[:, :hy]), north_pair(tables, 0))
        odd = dot3(split(value[:, hy:]), north_pair(tables, 2))
        return even + odd, even - odd

    @pl.when(step == 0)
    def _():
        width = ny // slabs
        west, east_end = [], []
        hx = nx // 2
        for j in range(slabs):
            lanes = slice(j * width, (j + 1) * width)
            below[:hx, lanes] = solved[j, 0:hx, :width]
            below[hx:, lanes] = solved[j, 0:hx, width:]
            above[:hx, lanes] = solved[j, hx:nx, :width]
            above[hx:, lanes] = solved[j, hx:nx, width:]
            west.append(solved[j, nx : nx + nz, :width])
            east_end.append(solved[j, nx : nx + nz, width:])
        west = jnp.concatenate(west, 1)
        east_end = jnp.concatenate(east_end, 1)
        found[0] = west - east_end
        found[1] = west + east_end
        blocks = nx // 8

        def solve(n, carry):
            at = pl.ds(pl.multiple_of(n * 8, 8), 8)
            parity = n // (blocks // 2)
            for lane in range(0, ny, 128):
                lanes = slice(lane, lane + 128)
                shift = east_values[0, at, :] + lam_b[:, lanes]
                weight = east_values[1, at, :]
                right = []
                for k in range(nz):
                    q = jnp.broadcast_to(found[parity, pl.ds(k, 1), lanes], weight.shape)
                    plane = modes[k, at, lanes] if k < nz - 1 else crown[at, lanes]
                    right.append(plane + weight * q)
                right[0] = right[0] + below[at, lanes]
                right[nz - 1] = right[nz - 1] + above[at, lanes]
                local = slab_solve(shift, right)
                for k in range(nz):
                    work[k, at, lanes] = local[k]
            return carry

        lax.fori_loop(0, blocks, solve, 0)
        left = east_left(east_table[1])
        for k in range(nz):
            put_lanes(half, pl.ds(nz + k, nx, stride=nz), east_dot(left, work[k]), 0)
        first, final = slice(nz, 2 * nz), slice(nx * nz, (nx + 1) * nz)
        put_lanes(half, slice(0, nz), get_lanes(half, first) + west, 0)
        put_lanes(half, slice((nx + 1) * nz, (nx + 2) * nz), get_lanes(half, final) - east_end, 0)
        both = jnp.concatenate(
            [east_dot(left, below[...]), east_dot(left, above[...]), get_lanes(half, slice(0, size + nz))], 0
        )
        both = jnp.concatenate(north_back(both), 1)
        p_below[...] = both[:nx] - f_below[...] * low[1]
        p_above[...] = both[nx : 2 * nx]
        press[...] = both[2 * nx :]

    base = step * chunk

    def cells(x):
        return pl.ds(pl.multiple_of(x * nz, nz), nz)

    rows = pl.ds(pl.multiple_of((base + chunk + 1) * nz, nz), size)
    coming[:, :hy], coming[:, hy:] = north_back(get_lanes(half, rows))

    lanes = from_west.shape[1]
    total = from_west.shape[0] - nz * (ny // lanes)
    side_west = jnp.concatenate(
        [from_west[total + n * nz : total + (n + 1) * nz, :] for n in range(ny // lanes)], 1
    )
    here = fluid_of(obs[cells(base), :])
    before = fluid_of(obs[cells(jnp.maximum(base - 1, 0)), :])
    before = jnp.where(step == 0, side_west, before)
    after_row = cells(jnp.minimum(base + chunk, nx - 1))
    after_fluid = fluid_of(obs[after_row, :])
    after_flux = jnp.where(last, side_east[nz:, :], after_fluid * east[after_row, :])
    after_fluid = jnp.where(last, side_east[0:nz, :], after_fluid)

    p = press[nz : 2 * nz, :]
    first_flux = here * before * east[cells(base), :]
    p_before = press[0:nz, :] - jnp.where(step == 0, 1.0, 0.0).astype(F32) * first_flux
    east_done = first_flux - here * before * (p - p_before)
    for i in range(chunk):
        at = slice(i * nz, (i + 1) * nz)
        own = cells(base + i)
        line = pl.ds(base + i, 1)
        if i < chunk - 1:
            nxt = cells(base + i + 1)
            after = fluid_of(obs[nxt, :])
            flux = after * east[nxt, :]
            p_next = press[(i + 2) * nz : (i + 3) * nz, :]
        else:
            after, flux = after_fluid, after_flux
            p_next = coming[0:nz, :] + jnp.where(last, 1.0, 0.0).astype(F32) * (here * flux)
        east_next_done = here * (flux - after * (p_next - p))
        north_done = here * north_roll(here, 1) * (north[own, :] - (p - north_roll(p, 1)))
        fluid_below = below_of(here, f_below[line, :] + lift)
        up_done = here * fluid_below * (up[own, :] - (p - below_of(p, p_below[line, :])))
        edge = here[nz - 1 : nz, :] * (
            low_above[1, line, :] - low_above[0, line, :] * (p_above[line, :] - p[nz - 1 : nz, :])
        )
        out_east[at, :] = east_done
        out_north[at, :] = north_done
        out_up[at, :] = up_done
        out_p[at, :] = p
        out_r[at, :] = (
            (east_done - east_next_done)
            + (north_done - north_roll(north_done, -1))
            + (up_done - above_of(up_done, edge))
        )
        here, p, east_done = after, p_next, east_next_done
    press[0:nz, :] = press[size : size + nz, :]
    press[nz:, :] = coming[...]


def local(groups, slabs, east_velocity, north_velocity, upward_velocity, obstacle):
    nx, nz, ny = east_velocity.shape
    total = slabs * nz
    width = ny // slabs
    flat = [a.reshape(nx * nz, ny) for a in (obstacle, east_velocity, north_velocity, upward_velocity)]
    obs, east, north, up_in = flat

    even_np, odd_np, lam_b_np = north_tables(ny)
    block_np, lam_a_np = east_tables(nx)
    sine_np, mu_np = sine_table(total)
    tables = np.concatenate([*pair_np(even_np), *pair_np(odd_np), *pair_np(odd_np.T)], 0)
    east_table = np.stack([np.concatenate(pair_np(t), 1) for t in (block_np, block_np.T)])
    sines = np.concatenate(pair_np(sine_np), 0)
    sums = np.repeat(sines, 8, axis=1)
    east_values = np.stack([np.repeat(v[:, None], 128, 1) for v in (lam_a_np, block_np[:, 0])]).astype(np.float32)
    lam_b = np.repeat(lam_b_np[None], 8, 0).astype(np.float32)
    part = np.tile(lam_b_np.reshape(slabs, 1, width), (1, 8, 2)).astype(np.float32)

    def paired(column):
        return np.repeat(column.reshape(2, nx // 2).T, width, 1)

    pairs = np.concatenate(
        [paired(lam_a_np), paired(block_np[:, 0]), np.repeat(mu_np[:, None], 2 * width, 1)], 0
    ).astype(np.float32)

    chunk = 16
    steps = nx // chunk
    lanes = ny // 128
    params = pltpu.CompilerParams(vmem_limit_bytes=VMEM_LIMIT)
    kept = pl.BlockSpec(memory_space=pltpu.VMEM)
    far = pl.BlockSpec(memory_space=pltpu.HBM)

    def array(*shape):
        return jax.ShapeDtypeStruct(shape, F32)

    blocked = array(lanes, nx * nz, 128)
    fluid, up, high, low, side, final = pl.pallas_call(
        functools.partial(load_kernel, nz),
        in_specs=[far] * 3,
        out_specs=[kept] * 6,
        out_shape=[blocked, blocked, array(nx, ny), array(2, nx, ny), array(2 * nz, ny), array(nz, ny)],
        scratch_shapes=[
            pltpu.VMEM((lanes, nx * nz, 128), jnp.int32),
            pltpu.VMEM((nz, ny), F32),
            pltpu.SemaphoreType.DMA((2 * lanes + 1,)),
        ],
        compiler_params=pltpu.CompilerParams(vmem_limit_bytes=LOAD_LIMIT),
        name="load",
    )(obs, up_in, east)

    rising = [(i, i + 1) for i in range(slabs - 1)]
    falling = [(i + 1, i) for i in range(slabs - 1)]
    low_above = lax.ppermute(low, "gz", falling)
    side_east = lax.ppermute(side, "xy", [((i + 1) % groups, i) for i in range(groups)])

    cells = nx * nz * ny
    modes = pl.pallas_call(
        functools.partial(interior_kernel, nz, chunk),
        in_specs=[kept] * 6,
        out_specs=kept,
        out_shape=array(nz, nx, ny),
        scratch_shapes=[
            pltpu.VMEM((chunk * nz, ny), F32),
            pltpu.VMEM((chunk * nz, ny), F32),
            pltpu.VMEM((lanes, nx * nz, 128), F32),
        ],
        compiler_params=params,
        cost_estimate=pl.CostEstimate(flops=cells * 2 * 3 * (ny // 2 + nx), bytes_accessed=20 * cells, transcendentals=0),
        name="interior",
    )(fluid, up, east, north, tables, east_table)
    ends_shape = array(slabs, nx + nz, 2 * width)
    crown, ends = pl.pallas_call(
        functools.partial(joined_kernel, nz, slabs),
        in_specs=[kept] * 9,
        out_specs=[kept] * 2,
        out_shape=[array(nx, ny), ends_shape],
        scratch_shapes=[
            pltpu.VMEM((nx, ny), F32),
            pltpu.VMEM((nx, ny), F32),
            pltpu.VMEM((2, nz, 8, ny), F32),
        ],
        compiler_params=params,
        name="joined",
    )(modes, high, low_above, final, side_east, tables, east_table, east_values, lam_b)

    ends = lax.all_to_all(ends, "gz", split_axis=0, concat_axis=0, tiled=True)
    own, own_more = pl.pallas_call(
        functools.partial(ends_kernel, nz),
        in_specs=[kept] * 6,
        out_specs=[kept] * 2,
        out_shape=[array(total, 2 * width), array(total + nz * ny // (2 * width), 2 * width)],
        scratch_shapes=[pltpu.VMEM((total * 8, 2 * width), F32)],
        compiler_params=params,
        name="ends",
    )(ends, final, pairs, part, sums, sines)
    found = [own]
    for shift in range(1, groups):
        sent = own_more if shift == groups - 1 else own
        found.append(lax.ppermute(sent, "xy", [((i + shift) % groups, i) for i in range(groups)]))
    high, own = lax.optimization_barrier((high, own))
    f_below = lax.ppermute(high, "gz", rising)
    f_below, found[0] = lax.optimization_barrier((f_below, found[0]))
    solved = pl.pallas_call(
        functools.partial(correct_kernel, nz, groups),
        in_specs=[kept] * (groups + 4),
        out_specs=kept,
        out_shape=ends_shape,
        scratch_shapes=[pltpu.VMEM((total, 2 * width), F32)],
        compiler_params=params,
        name="correct",
    )(ends, *found, pairs, part, sines)
    solved = lax.all_to_all(solved, "gz", split_axis=0, concat_axis=0, tiled=True)

    big = pl.BlockSpec((chunk * nz, ny), lambda i: (i, 0))
    outs = pl.pallas_call(
        functools.partial(backward_kernel, nz, slabs, chunk),
        grid=(steps,),
        in_specs=[kept] * 16,
        out_specs=[big] * 5,
        out_shape=[array(nx * nz, ny)] * 5,
        scratch_shapes=[
            pltpu.VMEM((nz, nx, ny), F32),
            pltpu.VMEM((nx, ny), F32),
            pltpu.VMEM((nx, ny), F32),
            pltpu.VMEM((2, nz, ny), F32),
            pltpu.VMEM((lanes, (nx + chunk + 1) * nz, 128), F32),
            pltpu.VMEM(((chunk + 1) * nz, ny), F32),
            pltpu.VMEM((chunk * nz, ny), F32),
            pltpu.VMEM((nx, ny), F32),
            pltpu.VMEM((nx, ny), F32),
        ],
        compiler_params=params,
        name="backward",
    )(modes, crown, solved, obs, up_in, east, north, found[-1], side_east, f_below, low, low_above,
      tables, east_table, east_values, lam_b)
    return tuple(o.reshape(nx, nz, ny) for o in outs)


def solution(mesh):
    placed = P("xy", "gz", None)
    return jax.shard_map(
        functools.partial(local, mesh.shape["xy"], mesh.shape["gz"]),
        mesh=mesh,
        in_specs=(placed,) * 4,
        out_specs=(placed,) * 5,
        check_vma=False,
    )
```

time: 73.1 us -> 65.6 us (0.90)
  local copies, waits for them, and re-layouts: 6.03 us -> 0.07 us
  blocking collectives: 27.7 us -> 26.1 us
  waiting for transfers between devices: 2 us -> 3.21 us
  Pallas kernels: 21.2 us -> 20.2 us
  starting transfers between devices: 13.5 us -> 14.3 us
  other arithmetic: 0.76 us -> 0 us
    unnamed x58 -> x24, local copies, waits for them, and re-layouts: 6.03 us -> 0.07 us
    ppermute x5 -> x4, starting transfers between devices: 7.45 us -> 9.58 us  [the longest x1 4.85 us: local(): lax.ppermute(side, 'xy', [((i + 1) % groups, i) for i in range(groups)])]
    ppermute x1, starting transfers between devices: 4.09 us -> 2.65 us  [local(): f_below = lax.ppermute(high, 'gz', rising)]
    pallas_call x1, Pallas kernels: 11.6 us -> 10.2 us  [local(): pl.pallas_call(functools.partial(backward_kernel, nz, slabs, chunk), grid...]
    all_to_all x1, blocking collectives: 14.2 us -> 13.3 us  [local(): ends = lax.all_to_all(ends, 'gz', split_axis=0, concat_axis=0, tiled=True)]
    ppermute x1, waiting for transfers between devices: 0.01 us -> 0.9 us  [local(): low_above = lax.ppermute(low, 'gz', falling)]
    pallas_call x4, Pallas kernels: 7.41 us -> 8.17 us  [the longest x1 3.62 us: local(): pl.pallas_call(functools.partial(interior_kernel, nz, chunk), in_specs=[k...]
    convert_element_type x1 -> x0, other arithmetic: 0.75 us -> none  [local(): f_first = (1 - obs[:nz]).astype(F32)]
  transfers between devices with their start and end apart: 7 -> 6, of which waited for: 2 -> 2; matrix products, arithmetic and copies ran while one was open for 0% -> 0% of each run, Pallas kernels for 8% -> 6%
where the time goes in v4:
time: 65.6 us; the launch traced here: 64.6 us
  blocking collectives  26.1 us (40%)
  Pallas kernels  20.2 us (31%)
  starting transfers between devices  14.3 us (22%)
  waiting for transfers between devices  3.21 us (5%)
  between operations  0.8 us (1%)
    all_to_all x1, blocking collectives, local(): ends = lax.all_to_all(ends, 'gz', split_axis=0, concat_axis=0, tiled=True)  13.3 us
    all_to_all x1, blocking collectives, local(): lax.all_to_all(solved, 'gz', split_axis=0, concat_axis=0, tiled=True)  12.8 us
    pallas_call x1, Pallas kernels, local(): pl.pallas_call(functools.partial(backward_kernel, nz, slabs, chunk), grid...  10.2 us
    ppermute x1, starting transfers between devices, local(): lax.ppermute(side, 'xy', [((i + 1) % groups, i) for i in range(groups)])  4.85 us
    ppermute x3, starting transfers between devices, local(): lax.ppermute(sent, 'xy', [((i + shift) % groups, i) for i in range(groups)])  4.73 us
    pallas_call x1, Pallas kernels, local(): pl.pallas_call(functools.partial(interior_kernel, nz, chunk), in_specs=[k...  3.62 us
    pallas_call x1, Pallas kernels, local(): pl.pallas_call(functools.partial(load_kernel, nz), in_specs=[far] * 3, ou...  2.68 us
    ppermute x1, starting transfers between devices, local(): f_below = lax.ppermute(high, 'gz', rising)  2.65 us
  transfers between devices with their start and end apart: 6, of which 2 were waited for; matrix products, arithmetic and copies ran while one was open for 0% of the time, Pallas kernels for 6%

profile of v4, /device:TPU:1, one launch (start us, length us, event | category | flops | bytes accessed | tf_op | source)
XLA Modules:
  0.0 64.6 jit_solution(14335178818672424133)
XLA Ops:
  0.6 0.0 copy-start
  0.6 0.0 copy-start.3
  0.7 0.0 copy-start.4
  0.7 0.0 copy-start.5
  0.7 2.7 %load.1 = (f32[4,1024,128]{2,1,0:T(8,128)S(1)}, f32[4,1024,128]{2,1,0:T(8,128)S(1)}, f32[128,512]{1,0:T(8,128)S(1)}, f32[2,128,512]{2,1,0:T(8,128)S(1)}, f32[16,512]{1,0:T(8,128)S(1)}, /*index=5*/f32[8,512]{1,0:T(8,128)S(1)}) custom-call(s32[1024,512]{1,0:T(8,128)} %bitcast.12, f32[1024,512]{1,0:T(8,128)} %bitcast.14, f32[1024,512]{1,0:T(8,128)} %bitcast.9), custom_call_target="tpu_custom_call" | custom-call | tf_op jit(solution)/shard_map/load/pallas_call | solution.py:601
  3.4 2.1 %collective-permute-start = (f32[2,128,512]{2,1,0:T(8,128)S(1)}, f32[2,128,512]{2,1,0:T(8,128)S(1)}, u32[]{:S(2)}, u32[]{:S(2)}) collective-permute-start(f32[2,128,512]{2,1,0:T(8,128)S(1)} %get-tuple-element.26.low), channel_id=1, source_target_pairs={{4,0},{8,4},{12,8},{16,12},{20,16},{24,20},{28,24},{5,1},{9,5},{13... | collective-permute-start | bytes 1572872 | tf_op jit(solution)/shard_map/ppermute | solution.py:617
  5.4 4.8 %collective-permute-start.1 = (f32[16,512]{1,0:T(8,128)S(1)}, f32[16,512]{1,0:T(8,128)S(1)}, u32[]{:S(2)}, u32[]{:S(2)}) collective-permute-start(f32[16,512]{1,0:T(8,128)S(1)} %get-tuple-element.28), channel_id=1, source_target_pairs={{1,0},{2,1},{3,2},{0,3},{5,4},{6,5},{7,6},{4,7},{9,8},{10,9},{11,1... | collective-permute-start | bytes 98312 | tf_op jit(solution)/shard_map/ppermute | solution.py:618
  10.3 0.0 copy-done
  10.3 0.0 copy-done.3
  10.3 0.0 copy-done.4
  10.3 0.0 copy-done.5
  10.3 0.0 copy-start.6
  10.3 0.0 copy-start.11
  10.3 3.6 %interior.1.modes_in.modes = f32[8,128,512]{2,1,0:T(8,128)S(1)} custom-call(f32[4,1024,128]{2,1,0:T(8,128)S(1)} %get-tuple-element.23.fluid, f32[4,1024,128]{2,1,0:T(8,128)S(1)} %get-tuple-element.24.up, f32[1024,512]{1,0:T(8,128)S(1)} %bitcast.10, f32[1024,512]{1,0:T(8,128)S(1)} %bitcast.16, bf16[1536,256]{1,0:T(8,128)(2,1)S(1)} %copy-done.4, ...), custom_call_target="tpu_custom_call" | custom-call | flops 1207959552 | bytes 10485760 | tf_op jit(solution)/shard_map/interior/pallas_call | solution.py:621
  13.9 0.0 collective-permute-done.1.side_east
  14.0 0.9 %collective-permute-done.low_above = f32[2,128,512]{2,1,0:T(8,128)S(1)} collective-permute-done((f32[2,128,512]{2,1,0:T(8,128)S(1)}, f32[2,128,512]{2,1,0:T(8,128)S(1)}, u32[]{:S(2)}, u32[]{:S(2)}) %collective-permute-start) | collective-permute-done | bytes 524320 | tf_op jit(solution)/shard_map/ppermute | solution.py:617
  14.9 0.0 copy-done.6
  14.9 0.0 copy-done.11
  14.9 0.0 copy-start.7
  14.9 0.0 copy-start.8
  14.9 0.0 copy-start.9
  14.9 0.0 copy-start.10
  14.9 1.8 %joined.1 = (f32[128,512]{1,0:T(8,128)S(1)}, f32[8,136,128]{2,1,0:T(8,128)S(1)}) custom-call(f32[8,128,512]{2,1,0:T(8,128)S(1)} %interior.1.modes_in.modes, f32[128,512]{1,0:T(8,128)S(1)} %get-tuple-element.32.high, f32[2,128,512]{2,1,0:T(8,128)S(1)} %collective-permute-done.low_above, f32[8,512]{1,0:T(8,128)S(1)} %get-tuple-element.27.final, ...), custom_call_target="tpu_custom_call" | custom-call | tf_op jit(solution)/shard_map/joined/pallas_call | solution.py:636
  16.7 0.0 copy-start.1
  16.7 0.0 copy-start.2
  16.7 13.3 %all_to_all.10.ends = f32[8,136,128]{2,1,0:T(8,128)S(1)} all-to-all(f32[8,136,128]{2,1,0:T(8,128)S(1)} %get-tuple-element.30), channel_id=1, replica_groups=mesh['gz'=8,'xy'=4] {'gz'}, dimensions={0} | all-to-all | bytes 1114112 | tf_op jit(solution)/shard_map/all_to_all | solution.py:650
  30.0 0.0 copy-done.7
  30.0 0.0 copy-done.8
  30.0 0.0 copy-done.9
  30.0 0.0 copy-done.10
  30.1 0.8 %ends.1 = (f32[64,128]{1,0:T(8,128)S(1)}, f32[96,128]{1,0:T(8,128)S(1)}) custom-call(f32[8,136,128]{2,1,0:T(8,128)S(1)} %all_to_all.10.ends, f32[8,512]{1,0:T(8,128)S(1)} %get-tuple-element.27.final, f32[192,128]{1,0:T(8,128)S(1)} %copy-done.7, f32[8,8,128]{2,1,0:T(8,128)S(1)} %copy-done.10, bf16[128,512]{1,0:T(8,128)(2,1)S(1)} %copy-done.8, ...), custom_call_target="tpu_custom_call" | custom-call | tf_op jit(solution)/shard_map/ends/pallas_call | solution.py:651
  30.9 2.6 %collective-permute-start.2 = (f32[128,512]{1,0:T(8,128)S(1)}, f32[128,512]{1,0:T(8,128)S(1)}, u32[]{:S(2)}, u32[]{:S(2)}) collective-permute-start(f32[128,512]{1,0:T(8,128)S(1)} %get-tuple-element.32.high), channel_id=1, source_target_pairs={{0,4},{4,8},{8,12},{12,16},{16,20},{20,24},{24,28},{1,5},{5,9},{9,... | collective-permute-start | bytes 786440 | tf_op jit(solution)/shard_map/ppermute | solution.py:665
  33.5 1.4 %collective-permute-start.5 = (f32[96,128]{1,0:T(8,128)S(1)}, f32[96,128]{1,0:T(8,128)S(1)}, u32[]{:S(2)}, u32[]{:S(2)}) collective-permute-start(f32[96,128]{1,0:T(8,128)S(1)} %get-tuple-element.34), channel_id=1, source_target_pairs={{3,0},{0,1},{1,2},{2,3},{7,4},{4,5},{5,6},{6,7},{11,8},{8,9},{9,10... | collective-permute-start | bytes 147464 | tf_op jit(solution)/shard_map/ppermute | solution.py:663
  34.9 2.3 %collective-permute-start.4 = (f32[64,128]{1,0:T(8,128)S(1)}, f32[64,128]{1,0:T(8,128)S(1)}, u32[]{:S(2)}, u32[]{:S(2)}) collective-permute-start(f32[64,128]{1,0:T(8,128)S(1)} %get-tuple-element.33.rest_0_), channel_id=1, source_target_pairs={{2,0},{3,1},{0,2},{1,3},{6,4},{7,5},{4,6},{5,7},{10,8},{11,9},{8,1... | collective-permute-start | bytes 98312 | tf_op jit(solution)/shard_map/ppermute | solution.py:663
  37.2 1.1 %collective-permute-start.3 = (f32[64,128]{1,0:T(8,128)S(1)}, f32[64,128]{1,0:T(8,128)S(1)}, u32[]{:S(2)}, u32[]{:S(2)}) collective-permute-start(f32[64,128]{1,0:T(8,128)S(1)} %get-tuple-element.33.rest_0_), channel_id=1, source_target_pairs={{1,0},{2,1},{3,2},{0,3},{5,4},{6,5},{7,6},{4,7},{9,8},{10,9},{11,1... | collective-permute-start | bytes 98312 | tf_op jit(solution)/shard_map/ppermute | solution.py:663
  38.3 0.0 collective-permute-done.2.f_below
  38.3 2.3 %collective-permute-done.4.rest_2_ = f32[64,128]{1,0:T(8,128)S(1)} collective-permute-done((f32[64,128]{1,0:T(8,128)S(1)}, f32[64,128]{1,0:T(8,128)S(1)}, u32[]{:S(2)}, u32[]{:S(2)}) %collective-permute-start.4) | collective-permute-done | bytes 32800 | tf_op jit(solution)/shard_map/ppermute | solution.py:663
  40.6 0.0 collective-permute-done.3.rest_1_
  40.6 0.0 collective-permute-done.5.rest_3_.from_west
  40.6 1.1 %correct.1 = f32[8,136,128]{2,1,0:T(8,128)S(1)} custom-call(f32[8,136,128]{2,1,0:T(8,128)S(1)} %all_to_all.10.ends, f32[64,128]{1,0:T(8,128)S(1)} %get-tuple-element.33.rest_0_, f32[64,128]{1,0:T(8,128)S(1)} %collective-permute-done.3.rest_1_, f32[64,128]{1,0:T(8,128)S(1)} %collective-permute-done.4.rest_2_, ...), custom_call_target="tpu_custom_call" | custom-call | tf_op jit(solution)/shard_map/correct/pallas_call | solution.py:667
  41.6 12.8 %all_to_all.11.solved = f32[8,136,128]{2,1,0:T(8,128)S(1)} all-to-all(f32[8,136,128]{2,1,0:T(8,128)S(1)} %correct.1), channel_id=1, replica_groups=mesh['gz'=8,'xy'=4] {'gz'}, dimensions={0} | all-to-all | bytes 1114112 | tf_op jit(solution)/shard_map/all_to_all | solution.py:676
  54.4 0.0 copy-done.1
  54.4 0.0 copy-done.2
  54.4 10.2 %backward.1 = (f32[1024,512]{1,0:T(8,128)}, f32[1024,512]{1,0:T(8,128)}, f32[1024,512]{1,0:T(8,128)}, f32[1024,512]{1,0:T(8,128)}, f32[1024,512]{1,0:T(8,128)}) custom-call(f32[8,128,512]{2,1,0:T(8,128)S(1)} %interior.1.modes_in.modes, f32[128,512]{1,0:T(8,128)S(1)} %get-tuple-element.29.crown, f32[8,136,128]{2,1,0:T(8,128)S(1)} %all_to_all.11.solved, ...), custom_call_target="tpu_custom_call" | custom-call | tf_op jit(solution)/shard_map/backward/pallas_call | solution.py:679
Async XLA Ops:
  0.6 9.7 %copy-start = (f32[128,8,512]{2,1,0:T(8,128)S(1)}, f32[128,8,512]{2,1,0:T(8,128)}, u32[]{:S(2)}) copy-start(f32[128,8,512]{2,1,0:T(8,128)} %param.12) | copy-start | bytes 6291460
  0.6 9.6 %copy-start.3 = (f32[128,8,512]{2,1,0:T(8,128)S(1)}, f32[128,8,512]{2,1,0:T(8,128)}, u32[]{:S(2)}) copy-start(f32[128,8,512]{2,1,0:T(8,128)} %param.13) | copy-start | bytes 6291460
  0.7 9.6 %copy-start.4 = (bf16[1536,256]{1,0:T(8,128)(2,1)S(1)}, bf16[1536,256]{1,0:T(8,128)(2,1)}, u32[]{:S(2)}) copy-start(bf16[1536,256]{1,0:T(8,128)(2,1)} %constant.16.clone.tables) | copy-start | bytes 2359300
  0.7 9.6 %copy-start.5 = (bf16[2,128,256]{2,1,0:T(8,128)(2,1)S(1)}, bf16[2,128,256]{2,1,0:T(8,128)(2,1)}, u32[]{:S(2)}) copy-start(bf16[2,128,256]{2,1,0:T(8,128)(2,1)} %constant.17.clone.east_table) | copy-start | bytes 393220
  3.4 11.5 %collective-permute-start = (f32[2,128,512]{2,1,0:T(8,128)S(1)}, f32[2,128,512]{2,1,0:T(8,128)S(1)}, u32[]{:S(2)}, u32[]{:S(2)}) collective-permute-start(f32[2,128,512]{2,1,0:T(8,128)S(1)} %get-tuple-element.26.low), channel_id=1, source_target_pairs={{4,0},{8,4},{12,8},{16,12},{20,16},{24,20},{28,24},{5,1},{9,5},{13... | collective-permute-start | bytes 1572872 | tf_op jit(solution)/shard_map/ppermute | solution.py:617
  5.4 8.5 %collective-permute-start.1 = (f32[16,512]{1,0:T(8,128)S(1)}, f32[16,512]{1,0:T(8,128)S(1)}, u32[]{:S(2)}, u32[]{:S(2)}) collective-permute-start(f32[16,512]{1,0:T(8,128)S(1)} %get-tuple-element.28), channel_id=1, source_target_pairs={{1,0},{2,1},{3,2},{0,3},{5,4},{6,5},{7,6},{4,7},{9,8},{10,9},{11,1... | collective-permute-start | bytes 98312 | tf_op jit(solution)/shard_map/ppermute | solution.py:618
  10.3 4.6 %copy-start.6 = (f32[2,128,128]{2,1,0:T(8,128)S(1)}, f32[2,128,128]{2,1,0:T(8,128)}, u32[]{:S(2)}) copy-start(f32[2,128,128]{2,1,0:T(8,128)} %constant.18.clone.east_values) | copy-start | bytes 393220
  10.3 4.6 %copy-start.11 = (f32[8,512]{1,0:T(8,128)S(1)}, f32[8,512]{1,0:T(8,128)}, u32[]{:S(2)}) copy-start(f32[8,512]{1,0:T(8,128)} %constant.19.clone.lam_b) | copy-start | bytes 49156
  14.9 15.2 %copy-start.7 = (f32[192,128]{1,0:T(8,128)S(1)}, f32[192,128]{1,0:T(8,128)}, u32[]{:S(2)}) copy-start(f32[192,128]{1,0:T(8,128)} %constant.20.clone.pairs.rest_4_) | copy-start | bytes 294916
  14.9 15.2 %copy-start.8 = (bf16[128,512]{1,0:T(8,128)(2,1)S(1)}, bf16[128,512]{1,0:T(8,128)(2,1)}, u32[]{:S(2)}) copy-start(bf16[128,512]{1,0:T(8,128)(2,1)} %constant.22.clone.sums) | copy-start | bytes 393220
  14.9 15.2 %copy-start.9 = (bf16[128,64]{1,0:T(8,128)(2,1)S(1)}, bf16[128,64]{1,0:T(8,128)(2,1)}, u32[]{:S(2)}) copy-start(bf16[128,64]{1,0:T(8,128)(2,1)} %constant.23.clone.sines.rest_6_) | copy-start | bytes 49156
  14.9 15.2 %copy-start.10 = (f32[8,8,128]{2,1,0:T(8,128)S(1)}, f32[8,8,128]{2,1,0:T(8,128)}, u32[]{:S(2)}) copy-start(f32[8,8,128]{2,1,0:T(8,128)} %constant.21.clone.lam_b.rest_5_) | copy-start | bytes 98308
  16.7 37.7 %copy-start.1 = (s32[128,8,512]{2,1,0:T(8,128)S(1)}, s32[128,8,512]{2,1,0:T(8,128)}, u32[]{:S(2)}) copy-start(s32[128,8,512]{2,1,0:T(8,128)} %param.15) | copy-start | bytes 6291460
  16.7 37.7 %copy-start.2 = (f32[128,8,512]{2,1,0:T(8,128)S(1)}, f32[128,8,512]{2,1,0:T(8,128)}, u32[]{:S(2)}) copy-start(f32[128,8,512]{2,1,0:T(8,128)} %param.14) | copy-start | bytes 6291460
  30.9 7.4 %collective-permute-start.2 = (f32[128,512]{1,0:T(8,128)S(1)}, f32[128,512]{1,0:T(8,128)S(1)}, u32[]{:S(2)}, u32[]{:S(2)}) collective-permute-start(f32[128,512]{1,0:T(8,128)S(1)} %get-tuple-element.32.high), channel_id=1, source_target_pairs={{0,4},{4,8},{8,12},{12,16},{16,20},{20,24},{24,28},{1,5},{5,9},{9,... | collective-permute-start | bytes 786440 | tf_op jit(solution)/shard_map/ppermute | solution.py:665
  33.5 7.0 %collective-permute-start.5 = (f32[96,128]{1,0:T(8,128)S(1)}, f32[96,128]{1,0:T(8,128)S(1)}, u32[]{:S(2)}, u32[]{:S(2)}) collective-permute-start(f32[96,128]{1,0:T(8,128)S(1)} %get-tuple-element.34), channel_id=1, source_target_pairs={{3,0},{0,1},{1,2},{2,3},{7,4},{4,5},{5,6},{6,7},{11,8},{8,9},{9,10... | collective-permute-start | bytes 147464 | tf_op jit(solution)/shard_map/ppermute | solution.py:663
  34.9 5.7 %collective-permute-start.4 = (f32[64,128]{1,0:T(8,128)S(1)}, f32[64,128]{1,0:T(8,128)S(1)}, u32[]{:S(2)}, u32[]{:S(2)}) collective-permute-start(f32[64,128]{1,0:T(8,128)S(1)} %get-tuple-element.33.rest_0_), channel_id=1, source_target_pairs={{2,0},{3,1},{0,2},{1,3},{6,4},{7,5},{4,6},{5,7},{10,8},{11,9},{8,1... | collective-permute-start | bytes 98312 | tf_op jit(solution)/shard_map/ppermute | solution.py:663
  37.2 3.4 %collective-permute-start.3 = (f32[64,128]{1,0:T(8,128)S(1)}, f32[64,128]{1,0:T(8,128)S(1)}, u32[]{:S(2)}, u32[]{:S(2)}) collective-permute-start(f32[64,128]{1,0:T(8,128)S(1)} %get-tuple-element.33.rest_0_), channel_id=1, source_target_pairs={{1,0},{2,1},{3,2},{0,3},{5,4},{6,5},{7,6},{4,7},{9,8},{10,9},{11,1... | collective-permute-start | bytes 98312 | tf_op jit(solution)/shard_map/ppermute | solution.py:663

commit v5 on v4

--- a/solution.py
+++ b/solution.py
@@ -12,6 +12,8 @@
 F32 = jnp.float32
 BF16 = jnp.bfloat16
 VMEM_LIMIT = 24 * 1024 * 1024
+BACK_ROWS = 8
+BACK_LIMIT = 28 * 1024 * 1024
 LOAD_LIMIT = 48 * 1024 * 1024
 
 
@@ -71,22 +73,30 @@
     return values
 
 
-def slab_solve(shift, right):
+def slab_weights(shift, count):
+    u = chebyshev(shift, count)
+    return u[1:count] + [1.0 / u[count]]
+
+
+def slab_solve(weights, right):
     count = len(right)
-    u = chebyshev(shift, count)
-    inverse = 1.0 / u[count]
+    u, inverse = weights[: count - 1], weights[count - 1]
+
+    def times(n, value):
+        return value if n == 0 else u[n - 1] * value
+
     lower = [right[0]]
     for k in range(1, count):
-        lower.append(lower[-1] + u[k] * right[k])
+        lower.append(lower[-1] + times(k, right[k]))
     upper = [None] * count
     for k in range(count - 2, -1, -1):
-        term = u[count - 2 - k] * right[k + 1] if k < count - 2 else right[k + 1]
+        term = times(count - 2 - k, right[k + 1])
         upper[k] = term if upper[k + 1] is None else upper[k + 1] + term
     out = []
     for k in range(count):
-        value = u[count - 1 - k] * lower[k]
+        value = times(count - 1 - k, lower[k])
         if upper[k] is not None:
-            value = value + u[k] * upper[k]
+            value = value + times(k, upper[k])
         out.append(value * inverse)
     return out
 
@@ -210,7 +220,11 @@
     return dot3(split(low + high), even), dot3(split(low - high), odd)
 
 
-def interior_kernel(nz, chunk, fluid, up, east, north, tables, east_table, modes, src, ready, half):
+def interior_kernel(
+    nz, chunk, fluid, up, east, north, tables, east_table, east_values, lam_b,
+    modes, weights, bottom, top, sums,
+    src, ready, half,
+):
     ny = src.shape[1]
     nx = modes.shape[1]
     count = nx // chunk
@@ -266,13 +280,34 @@
     for k in range(nz):
         modes[k] = east_dot(left, get_lanes(half, pl.ds(k, nx, stride=nz)))
 
+    sums[...] = jnp.zeros_like(sums)
+    blocks = nx // 8
+
+    def solve(n, carry):
+        at = pl.ds(pl.multiple_of(n * 8, 8), 8)
+        parity = n // (blocks // 2)
+        for lane in range(0, ny, 128):
+            lanes = slice(lane, lane + 128)
+            values = slab_weights(east_values[0, at, :] + lam_b[:, lanes], nz)
+            for k in range(nz):
+                weights[k, at, lanes] = values[k]
+            local = slab_solve(values, [modes[k, at, lanes] for k in range(nz)])
+            bottom[at, lanes] = local[0]
+            top[at, lanes] = local[nz - 1]
+            weight = east_values[1, at, :]
+            for k in range(nz):
+                sums[parity, k, :, lanes] += weight * local[k]
+        return carry
+
+    lax.fori_loop(0, blocks, solve, 0)
+
 
 def joined_kernel(
     nz, slabs,
-    modes_in, high, low_above, final, side_east,
-    tables, east_table, east_values, lam_b,
+    modes, weights, bottom_in, top_in, sums_in, high, low_above, final, side_east,
+    tables, east_table, east_values,
     crown, out,
-    bottom, top, acc,
+    bottom, top, sums,
 ):
     nx, ny = high.shape
     leaving = final[...] * side_east[nz:, :]
@@ -280,30 +315,28 @@
     stacked = jnp.concatenate(north_forward(stacked, north_pair(tables, 0), north_pair(tables, 1)), 1)
     top[...] = east_dot(east_left(east_table[0]), stacked[:nx])
     leaving = stacked[nx:]
-    acc[...] = jnp.zeros_like(acc)
+    sums[...] = sums_in[...]
     blocks = nx // 8
 
-    def solve(n, carry):
+    def share(n, carry):
         at = pl.ds(pl.multiple_of(n * 8, 8), 8)
         parity = n // (blocks // 2)
         for lane in range(0, ny, 128):
             lanes = slice(lane, lane + 128)
-            shift = east_values[0, at, :] + lam_b[:, lanes]
-            weight = east_values[1, at, :]
             rising = top[at, lanes]
-            right = [modes_in[k, at, lanes] for k in range(nz)]
-            right[nz - 1] = right[nz - 1] - rising
-            crown[at, lanes] = right[nz - 1]
-            local = slab_solve(shift, right)
-            bottom[at, lanes] = local[0]
-            top[at, lanes] = local[nz - 1] + rising
-            for k in range(nz):
-                acc[parity, k, :, lanes] += weight * local[k]
+            scaled = rising * weights[nz - 1, at, lanes]
+            crown[at, lanes] = modes[nz - 1, at, lanes] - rising
+            bottom[at, lanes] = bottom_in[at, lanes] - scaled
+            top[at, lanes] = top_in[at, lanes] - weights[nz - 2, at, lanes] * scaled + rising
+            scaled = east_values[1, at, :] * scaled
+            sums[parity, 0, :, lanes] -= scaled
+            for k in range(1, nz):
+                sums[parity, k, :, lanes] -= weights[k - 1, at, lanes] * scaled
         return carry
 
-    lax.fori_loop(0, blocks, solve, 0)
-    even = [jnp.sum(acc[0, k], axis=0, keepdims=True) for k in range(nz)]
-    odd = [jnp.sum(acc[1, k], axis=0, keepdims=True) for k in range(nz)]
+    lax.fori_loop(0, blocks, share, 0)
+    even = [jnp.sum(sums[0, k], axis=0, keepdims=True) for k in range(nz)]
+    odd = [jnp.sum(sums[1, k], axis=0, keepdims=True) for k in range(nz)]
     west = jnp.concatenate([e + o for e, o in zip(even, odd)], 0)
     east_end = jnp.concatenate([e - o for e, o in zip(even, odd)], 0) + leaving
     width = ny // slabs
@@ -431,19 +464,19 @@
 
 def backward_kernel(
     nz, slabs, chunk,
-    modes, crown, solved,
-    obs, up, east, north,
-    from_west, side_east, f_below, low, low_above,
-    tables, east_table, east_values, lam_b,
-    out_east, out_north, out_up, out_p, out_r,
-    work, below, above, found, half, press, coming, p_below, p_above,
+    modes, weights, crown, solved,
+    fluid, up, east, north,
+    from_west, side_east, f_below, high, low, low_above,
+    tables, east_table, east_values,
+    far_east, far_north, far_up, far_p, far_r,
+    done, sems, work, below, above, found, half, press, coming, p_below, floor, leaving,
 ):
-    step = pl.program_id(0)
-    last = step == pl.num_programs(0) - 1
     ny = east.shape[1]
     hy = ny // 2
-    nx = chunk * pl.num_programs(0)
+    nx = modes.shape[1]
+    steps = nx // chunk
     size = chunk * nz
+    fields = (far_east, far_north, far_up, far_p, far_r)
     lift = jnp.where(lax.axis_index("gz") == 0, 1.0, 0.0).astype(F32)
 
     def north_back(value):
@@ -451,115 +484,123 @@
         odd = dot3(split(value[:, hy:]), north_pair(tables, 2))
         return even + odd, even - odd
 
-    @pl.when(step == 0)
-    def _():
-        width = ny // slabs
-        west, east_end = [], []
-        hx = nx // 2
-        for j in range(slabs):
-            lanes = slice(j * width, (j + 1) * width)
-            below[:hx, lanes] = solved[j, 0:hx, :width]
-            below[hx:, lanes] = solved[j, 0:hx, width:]
-            above[:hx, lanes] = solved[j, hx:nx, :width]
-            above[hx:, lanes] = solved[j, hx:nx, width:]
-            west.append(solved[j, nx : nx + nz, :width])
-            east_end.append(solved[j, nx : nx + nz, width:])
-        west = jnp.concatenate(west, 1)
-        east_end = jnp.concatenate(east_end, 1)
-        found[0] = west - east_end
-        found[1] = west + east_end
-        blocks = nx // 8
-
-        def solve(n, carry):
-            at = pl.ds(pl.multiple_of(n * 8, 8), 8)
-            parity = n // (blocks // 2)
-            for lane in range(0, ny, 128):
-                lanes = slice(lane, lane + 128)
-                shift = east_values[0, at, :] + lam_b[:, lanes]
-                weight = east_values[1, at, :]
-                right = []
-                for k in range(nz):
-                    q = jnp.broadcast_to(found[parity, pl.ds(k, 1), lanes], weight.shape)
-                    plane = modes[k, at, lanes] if k < nz - 1 else crown[at, lanes]
-                    right.append(plane + weight * q)
-                right[0] = right[0] + below[at, lanes]
-                right[nz - 1] = right[nz - 1] + above[at, lanes]
-                local = slab_solve(shift, right)
-                for k in range(nz):
-                    work[k, at, lanes] = local[k]
-            return carry
-
-        lax.fori_loop(0, blocks, solve, 0)
-        left = east_left(east_table[1])
-        for k in range(nz):
-            put_lanes(half, pl.ds(nz + k, nx, stride=nz), east_dot(left, work[k]), 0)
-        first, final = slice(nz, 2 * nz), slice(nx * nz, (nx + 1) * nz)
-        put_lanes(half, slice(0, nz), get_lanes(half, first) + west, 0)
-        put_lanes(half, slice((nx + 1) * nz, (nx + 2) * nz), get_lanes(half, final) - east_end, 0)
-        both = jnp.concatenate(
-            [east_dot(left, below[...]), east_dot(left, above[...]), get_lanes(half, slice(0, size + nz))], 0
-        )
-        both = jnp.concatenate(north_back(both), 1)
-        p_below[...] = both[:nx] - f_below[...] * low[1]
-        p_above[...] = both[nx : 2 * nx]
-        press[...] = both[2 * nx :]
-
-    base = step * chunk
+    width = ny // slabs
+    west, east_end = [], []
+    hx = nx // 2
+    for j in range(slabs):
+        lanes = slice(j * width, (j + 1) * width)
+        below[:hx, lanes] = solved[j, 0:hx, :width]
+        below[hx:, lanes] = solved[j, 0:hx, width:]
+        above[:hx, lanes] = solved[j, hx:nx, :width]
+        above[hx:, lanes] = solved[j, hx:nx, width:]
+        west.append(solved[j, nx : nx + nz, :width])
+        east_end.append(solved[j, nx : nx + nz, width:])
+    west = jnp.concatenate(west, 1)
+    east_end = jnp.concatenate(east_end, 1)
+    found[0] = west - east_end
+    found[1] = west + east_end
+    blocks = nx // 8
+
+    def solve(n, carry):
+        at = pl.ds(pl.multiple_of(n * 8, 8), 8)
+        parity = n // (blocks // 2)
+        for lane in range(0, ny, 128):
+            lanes = slice(lane, lane + 128)
+            weight = east_values[1, at, :]
+            right = []
+            for k in range(nz):
+                q = jnp.broadcast_to(found[parity, pl.ds(k, 1), lanes], weight.shape)
+                plane = modes[k, at, lanes] if k < nz - 1 else crown[at, lanes]
+                right.append(plane + weight * q)
+            right[0] = right[0] + below[at, lanes]
+            right[nz - 1] = right[nz - 1] + above[at, lanes]
+            local = slab_solve([weights[k, at, lanes] for k in range(nz)], right)
+            for k in range(nz):
+                work[k, at, lanes] = local[k]
+        return carry
+
+    lax.fori_loop(0, blocks, solve, 0)
+    left = east_left(east_table[1])
+    crest = None
+    for k in range(nz):
+        crest = east_dot(left, work[k])
+        put_lanes(half, pl.ds(nz + k, nx, stride=nz), crest, 0)
+    first, final = slice(nz, 2 * nz), slice(nx * nz, (nx + 1) * nz)
+    put_lanes(half, slice(0, nz), get_lanes(half, first) + west, 0)
+    put_lanes(half, slice((nx + 1) * nz, (nx + 2) * nz), get_lanes(half, final) - east_end, 0)
+    both = jnp.concatenate(
+        [east_dot(left, below[...]), east_dot(left, above[...]) - crest, get_lanes(half, slice(0, size + nz))], 0
+    )
+    both = jnp.concatenate(north_back(both), 1)
+    p_below[...] = both[:nx] - f_below[...] * low[1]
+    floor[...] = f_below[...] + lift
+    leaving[...] = high[...] * (low_above[1] - low_above[0] * both[nx : 2 * nx])
+    press[...] = both[2 * nx :]
+
 
     def cells(x):
         return pl.ds(pl.multiple_of(x * nz, nz), nz)
-
-    rows = pl.ds(pl.multiple_of((base + chunk + 1) * nz, nz), size)
-    coming[:, :hy], coming[:, hy:] = north_back(get_lanes(half, rows))
 
     lanes = from_west.shape[1]
     total = from_west.shape[0] - nz * (ny // lanes)
     side_west = jnp.concatenate(
         [from_west[total + n * nz : total + (n + 1) * nz, :] for n in range(ny // lanes)], 1
     )
-    here = fluid_of(obs[cells(base), :])
-    before = fluid_of(obs[cells(jnp.maximum(base - 1, 0)), :])
-    before = jnp.where(step == 0, side_west, before)
-    after_row = cells(jnp.minimum(base + chunk, nx - 1))
-    after_fluid = fluid_of(obs[after_row, :])
-    after_flux = jnp.where(last, side_east[nz:, :], after_fluid * east[after_row, :])
-    after_fluid = jnp.where(last, side_east[0:nz, :], after_fluid)
-
-    p = press[nz : 2 * nz, :]
-    first_flux = here * before * east[cells(base), :]
-    p_before = press[0:nz, :] - jnp.where(step == 0, 1.0, 0.0).astype(F32) * first_flux
-    east_done = first_flux - here * before * (p - p_before)
-    for i in range(chunk):
-        at = slice(i * nz, (i + 1) * nz)
-        own = cells(base + i)
-        line = pl.ds(base + i, 1)
-        if i < chunk - 1:
-            nxt = cells(base + i + 1)
-            after = fluid_of(obs[nxt, :])
-            flux = after * east[nxt, :]
-            p_next = press[(i + 2) * nz : (i + 3) * nz, :]
-        else:
-            after, flux = after_fluid, after_flux
-            p_next = coming[0:nz, :] + jnp.where(last, 1.0, 0.0).astype(F32) * (here * flux)
-        east_next_done = here * (flux - after * (p_next - p))
-        north_done = here * north_roll(here, 1) * (north[own, :] - (p - north_roll(p, 1)))
-        fluid_below = below_of(here, f_below[line, :] + lift)
-        up_done = here * fluid_below * (up[own, :] - (p - below_of(p, p_below[line, :])))
-        edge = here[nz - 1 : nz, :] * (
-            low_above[1, line, :] - low_above[0, line, :] * (p_above[line, :] - p[nz - 1 : nz, :])
-        )
-        out_east[at, :] = east_done
-        out_north[at, :] = north_done
-        out_up[at, :] = up_done
-        out_p[at, :] = p
-        out_r[at, :] = (
-            (east_done - east_next_done)
-            + (north_done - north_roll(north_done, -1))
-            + (up_done - above_of(up_done, edge))
-        )
-        here, p, east_done = after, p_next, east_next_done
-    press[0:nz, :] = press[size : size + nz, :]
-    press[nz:, :] = coming[...]
+
+    def advance(step, carry):
+        last = step == steps - 1
+        base = step * chunk
+
+        rows = pl.ds(pl.multiple_of((base + chunk + 1) * nz, nz), size)
+        coming[:, :hy], coming[:, hy:] = north_back(get_lanes(half, rows))
+
+        here = get_lanes(fluid, cells(base))
+        before = get_lanes(fluid, cells(jnp.maximum(base - 1, 0)))
+        before = jnp.where(step == 0, side_west, before)
+        after_row = cells(jnp.minimum(base + chunk, nx - 1))
+        after_fluid = get_lanes(fluid, after_row)
+        after_flux = jnp.where(last, side_east[nz:, :], after_fluid * east[after_row, :])
+        after_fluid = jnp.where(last, side_east[0:nz, :], after_fluid)
+
+        p = press[nz : 2 * nz, :]
+        first_flux = here * before * east[cells(base), :]
+        p_before = press[0:nz, :] - jnp.where(step == 0, 1.0, 0.0).astype(F32) * first_flux
+        east_done = first_flux - here * before * (p - p_before)
+        for i in range(chunk):
+            own = cells(base + i)
+            line = pl.ds(base + i, 1)
+            if i < chunk - 1:
+                nxt = cells(base + i + 1)
+                after = get_lanes(fluid, nxt)
+                flux = after * east[nxt, :]
+                p_next = press[(i + 2) * nz : (i + 3) * nz, :]
+            else:
+                after, flux = after_fluid, after_flux
+                p_next = coming[0:nz, :] + jnp.where(last, 1.0, 0.0).astype(F32) * (here * flux)
+            east_next_done = here * (flux - after * (p_next - p))
+            north_done = here * north_roll(here, 1) * (north[own, :] - (p - north_roll(p, 1)))
+            fluid_below = below_of(here, floor[line, :])
+            up_done = here * fluid_below * (get_lanes(up, own) - (p - below_of(p, p_below[line, :])))
+            done[0, own, :] = east_done
+            done[1, own, :] = north_done
+            done[2, own, :] = up_done
+            done[3, own, :] = p
+            done[4, own, :] = (
+                (east_done - east_next_done)
+                + (north_done - north_roll(north_done, -1))
+                + (up_done - above_of(up_done, leaving[line, :]))
+            )
+            here, p, east_done = after, p_next, east_next_done
+        press[0:nz, :] = press[size : size + nz, :]
+        press[nz:, :] = coming[...]
+        sent = pl.ds(pl.multiple_of(base * nz, size), size)
+        for n, field in enumerate(fields):
+            pltpu.make_async_copy(done.at[n, sent, :], field.at[sent, :], sems.at[n]).start()
+        return carry
+
+    lax.fori_loop(0, steps, advance, 0)
+    for n, field in enumerate(fields):
+        pltpu.make_async_copy(done.at[n], field, sems.at[n]).wait()
 
 
 def local(groups, slabs, east_velocity, north_velocity, upward_velocity, obstacle):
@@ -588,7 +629,6 @@
     ).astype(np.float32)
 
     chunk = 16
-    steps = nx // chunk
     lanes = ny // 128
     params = pltpu.CompilerParams(vmem_limit_bytes=VMEM_LIMIT)
     kept = pl.BlockSpec(memory_space=pltpu.VMEM)
@@ -618,11 +658,11 @@
     side_east = lax.ppermute(side, "xy", [((i + 1) % groups, i) for i in range(groups)])
 
     cells = nx * nz * ny
-    modes = pl.pallas_call(
+    modes, weights, bottom, top, folded = pl.pallas_call(
         functools.partial(interior_kernel, nz, chunk),
-        in_specs=[kept] * 6,
-        out_specs=kept,
-        out_shape=array(nz, nx, ny),
+        in_specs=[kept] * 8,
+        out_specs=[kept] * 5,
+        out_shape=[array(nz, nx, ny)] * 2 + [array(nx, ny)] * 2 + [array(2, nz, 8, ny)],
         scratch_shapes=[
             pltpu.VMEM((chunk * nz, ny), F32),
             pltpu.VMEM((chunk * nz, ny), F32),
@@ -631,11 +671,11 @@
         compiler_params=params,
         cost_estimate=pl.CostEstimate(flops=cells * 2 * 3 * (ny // 2 + nx), bytes_accessed=20 * cells, transcendentals=0),
         name="interior",
-    )(fluid, up, east, north, tables, east_table)
+    )(fluid, up, east, north, tables, east_table, east_values, lam_b)
     ends_shape = array(slabs, nx + nz, 2 * width)
     crown, ends = pl.pallas_call(
         functools.partial(joined_kernel, nz, slabs),
-        in_specs=[kept] * 9,
+        in_specs=[kept] * 12,
         out_specs=[kept] * 2,
         out_shape=[array(nx, ny), ends_shape],
         scratch_shapes=[
@@ -645,7 +685,7 @@
         ],
         compiler_params=params,
         name="joined",
-    )(modes, high, low_above, final, side_east, tables, east_table, east_values, lam_b)
+    )(modes, weights, bottom, top, folded, high, low_above, final, side_east, tables, east_table, east_values)
 
     ends = lax.all_to_all(ends, "gz", split_axis=0, concat_axis=0, tiled=True)
     own, own_more = pl.pallas_call(
@@ -661,8 +701,8 @@
     for shift in range(1, groups):
         sent = own_more if shift == groups - 1 else own
         found.append(lax.ppermute(sent, "xy", [((i + shift) % groups, i) for i in range(groups)]))
-    high, own = lax.optimization_barrier((high, own))
-    f_below = lax.ppermute(high, "gz", rising)
+    rising_flags, own = lax.optimization_barrier((high, own))
+    f_below = lax.ppermute(rising_flags, "gz", rising)
     f_below, found[0] = lax.optimization_barrier((f_below, found[0]))
     solved = pl.pallas_call(
         functools.partial(correct_kernel, nz, groups),
@@ -675,37 +715,39 @@
     )(ends, *found, pairs, part, sines)
     solved = lax.all_to_all(solved, "gz", split_axis=0, concat_axis=0, tiled=True)
 
-    big = pl.BlockSpec((chunk * nz, ny), lambda i: (i, 0))
     outs = pl.pallas_call(
-        functools.partial(backward_kernel, nz, slabs, chunk),
-        grid=(steps,),
-        in_specs=[kept] * 16,
-        out_specs=[big] * 5,
+        functools.partial(backward_kernel, nz, slabs, BACK_ROWS),
+        in_specs=[kept] * 17,
+        out_specs=[far] * 5,
         out_shape=[array(nx * nz, ny)] * 5,
         scratch_shapes=[
+            pltpu.VMEM((5, nx * nz, ny), F32),
+            pltpu.SemaphoreType.DMA((5,)),
             pltpu.VMEM((nz, nx, ny), F32),
             pltpu.VMEM((nx, ny), F32),
             pltpu.VMEM((nx, ny), F32),
             pltpu.VMEM((2, nz, ny), F32),
-            pltpu.VMEM((lanes, (nx + chunk + 1) * nz, 128), F32),
-            pltpu.VMEM(((chunk + 1) * nz, ny), F32),
-            pltpu.VMEM((chunk * nz, ny), F32),
+            pltpu.VMEM((lanes, (nx + BACK_ROWS + 1) * nz, 128), F32),
+            pltpu.VMEM(((BACK_ROWS + 1) * nz, ny), F32),
+            pltpu.VMEM((BACK_ROWS * nz, ny), F32),
+            pltpu.VMEM((nx, ny), F32),
             pltpu.VMEM((nx, ny), F32),
             pltpu.VMEM((nx, ny), F32),
         ],
-        compiler_params=params,
+        compiler_params=pltpu.CompilerParams(vmem_limit_bytes=BACK_LIMIT),
         name="backward",
-    )(modes, crown, solved, obs, up_in, east, north, found[-1], side_east, f_below, low, low_above,
-      tables, east_table, east_values, lam_b)
+    )(modes, weights, crown, solved, fluid, up, east, north, found[-1], side_east, f_below, high, low,
+      low_above, tables, east_table, east_values)
     return tuple(o.reshape(nx, nz, ny) for o in outs)
 
 
 def solution(mesh):
     placed = P("xy", "gz", None)
-    return jax.shard_map(
+    step = jax.shard_map(
         functools.partial(local, mesh.shape["xy"], mesh.shape["gz"]),
         mesh=mesh,
         in_specs=(placed,) * 4,
         out_specs=(placed,) * 5,
         check_vma=False,
     )
+    return step

time: 65.6 us -> 62.2 us (0.948)
  Pallas kernels: 20.2 us -> 18.1 us
  waiting for transfers between devices: 3.21 us -> 2.49 us
    pallas_call x1, Pallas kernels: 10.2 us -> 7.66 us  [local(): pl.pallas_call(functools.partial(backward_kernel, nz, slabs, BACK_ROWS),...]
    pallas_call x1, Pallas kernels: 3.62 us -> 4.71 us  [local(): pl.pallas_call(functools.partial(interior_kernel, nz, chunk), in_specs=[k...]
    ppermute x1, waiting for transfers between devices: 0.9 us -> 0.01 us  [local(): low_above = lax.ppermute(low, 'gz', falling)]
    pallas_call x1, Pallas kernels: 1.82 us -> 1.15 us  [local(): pl.pallas_call(functools.partial(joined_kernel, nz, slabs), in_specs=[kep...]
  transfers between devices with their start and end apart: 6 -> 6, of which waited for: 2 -> 1; matrix products, arithmetic and copies ran while one was open for 0% -> 0% of each run, Pallas kernels for 6% -> 8%
where the time goes in v5:
time: 62.2 us; the launch traced here: 61.3 us
  blocking collectives  26.1 us (42%)
  Pallas kernels  18.1 us (29%)
  starting transfers between devices  13.8 us (22%)
  waiting for transfers between devices  2.49 us (4%)
  between operations  0.82 us (1%)
    all_to_all x1, blocking collectives, local(): ends = lax.all_to_all(ends, 'gz', split_axis=0, concat_axis=0, tiled=True)  13.3 us
    all_to_all x1, blocking collectives, local(): lax.all_to_all(solved, 'gz', split_axis=0, concat_axis=0, tiled=True)  12.8 us
    pallas_call x1, Pallas kernels, local(): pl.pallas_call(functools.partial(backward_kernel, nz, slabs, BACK_ROWS),...  7.66 us
    ppermute x1, starting transfers between devices, local(): lax.ppermute(side, 'xy', [((i + 1) % groups, i) for i in range(groups)])  4.85 us
    pallas_call x1, Pallas kernels, local(): pl.pallas_call(functools.partial(interior_kernel, nz, chunk), in_specs=[k...  4.71 us
    ppermute x3, starting transfers between devices, local(): lax.ppermute(sent, 'xy', [((i + shift) % groups, i) for i in range(groups)])  4.21 us
    pallas_call x1, Pallas kernels, local(): pl.pallas_call(functools.partial(load_kernel, nz), in_specs=[far] * 3, ou...  2.68 us
    ppermute x1, starting transfers between devices, local(): f_below = lax.ppermute(rising_flags, 'gz', rising)  2.65 us
  transfers between devices with their start and end apart: 6, of which 1 were waited for; matrix products, arithmetic and copies ran while one was open for 0% of the time, Pallas kernels for 8%

profile of v5, /device:TPU:1, one launch (start us, length us, event | category | flops | bytes accessed | tf_op | source)
XLA Modules:
  0.0 61.3 jit_solution(12623328955843827356)
XLA Ops:
  0.6 0.0 copy-start
  0.6 0.0 copy-start.1
  0.7 0.0 copy-start.2
  0.7 0.0 copy-start.3
  0.7 0.0 copy-start.4
  0.7 0.0 copy-start.9
  0.7 2.7 %load.1 = (f32[4,1024,128]{2,1,0:T(8,128)S(1)}, f32[4,1024,128]{2,1,0:T(8,128)S(1)}, f32[128,512]{1,0:T(8,128)S(1)}, f32[2,128,512]{2,1,0:T(8,128)S(1)}, f32[16,512]{1,0:T(8,128)S(1)}, /*index=5*/f32[8,512]{1,0:T(8,128)S(1)}) custom-call(s32[1024,512]{1,0:T(8,128)} %bitcast.14, f32[1024,512]{1,0:T(8,128)} %bitcast.15, f32[1024,512]{1,0:T(8,128)} %bitcast.9), custom_call_target="tpu_custom_call" | custom-call | tf_op jit(solution)/shard_map/load/pallas_call | solution.py:641
  3.4 2.1 %collective-permute-start = (f32[2,128,512]{2,1,0:T(8,128)S(1)}, f32[2,128,512]{2,1,0:T(8,128)S(1)}, u32[]{:S(2)}, u32[]{:S(2)}) collective-permute-start(f32[2,128,512]{2,1,0:T(8,128)S(1)} %get-tuple-element.36.low), channel_id=1, source_target_pairs={{4,0},{8,4},{12,8},{16,12},{20,16},{24,20},{28,24},{5,1},{9,5},{13... | collective-permute-start | bytes 1572872 | tf_op jit(solution)/shard_map/ppermute | solution.py:657
  5.5 4.8 %collective-permute-start.1 = (f32[16,512]{1,0:T(8,128)S(1)}, f32[16,512]{1,0:T(8,128)S(1)}, u32[]{:S(2)}, u32[]{:S(2)}) collective-permute-start(f32[16,512]{1,0:T(8,128)S(1)} %get-tuple-element.38), channel_id=1, source_target_pairs={{1,0},{2,1},{3,2},{0,3},{5,4},{6,5},{7,6},{4,7},{9,8},{10,9},{11,1... | collective-permute-start | bytes 98312 | tf_op jit(solution)/shard_map/ppermute | solution.py:658
  10.3 0.0 copy-done
  10.3 0.0 copy-done.1
  10.3 0.0 copy-done.2
  10.3 0.0 copy-done.3
  10.3 0.0 copy-done.4
  10.3 0.0 copy-done.9
  10.3 4.7 %interior.1 = (f32[8,128,512]{2,1,0:T(8,128)S(1)}, f32[8,128,512]{2,1,0:T(8,128)S(1)}, f32[128,512]{1,0:T(8,128)S(1)}, f32[128,512]{1,0:T(8,128)S(1)}, f32[2,8,8,512]{3,2,1,0:T(8,128)S(1)}) custom-call(f32[4,1024,128]{2,1,0:T(8,128)S(1)} %get-tuple-element.28.fluid, f32[4,1024,128]{2,1,0:T(8,128)S(1)} %get-tuple-element.29.up, f32[1024,512]{1,0:T(8,128)S(1)} %bitcast.10, ...), custom_call_target="tpu_custom_call" | custom-call | flops 1207959552 | bytes 10485760 | tf_op jit(solution)/shard_map/interior/pallas_call | solution.py:661
  15.1 0.0 collective-permute-done.1.side_east
  15.1 0.0 collective-permute-done.low_above
  15.1 0.0 copy-start.5
  15.1 0.0 copy-start.6
  15.1 0.0 copy-start.7
  15.1 0.0 copy-start.8
  15.1 1.2 %joined.1 = (f32[128,512]{1,0:T(8,128)S(1)}, f32[8,136,128]{2,1,0:T(8,128)S(1)}) custom-call(f32[8,128,512]{2,1,0:T(8,128)S(1)} %get-tuple-element.30.modes, f32[8,128,512]{2,1,0:T(8,128)S(1)} %get-tuple-element.31.weights, f32[128,512]{1,0:T(8,128)S(1)} %get-tuple-element.32.bottom_in, f32[128,512]{1,0:T(8,128)S(1)} %get-tuple-element.33.top_in, ...), custom_call_target="tpu_custom_call" | custom-call | tf_op jit(solution)/shard_map/joined/pallas_call | solution.py:676
  16.3 13.3 %all_to_all.10.ends = f32[8,136,128]{2,1,0:T(8,128)S(1)} all-to-all(f32[8,136,128]{2,1,0:T(8,128)S(1)} %get-tuple-element.40), channel_id=1, replica_groups=mesh['gz'=8,'xy'=4] {'gz'}, dimensions={0} | all-to-all | bytes 1114112 | tf_op jit(solution)/shard_map/all_to_all | solution.py:690
  29.6 0.0 copy-done.5
  29.6 0.0 copy-done.6
  29.6 0.0 copy-done.7
  29.6 0.0 copy-done.8
  29.6 0.8 %ends.1 = (f32[64,128]{1,0:T(8,128)S(1)}, f32[96,128]{1,0:T(8,128)S(1)}) custom-call(f32[8,136,128]{2,1,0:T(8,128)S(1)} %all_to_all.10.ends, f32[8,512]{1,0:T(8,128)S(1)} %get-tuple-element.37.final, f32[192,128]{1,0:T(8,128)S(1)} %copy-done.5, f32[8,8,128]{2,1,0:T(8,128)S(1)} %copy-done.8, bf16[128,512]{1,0:T(8,128)(2,1)S(1)} %copy-done.6, ...), custom_call_target="tpu_custom_call" | custom-call | tf_op jit(solution)/shard_map/ends/pallas_call | solution.py:691
  30.4 2.7 %collective-permute-start.2 = (f32[128,512]{1,0:T(8,128)S(1)}, f32[128,512]{1,0:T(8,128)S(1)}, u32[]{:S(2)}, u32[]{:S(2)}) collective-permute-start(f32[128,512]{1,0:T(8,128)S(1)} %get-tuple-element.42.high), channel_id=1, source_target_pairs={{0,4},{4,8},{8,12},{12,16},{16,20},{20,24},{24,28},{1,5},{5,9},{9,... | collective-permute-start | bytes 786440 | tf_op jit(solution)/shard_map/ppermute | solution.py:705
  33.1 0.8 %collective-permute-start.5 = (f32[96,128]{1,0:T(8,128)S(1)}, f32[96,128]{1,0:T(8,128)S(1)}, u32[]{:S(2)}, u32[]{:S(2)}) collective-permute-start(f32[96,128]{1,0:T(8,128)S(1)} %get-tuple-element.44), channel_id=1, source_target_pairs={{3,0},{0,1},{1,2},{2,3},{7,4},{4,5},{5,6},{6,7},{11,8},{8,9},{9,10... | collective-permute-start | bytes 147464 | tf_op jit(solution)/shard_map/ppermute | solution.py:703
  33.9 2.3 %collective-permute-start.4 = (f32[64,128]{1,0:T(8,128)S(1)}, f32[64,128]{1,0:T(8,128)S(1)}, u32[]{:S(2)}, u32[]{:S(2)}) collective-permute-start(f32[64,128]{1,0:T(8,128)S(1)} %get-tuple-element.43.rest_0_), channel_id=1, source_target_pairs={{2,0},{3,1},{0,2},{1,3},{6,4},{7,5},{4,6},{5,7},{10,8},{11,9},{8,1... | collective-permute-start | bytes 98312 | tf_op jit(solution)/shard_map/ppermute | solution.py:703
  36.2 1.1 %collective-permute-start.3 = (f32[64,128]{1,0:T(8,128)S(1)}, f32[64,128]{1,0:T(8,128)S(1)}, u32[]{:S(2)}, u32[]{:S(2)}) collective-permute-start(f32[64,128]{1,0:T(8,128)S(1)} %get-tuple-element.43.rest_0_), channel_id=1, source_target_pairs={{1,0},{2,1},{3,2},{0,3},{5,4},{6,5},{7,6},{4,7},{9,8},{10,9},{11,1... | collective-permute-start | bytes 98312 | tf_op jit(solution)/shard_map/ppermute | solution.py:703
  37.3 0.0 collective-permute-done.2.f_below
  37.3 2.5 %collective-permute-done.4.rest_2_ = f32[64,128]{1,0:T(8,128)S(1)} collective-permute-done((f32[64,128]{1,0:T(8,128)S(1)}, f32[64,128]{1,0:T(8,128)S(1)}, u32[]{:S(2)}, u32[]{:S(2)}) %collective-permute-start.4) | collective-permute-done | bytes 32800 | tf_op jit(solution)/shard_map/ppermute | solution.py:703
  39.8 0.0 collective-permute-done.3.rest_1_
  39.8 0.0 collective-permute-done.5.rest_3_.from_west
  39.8 1.1 %correct.1 = f32[8,136,128]{2,1,0:T(8,128)S(1)} custom-call(f32[8,136,128]{2,1,0:T(8,128)S(1)} %all_to_all.10.ends, f32[64,128]{1,0:T(8,128)S(1)} %get-tuple-element.43.rest_0_, f32[64,128]{1,0:T(8,128)S(1)} %collective-permute-done.3.rest_1_, f32[64,128]{1,0:T(8,128)S(1)} %collective-permute-done.4.rest_2_, ...), custom_call_target="tpu_custom_call" | custom-call | tf_op jit(solution)/shard_map/correct/pallas_call | solution.py:707
  40.9 12.8 %all_to_all.11.solved = f32[8,136,128]{2,1,0:T(8,128)S(1)} all-to-all(f32[8,136,128]{2,1,0:T(8,128)S(1)} %correct.1), channel_id=1, replica_groups=mesh['gz'=8,'xy'=4] {'gz'}, dimensions={0} | all-to-all | bytes 1114112 | tf_op jit(solution)/shard_map/all_to_all | solution.py:716
  53.7 7.7 %backward.1 = (f32[1024,512]{1,0:T(8,128)}, f32[1024,512]{1,0:T(8,128)}, f32[1024,512]{1,0:T(8,128)}, f32[1024,512]{1,0:T(8,128)}, f32[1024,512]{1,0:T(8,128)}) custom-call(f32[8,128,512]{2,1,0:T(8,128)S(1)} %get-tuple-element.30.modes, f32[8,128,512]{2,1,0:T(8,128)S(1)} %get-tuple-element.31.weights, f32[128,512]{1,0:T(8,128)S(1)} %get-tuple-element.39.crown, ...), custom_call_target="tpu_custom_call" | custom-call | tf_op jit(solution)/shard_map/backward/pallas_call | solution.py:718
Async XLA Ops:
  0.6 9.7 %copy-start = (f32[128,8,512]{2,1,0:T(8,128)S(1)}, f32[128,8,512]{2,1,0:T(8,128)}, u32[]{:S(2)}) copy-start(f32[128,8,512]{2,1,0:T(8,128)} %param.12) | copy-start | bytes 6291460
  0.6 9.7 %copy-start.1 = (f32[128,8,512]{2,1,0:T(8,128)S(1)}, f32[128,8,512]{2,1,0:T(8,128)}, u32[]{:S(2)}) copy-start(f32[128,8,512]{2,1,0:T(8,128)} %param.13) | copy-start | bytes 6291460
  0.7 9.7 %copy-start.2 = (bf16[1536,256]{1,0:T(8,128)(2,1)S(1)}, bf16[1536,256]{1,0:T(8,128)(2,1)}, u32[]{:S(2)}) copy-start(bf16[1536,256]{1,0:T(8,128)(2,1)} %constant.16.clone.tables) | copy-start | bytes 2359300
  0.7 9.6 %copy-start.3 = (f32[2,128,128]{2,1,0:T(8,128)S(1)}, f32[2,128,128]{2,1,0:T(8,128)}, u32[]{:S(2)}) copy-start(f32[2,128,128]{2,1,0:T(8,128)} %constant.18.clone.east_values) | copy-start | bytes 393220
  0.7 9.6 %copy-start.4 = (bf16[2,128,256]{2,1,0:T(8,128)(2,1)S(1)}, bf16[2,128,256]{2,1,0:T(8,128)(2,1)}, u32[]{:S(2)}) copy-start(bf16[2,128,256]{2,1,0:T(8,128)(2,1)} %constant.17.clone.east_table) | copy-start | bytes 393220
  0.7 9.6 %copy-start.9 = (f32[8,512]{1,0:T(8,128)S(1)}, f32[8,512]{1,0:T(8,128)}, u32[]{:S(2)}) copy-start(f32[8,512]{1,0:T(8,128)} %constant.19.clone.lam_b) | copy-start | bytes 49156
  3.4 11.7 %collective-permute-start = (f32[2,128,512]{2,1,0:T(8,128)S(1)}, f32[2,128,512]{2,1,0:T(8,128)S(1)}, u32[]{:S(2)}, u32[]{:S(2)}) collective-permute-start(f32[2,128,512]{2,1,0:T(8,128)S(1)} %get-tuple-element.36.low), channel_id=1, source_target_pairs={{4,0},{8,4},{12,8},{16,12},{20,16},{24,20},{28,24},{5,1},{9,5},{13... | collective-permute-start | bytes 1572872 | tf_op jit(solution)/shard_map/ppermute | solution.py:657
  5.5 9.6 %collective-permute-start.1 = (f32[16,512]{1,0:T(8,128)S(1)}, f32[16,512]{1,0:T(8,128)S(1)}, u32[]{:S(2)}, u32[]{:S(2)}) collective-permute-start(f32[16,512]{1,0:T(8,128)S(1)} %get-tuple-element.38), channel_id=1, source_target_pairs={{1,0},{2,1},{3,2},{0,3},{5,4},{6,5},{7,6},{4,7},{9,8},{10,9},{11,1... | collective-permute-start | bytes 98312 | tf_op jit(solution)/shard_map/ppermute | solution.py:658
  15.1 14.5 %copy-start.5 = (f32[192,128]{1,0:T(8,128)S(1)}, f32[192,128]{1,0:T(8,128)}, u32[]{:S(2)}) copy-start(f32[192,128]{1,0:T(8,128)} %constant.20.clone.pairs.rest_4_) | copy-start | bytes 294916
  15.1 14.5 %copy-start.6 = (bf16[128,512]{1,0:T(8,128)(2,1)S(1)}, bf16[128,512]{1,0:T(8,128)(2,1)}, u32[]{:S(2)}) copy-start(bf16[128,512]{1,0:T(8,128)(2,1)} %constant.22.clone.sums) | copy-start | bytes 393220
  15.1 14.5 %copy-start.7 = (bf16[128,64]{1,0:T(8,128)(2,1)S(1)}, bf16[128,64]{1,0:T(8,128)(2,1)}, u32[]{:S(2)}) copy-start(bf16[128,64]{1,0:T(8,128)(2,1)} %constant.23.clone.sines.rest_6_) | copy-start | bytes 49156
  15.1 14.5 %copy-start.8 = (f32[8,8,128]{2,1,0:T(8,128)S(1)}, f32[8,8,128]{2,1,0:T(8,128)}, u32[]{:S(2)}) copy-start(f32[8,8,128]{2,1,0:T(8,128)} %constant.21.clone.lam_b.rest_5_) | copy-start | bytes 98308
  30.4 6.9 %collective-permute-start.2 = (f32[128,512]{1,0:T(8,128)S(1)}, f32[128,512]{1,0:T(8,128)S(1)}, u32[]{:S(2)}, u32[]{:S(2)}) collective-permute-start(f32[128,512]{1,0:T(8,128)S(1)} %get-tuple-element.42.high), channel_id=1, source_target_pairs={{0,4},{4,8},{8,12},{12,16},{16,20},{20,24},{24,28},{1,5},{5,9},{9,... | collective-permute-start | bytes 786440 | tf_op jit(solution)/shard_map/ppermute | solution.py:705
  33.1 6.7 %collective-permute-start.5 = (f32[96,128]{1,0:T(8,128)S(1)}, f32[96,128]{1,0:T(8,128)S(1)}, u32[]{:S(2)}, u32[]{:S(2)}) collective-permute-start(f32[96,128]{1,0:T(8,128)S(1)} %get-tuple-element.44), channel_id=1, source_target_pairs={{3,0},{0,1},{1,2},{2,3},{7,4},{4,5},{5,6},{6,7},{11,8},{8,9},{9,10... | collective-permute-start | bytes 147464 | tf_op jit(solution)/shard_map/ppermute | solution.py:703
  33.9 5.9 %collective-permute-start.4 = (f32[64,128]{1,0:T(8,128)S(1)}, f32[64,128]{1,0:T(8,128)S(1)}, u32[]{:S(2)}, u32[]{:S(2)}) collective-permute-start(f32[64,128]{1,0:T(8,128)S(1)} %get-tuple-element.43.rest_0_), channel_id=1, source_target_pairs={{2,0},{3,1},{0,2},{1,3},{6,4},{7,5},{4,6},{5,7},{10,8},{11,9},{8,1... | collective-permute-start | bytes 98312 | tf_op jit(solution)/shard_map/ppermute | solution.py:703
  36.2 3.6 %collective-permute-start.3 = (f32[64,128]{1,0:T(8,128)S(1)}, f32[64,128]{1,0:T(8,128)S(1)}, u32[]{:S(2)}, u32[]{:S(2)}) collective-permute-start(f32[64,128]{1,0:T(8,128)S(1)} %get-tuple-element.43.rest_0_), channel_id=1, source_target_pairs={{1,0},{2,1},{3,2},{0,3},{5,4},{6,5},{7,6},{4,7},{9,8},{10,9},{11,1... | collective-permute-start | bytes 98312 | tf_op jit(solution)/shard_map/ppermute | solution.py:703

commit v6 on v5

--- a/solution.py
+++ b/solution.py
@@ -8,6 +8,7 @@
 from jax.experimental import pallas as pl
 from jax.experimental.pallas import tpu as pltpu
 from jax.sharding import PartitionSpec as P
+
 
 F32 = jnp.float32
 BF16 = jnp.bfloat16
@@ -603,7 +604,11 @@
         pltpu.make_async_copy(done.at[n], field, sems.at[n]).wait()
 
 
-def local(groups, slabs, east_velocity, north_velocity, upward_velocity, obstacle):
+def local(groups, slabs, *fields):
+    return project(groups, slabs, *fields)
+
+
+def project(groups, slabs, east_velocity, north_velocity, upward_velocity, obstacle):
     nx, nz, ny = east_velocity.shape
     total = slabs * nz
     width = ny // slabs
@@ -656,6 +661,7 @@
     falling = [(i + 1, i) for i in range(slabs - 1)]
     low_above = lax.ppermute(low, "gz", falling)
     side_east = lax.ppermute(side, "xy", [((i + 1) % groups, i) for i in range(groups)])
+    f_below = lax.ppermute(high, "gz", rising)
 
     cells = nx * nz * ny
     modes, weights, bottom, top, folded = pl.pallas_call(
@@ -701,8 +707,6 @@
     for shift in range(1, groups):
         sent = own_more if shift == groups - 1 else own
         found.append(lax.ppermute(sent, "xy", [((i + shift) % groups, i) for i in range(groups)]))
-    rising_flags, own = lax.optimization_barrier((high, own))
-    f_below = lax.ppermute(rising_flags, "gz", rising)
     f_below, found[0] = lax.optimization_barrier((f_below, found[0]))
     solved = pl.pallas_call(
         functools.partial(correct_kernel, nz, groups),
@@ -743,11 +747,10 @@
 
 def solution(mesh):
     placed = P("xy", "gz", None)
-    step = jax.shard_map(
+    return jax.shard_map(
         functools.partial(local, mesh.shape["xy"], mesh.shape["gz"]),
         mesh=mesh,
         in_specs=(placed,) * 4,
         out_specs=(placed,) * 5,
         check_vma=False,
     )
-    return step

time: 62.2 us -> 74.7 us (1.20)
  local copies, waits for them, and re-layouts: 0.06 us -> 13.9 us
  blocking collectives: 26.1 us -> 16.5 us
  starting transfers between devices: 13.8 us -> 17.8 us
  waiting for transfers between devices: 2.49 us -> 5.26 us
  Pallas kernels: 18.1 us -> 19 us
    unnamed x20 -> x66, local copies, waits for them, and re-layouts: 0.06 us -> 13.9 us
    all_to_all x2 -> x1, blocking collectives: 26.1 us -> 16.5 us  [project(): lax.all_to_all(solved, 'gz', split_axis=0, concat_axis=0, tiled=True)]
    all_to_all x0 -> x1, starting transfers between devices: none -> 4.01 us  [project(): ends = lax.all_to_all(ends, 'gz', split_axis=0, concat_axis=0, tiled=True)]
    all_to_all x0 -> x1, waiting for transfers between devices: none -> 3.43 us  [project(): ends = lax.all_to_all(ends, 'gz', split_axis=0, concat_axis=0, tiled=True)]
    pallas_call x6, Pallas kernels: 18.1 us -> 19 us  [the longest x1 8.62 us: project(): pl.pallas_call(functools.partial(backward_kernel, nz, slabs, BACK_ROWS),...]
  transfers between devices with their start and end apart: 6 -> 7, of which waited for: 1 -> 3; matrix products, arithmetic and copies ran while one was open for 0% -> 0% of each run, Pallas kernels for 8% -> 8%
where the time goes in v6:
time: 74.7 us; the launch traced here: 73.4 us
  Pallas kernels  19 us (25%)
  starting transfers between devices  17.8 us (24%)
  blocking collectives  16.5 us (22%)
  local copies, waits for them, and re-layouts  13.9 us (19%)
  waiting for transfers between devices  5.26 us (7%)
  between operations  0.96 us (1%)
    all_to_all x1, blocking collectives, project(): lax.all_to_all(solved, 'gz', split_axis=0, concat_axis=0, tiled=True)  16.5 us
    unnamed x66, local copies, waits for them, and re-layouts  13.9 us
    pallas_call x1, Pallas kernels, project(): pl.pallas_call(functools.partial(backward_kernel, nz, slabs, BACK_ROWS),...  8.62 us
    ppermute x1, starting transfers between devices, project(): lax.ppermute(side, 'xy', [((i + 1) % groups, i) for i in range(groups)])  4.85 us
    pallas_call x1, Pallas kernels, project(): pl.pallas_call(functools.partial(interior_kernel, nz, chunk), in_specs=[k...  4.7 us
    all_to_all x1, starting transfers between devices, project(): ends = lax.all_to_all(ends, 'gz', split_axis=0, concat_axis=0, tiled=True)  4.01 us
    ppermute x1, starting transfers between devices, project(): f_below = lax.ppermute(high, 'gz', rising)  3.53 us
    all_to_all x1, waiting for transfers between devices, project(): ends = lax.all_to_all(ends, 'gz', split_axis=0, concat_axis=0, tiled=True)  3.43 us
  transfers between devices with their start and end apart: 7, of which 3 were waited for; matrix products, arithmetic and copies ran while one was open for 0% of the time, Pallas kernels for 8%

profile of v6, /device:TPU:1, one launch (start us, length us, event | category | flops | bytes accessed | tf_op | source)
XLA Modules:
  0.0 73.4 jit_solution(16615265213913219888)
XLA Ops:
  0.6 0.0 copy-start.5
  0.7 0.0 copy-start.11
  0.7 0.0 copy-start.14
  0.7 0.0 copy-start.16
  0.7 0.0 copy-start.32
  0.7 2.7 %load.1 = (f32[4,1024,128]{2,1,0:T(8,128)S(1)}, f32[4,1024,128]{2,1,0:T(8,128)S(1)}, f32[128,512]{1,0:T(8,128)S(1)}, f32[2,128,512]{2,1,0:T(8,128)S(1)}, f32[16,512]{1,0:T(8,128)S(1)}, /*index=5*/f32[8,512]{1,0:T(8,128)S(1)}) custom-call(s32[1024,512]{1,0:T(8,128)} %bitcast.14, f32[1024,512]{1,0:T(8,128)} %bitcast.15, f32[1024,512]{1,0:T(8,128)} %bitcast.9), custom_call_target="tpu_custom_call" | custom-call | tf_op jit(solution)/shard_map/load/pallas_call | solution.py:646
  3.4 0.0 copy-start.7
  3.4 0.0 copy-start.9
  3.4 2.1 %collective-permute-start = (f32[2,128,512]{2,1,0:T(8,128)S(1)}, f32[2,128,512]{2,1,0:T(8,128)S(1)}, u32[]{:S(2)}, u32[]{:S(2)}) collective-permute-start(f32[2,128,512]{2,1,0:T(8,128)S(1)} %get-tuple-element.35.low), channel_id=1, source_target_pairs={{4,0},{8,4},{12,8},{16,12},{20,16},{24,20},{28,24},{5,1},{9,5},{13... | collective-permute-start | bytes 1572872 | tf_op jit(solution)/shard_map/ppermute | solution.py:662
  5.5 4.8 %collective-permute-start.1 = (f32[16,512]{1,0:T(8,128)S(1)}, f32[16,512]{1,0:T(8,128)S(1)}, u32[]{:S(2)}, u32[]{:S(2)}) collective-permute-start(f32[16,512]{1,0:T(8,128)S(1)} %get-tuple-element.37), channel_id=1, source_target_pairs={{1,0},{2,1},{3,2},{0,3},{5,4},{6,5},{7,6},{4,7},{9,8},{10,9},{11,1... | collective-permute-start | bytes 98312 | tf_op jit(solution)/shard_map/ppermute | solution.py:663
  10.4 0.0 copy-done.11
  10.4 4.7 %interior.1 = (f32[8,128,512]{2,1,0:T(8,128)S(1)}, f32[8,128,512]{2,1,0:T(8,128)S(1)}, f32[128,512]{1,0:T(8,128)S(1)}, f32[128,512]{1,0:T(8,128)S(1)}, f32[2,8,8,512]{3,2,1,0:T(8,128)S(1)}) custom-call(f32[4,1024,128]{2,1,0:T(8,128)S(1)} %get-tuple-element.27.fluid, f32[4,1024,128]{2,1,0:T(8,128)S(1)} %get-tuple-element.28.up, f32[1024,512]{1,0:T(8,128)S(1)} %bitcast.10, ...), custom_call_target="tpu_custom_call" | custom-call | flops 1207959552 | bytes 10485760 | tf_op jit(solution)/shard_map/interior/pallas_call | solution.py:667
  15.1 0.0 copy-start.1
  15.1 0.0 copy-start.3
  15.1 0.0 collective-permute-done.1.side_east
  15.2 0.0 collective-permute-done.low_above
  15.2 0.0 copy-start.23
  15.2 1.2 %joined.1 = (f32[128,512]{1,0:T(8,128)S(1)}, f32[8,136,128]{2,1,0:T(8,128)S(1)}) custom-call(f32[8,128,512]{2,1,0:T(8,128)S(1)} %get-tuple-element.29.modes, f32[8,128,512]{2,1,0:T(8,128)S(1)} %get-tuple-element.30.weights, f32[128,512]{1,0:T(8,128)S(1)} %get-tuple-element.31.bottom_in, f32[128,512]{1,0:T(8,128)S(1)} %get-tuple-element.32.top_in, ...), custom_call_target="tpu_custom_call" | custom-call | tf_op jit(solution)/shard_map/joined/pallas_call | solution.py:682
  16.4 0.1 copy-done.1
  16.4 0.7 copy-done.3
  17.1 0.2 copy-done.12
  17.3 0.8 %copy-done.20 = f32[8,136,128]{2,1,0:T(8,128)} copy-done((f32[8,136,128]{2,1,0:T(8,128)}, f32[8,136,128]{2,1,0:T(8,128)S(1)}, u32[]{:S(2)}) %copy-start.20) | copy-done | bytes 557080
  18.2 0.7 copy-done.24
  18.8 4.0 %all-to-all-start = ((f32[8,136,128]{2,1,0:T(8,128)}), f32[8,136,128]{2,1,0:T(8,128)S(1)}, u32[]{:S(2)}, u32[]{:S(2)}) async-start(f32[8,136,128]{2,1,0:T(8,128)} %copy-done.20), calls=%async_computation | async-start | bytes 1114112 | tf_op jit(solution)/shard_map/all_to_all | solution.py:696
  22.9 3.5 %collective-permute-start.2 = (f32[128,512]{1,0:T(8,128)}, f32[128,512]{1,0:T(8,128)}, u32[]{:S(2)}, u32[]{:S(2)}) collective-permute-start(f32[128,512]{1,0:T(8,128)} %copy-done.18), channel_id=1, source_target_pairs={{0,4},{4,8},{8,12},{12,16},{16,20},{20,24},{24,28},{1,5},{5,9},{9,... | collective-permute-start | bytes 786440 | tf_op jit(solution)/shard_map/ppermute | solution.py:664
  26.4 3.4 %all-to-all-done.ends = f32[8,136,128]{2,1,0:T(8,128)S(1)} async-done(((f32[8,136,128]{2,1,0:T(8,128)}), f32[8,136,128]{2,1,0:T(8,128)S(1)}, u32[]{:S(2)}, u32[]{:S(2)}) %all-to-all-start) | async-done | bytes 557088 | tf_op jit(solution)/shard_map/all_to_all | solution.py:696
  29.8 0.9 %copy-done.28 = bf16[128,512]{1,0:T(8,128)(2,1)S(1)} copy-done((bf16[128,512]{1,0:T(8,128)(2,1)S(1)}, bf16[128,512]{1,0:T(8,128)(2,1)}, u32[]{:S(2)}) %copy-start.28) | copy-done | bytes 131096
  30.7 0.8 %copy-done.29 = bf16[128,64]{1,0:T(8,128)(2,1)S(1)} copy-done((bf16[128,64]{1,0:T(8,128)(2,1)S(1)}, bf16[128,64]{1,0:T(8,128)(2,1)}, u32[]{:S(2)}) %copy-start.29) | copy-done | bytes 16408
  31.5 0.8 %copy-done.30 = f32[8,8,128]{2,1,0:T(8,128)S(1)} copy-done((f32[8,8,128]{2,1,0:T(8,128)S(1)}, f32[8,8,128]{2,1,0:T(8,128)}, u32[]{:S(2)}) %copy-start.30) | copy-done | bytes 32792
  32.3 0.8 %ends.1 = (f32[64,128]{1,0:T(8,128)S(1)}, f32[96,128]{1,0:T(8,128)S(1)}) custom-call(f32[8,136,128]{2,1,0:T(8,128)S(1)} %all-to-all-done.ends, f32[8,512]{1,0:T(8,128)S(1)} %get-tuple-element.36.final, f32[192,128]{1,0:T(8,128)S(1)} %copy-done.23, f32[8,8,128]{2,1,0:T(8,128)S(1)} %copy-done.30, bf16[128,512]{1,0:T(8,128)(2,1)S(1)} %copy-done.28, ...), custom_call_target="tpu_custom_call" | custom-call | tf_op jit(solution)/shard_map/ends/pallas_call | solution.py:697
  33.1 0.1 collective-permute-start.5
  33.2 2.1 %collective-permute-start.4 = (f32[64,128]{1,0:T(8,128)S(1)}, f32[64,128]{1,0:T(8,128)S(1)}, u32[]{:S(2)}, u32[]{:S(2)}) collective-permute-start(f32[64,128]{1,0:T(8,128)S(1)} %get-tuple-element.41.rest_0_), channel_id=1, source_target_pairs={{2,0},{3,1},{0,2},{1,3},{6,4},{7,5},{4,6},{5,7},{10,8},{11,9},{8,1... | collective-permute-start | bytes 98312 | tf_op jit(solution)/shard_map/ppermute | solution.py:709
  35.3 1.1 %collective-permute-start.3 = (f32[64,128]{1,0:T(8,128)S(1)}, f32[64,128]{1,0:T(8,128)S(1)}, u32[]{:S(2)}, u32[]{:S(2)}) collective-permute-start(f32[64,128]{1,0:T(8,128)S(1)} %get-tuple-element.41.rest_0_), channel_id=1, source_target_pairs={{1,0},{2,1},{3,2},{0,3},{5,4},{6,5},{7,6},{4,7},{9,8},{10,9},{11,1... | collective-permute-start | bytes 98312 | tf_op jit(solution)/shard_map/ppermute | solution.py:709
  36.4 0.0 collective-permute-done.2.f_below
  36.4 0.5 collective-permute-done.4.rest_2_
  36.9 1.3 %collective-permute-done.3.rest_1_ = f32[64,128]{1,0:T(8,128)S(1)} collective-permute-done((f32[64,128]{1,0:T(8,128)S(1)}, f32[64,128]{1,0:T(8,128)S(1)}, u32[]{:S(2)}, u32[]{:S(2)}) %collective-permute-start.3) | collective-permute-done | bytes 32800 | tf_op jit(solution)/shard_map/ppermute | solution.py:709
  38.2 0.0 collective-permute-done.5.rest_3_.from_west
  38.3 0.8 %copy-done.31 = f32[8,8,128]{2,1,0:T(8,128)S(1)} copy-done((f32[8,8,128]{2,1,0:T(8,128)S(1)}, f32[8,8,128]{2,1,0:T(8,128)}, u32[]{:S(2)}) %copy-start.31) | copy-done | bytes 32792
  39.0 1.1 %correct.1 = f32[8,136,128]{2,1,0:T(8,128)S(1)} custom-call(f32[8,136,128]{2,1,0:T(8,128)S(1)} %all-to-all-done.ends, f32[64,128]{1,0:T(8,128)S(1)} %get-tuple-element.41.rest_0_, f32[64,128]{1,0:T(8,128)S(1)} %collective-permute-done.3.rest_1_, f32[64,128]{1,0:T(8,128)S(1)} %collective-permute-done.4.rest_2_, ...), custom_call_target="tpu_custom_call" | custom-call | tf_op jit(solution)/shard_map/correct/pallas_call | solution.py:711
  40.1 16.5 %all_to_all.10.solved = f32[8,136,128]{2,1,0:T(8,128)S(1)} all-to-all(f32[8,136,128]{2,1,0:T(8,128)S(1)} %correct.1), channel_id=1, replica_groups=mesh['gz'=8,'xy'=4] {'gz'}, dimensions={0} | all-to-all | bytes 1114112 | tf_op jit(solution)/shard_map/all_to_all | solution.py:720
  56.6 0.0 copy-start.4
  56.6 1.6 %copy-done.4 = f32[8,128,512]{2,1,0:T(8,128)S(1)} copy-done((f32[8,128,512]{2,1,0:T(8,128)S(1)}, f32[8,128,512]{2,1,0:T(8,128)}, u32[]{:S(2)}) %copy-start.4) | copy-done | bytes 2097176
  58.2 1.6 %copy-done.6 = f32[128,8,512]{2,1,0:T(8,128)S(1)} copy-done((f32[128,8,512]{2,1,0:T(8,128)S(1)}, f32[128,8,512]{2,1,0:T(8,128)}, u32[]{:S(2)}) %copy-start.6) | copy-done | bytes 2097176
  59.8 1.6 %copy-done.8 = f32[4,1024,128]{2,1,0:T(8,128)S(1)} copy-done((f32[4,1024,128]{2,1,0:T(8,128)S(1)}, f32[4,1024,128]{2,1,0:T(8,128)}, u32[]{:S(2)}) %copy-start.8) | copy-done | bytes 2097176
  61.4 1.6 %copy-done.10 = f32[4,1024,128]{2,1,0:T(8,128)S(1)} copy-done((f32[4,1024,128]{2,1,0:T(8,128)S(1)}, f32[4,1024,128]{2,1,0:T(8,128)}, u32[]{:S(2)}) %copy-start.10) | copy-done | bytes 2097176
  63.0 1.0 %copy-done.22 = f32[2,128,512]{2,1,0:T(8,128)S(1)} copy-done((f32[2,128,512]{2,1,0:T(8,128)S(1)}, f32[2,128,512]{2,1,0:T(8,128)}, u32[]{:S(2)}) %copy-start.22) | copy-done | bytes 524312
  64.0 0.8 %copy-done.27 = f32[16,512]{1,0:T(8,128)S(1)} copy-done((f32[16,512]{1,0:T(8,128)S(1)}, f32[16,512]{1,0:T(8,128)}, u32[]{:S(2)}) %copy-start.27) | copy-done | bytes 32792
  64.8 8.6 %backward.1 = (f32[1024,512]{1,0:T(8,128)}, f32[1024,512]{1,0:T(8,128)}, f32[1024,512]{1,0:T(8,128)}, f32[1024,512]{1,0:T(8,128)}, f32[1024,512]{1,0:T(8,128)}) custom-call(f32[8,128,512]{2,1,0:T(8,128)S(1)} %copy-done.2, f32[8,128,512]{2,1,0:T(8,128)S(1)} %copy-done.4, f32[128,512]{1,0:T(8,128)S(1)} %copy-done.25, f32[8,136,128]{2,1,0:T(8,128)S(1)} %all_to_all.10.solved, ...), custom_call_target="tpu_custom_call" | custom-call | tf_op jit(solution)/shard_map/backward/pallas_call | solution.py:722
  (39 shorter events, 0.1 us)
Async XLA Ops:
  0.6 9.7 %copy-start = (f32[128,8,512]{2,1,0:T(8,128)S(1)}, f32[128,8,512]{2,1,0:T(8,128)}, u32[]{:S(2)}) copy-start(f32[128,8,512]{2,1,0:T(8,128)} %param.12) | copy-start | bytes 6291460
  0.6 9.7 %copy-start.5 = (f32[128,8,512]{2,1,0:T(8,128)S(1)}, f32[128,8,512]{2,1,0:T(8,128)}, u32[]{:S(2)}) copy-start(f32[128,8,512]{2,1,0:T(8,128)} %param.13) | copy-start | bytes 6291460
  0.7 9.7 %copy-start.11 = (bf16[1536,256]{1,0:T(8,128)(2,1)S(1)}, bf16[1536,256]{1,0:T(8,128)(2,1)}, u32[]{:S(2)}) copy-start(bf16[1536,256]{1,0:T(8,128)(2,1)} %constant.16.clone.tables) | copy-start | bytes 2359300
  0.7 9.7 %copy-start.14 = (f32[2,128,128]{2,1,0:T(8,128)S(1)}, f32[2,128,128]{2,1,0:T(8,128)}, u32[]{:S(2)}) copy-start(f32[2,128,128]{2,1,0:T(8,128)} %constant.18.clone.east_values) | copy-start | bytes 393220
  0.7 9.7 %copy-start.16 = (bf16[2,128,256]{2,1,0:T(8,128)(2,1)S(1)}, bf16[2,128,256]{2,1,0:T(8,128)(2,1)}, u32[]{:S(2)}) copy-start(bf16[2,128,256]{2,1,0:T(8,128)(2,1)} %constant.17.clone.east_table) | copy-start | bytes 393220
  0.7 9.7 %copy-start.32 = (f32[8,512]{1,0:T(8,128)S(1)}, f32[8,512]{1,0:T(8,128)}, u32[]{:S(2)}) copy-start(f32[8,512]{1,0:T(8,128)} %constant.19.clone.lam_b) | copy-start | bytes 49156
  3.4 11.7 %copy-start.7 = (f32[4,1024,128]{2,1,0:T(8,128)}, f32[4,1024,128]{2,1,0:T(8,128)S(1)}, u32[]{:S(2)}) copy-start(f32[4,1024,128]{2,1,0:T(8,128)S(1)} %get-tuple-element.27.fluid) | copy-start | bytes 6291460
  3.4 11.7 %copy-start.9 = (f32[4,1024,128]{2,1,0:T(8,128)}, f32[4,1024,128]{2,1,0:T(8,128)S(1)}, u32[]{:S(2)}) copy-start(f32[4,1024,128]{2,1,0:T(8,128)S(1)} %get-tuple-element.28.up) | copy-start | bytes 6291460
  3.4 11.7 %copy-start.21 = (f32[2,128,512]{2,1,0:T(8,128)}, f32[2,128,512]{2,1,0:T(8,128)S(1)}, u32[]{:S(2)}) copy-start(f32[2,128,512]{2,1,0:T(8,128)S(1)} %get-tuple-element.35.low) | copy-start | bytes 1572868
  3.4 12.9 %copy-start.18 = (f32[128,512]{1,0:T(8,128)}, f32[128,512]{1,0:T(8,128)S(1)}, u32[]{:S(2)}) copy-start(f32[128,512]{1,0:T(8,128)S(1)} %get-tuple-element.34.high) | copy-start | bytes 786436
  3.4 11.7 %collective-permute-start = (f32[2,128,512]{2,1,0:T(8,128)S(1)}, f32[2,128,512]{2,1,0:T(8,128)S(1)}, u32[]{:S(2)}, u32[]{:S(2)}) collective-permute-start(f32[2,128,512]{2,1,0:T(8,128)S(1)} %get-tuple-element.35.low), channel_id=1, source_target_pairs={{4,0},{8,4},{12,8},{16,12},{20,16},{24,20},{28,24},{5,1},{9,5},{13... | collective-permute-start | bytes 1572872 | tf_op jit(solution)/shard_map/ppermute | solution.py:662
  5.5 9.6 %collective-permute-start.1 = (f32[16,512]{1,0:T(8,128)S(1)}, f32[16,512]{1,0:T(8,128)S(1)}, u32[]{:S(2)}, u32[]{:S(2)}) collective-permute-start(f32[16,512]{1,0:T(8,128)S(1)} %get-tuple-element.37), channel_id=1, source_target_pairs={{1,0},{2,1},{3,2},{0,3},{5,4},{6,5},{7,6},{4,7},{9,8},{10,9},{11,1... | collective-permute-start | bytes 98312 | tf_op jit(solution)/shard_map/ppermute | solution.py:663
  15.1 1.3 %copy-start.1 = (f32[8,128,512]{2,1,0:T(8,128)}, f32[8,128,512]{2,1,0:T(8,128)S(1)}, u32[]{:S(2)}) copy-start(f32[8,128,512]{2,1,0:T(8,128)S(1)} %get-tuple-element.29.modes) | copy-start | bytes 6291460
  15.1 2.0 %copy-start.3 = (f32[8,128,512]{2,1,0:T(8,128)}, f32[8,128,512]{2,1,0:T(8,128)S(1)}, u32[]{:S(2)}) copy-start(f32[8,128,512]{2,1,0:T(8,128)S(1)} %get-tuple-element.30.weights) | copy-start | bytes 6291460
  15.2 2.0 %copy-start.26 = (f32[16,512]{1,0:T(8,128)}, f32[16,512]{1,0:T(8,128)S(1)}, u32[]{:S(2)}) copy-start(f32[16,512]{1,0:T(8,128)S(1)} %collective-permute-done.1.side_east) | copy-start | bytes 98308
  15.2 2.2 %copy-start.12 = (f32[2,128,512]{2,1,0:T(8,128)}, f32[2,128,512]{2,1,0:T(8,128)S(1)}, u32[]{:S(2)}) copy-start(f32[2,128,512]{2,1,0:T(8,128)S(1)} %collective-permute-done.low_above) | copy-start | bytes 1572868
  15.2 14.6 %copy-start.23 = (f32[192,128]{1,0:T(8,128)S(1)}, f32[192,128]{1,0:T(8,128)}, u32[]{:S(2)}) copy-start(f32[192,128]{1,0:T(8,128)} %constant.20.clone.pairs.rest_4_) | copy-start | bytes 294916
  17.3 0.8 %copy-start.20 = (f32[8,136,128]{2,1,0:T(8,128)}, f32[8,136,128]{2,1,0:T(8,128)S(1)}, u32[]{:S(2)}) copy-start(f32[8,136,128]{2,1,0:T(8,128)S(1)} %get-tuple-element.39) | copy-start | bytes 1671172
  18.1 0.7 copy-start.24
  18.8 11.0 %all-to-all-start = ((f32[8,136,128]{2,1,0:T(8,128)}), f32[8,136,128]{2,1,0:T(8,128)S(1)}, u32[]{:S(2)}, u32[]{:S(2)}) async-start(f32[8,136,128]{2,1,0:T(8,128)} %copy-done.20), calls=%async_computation | async-start | bytes 1114112 | tf_op jit(solution)/shard_map/all_to_all | solution.py:696
  22.9 13.6 %collective-permute-start.2 = (f32[128,512]{1,0:T(8,128)}, f32[128,512]{1,0:T(8,128)}, u32[]{:S(2)}, u32[]{:S(2)}) collective-permute-start(f32[128,512]{1,0:T(8,128)} %copy-done.18), channel_id=1, source_target_pairs={{0,4},{4,8},{8,12},{12,16},{16,20},{20,24},{24,28},{1,5},{5,9},{9,... | collective-permute-start | bytes 786440 | tf_op jit(solution)/shard_map/ppermute | solution.py:664
  29.8 0.9 %copy-start.28 = (bf16[128,512]{1,0:T(8,128)(2,1)S(1)}, bf16[128,512]{1,0:T(8,128)(2,1)}, u32[]{:S(2)}) copy-start(bf16[128,512]{1,0:T(8,128)(2,1)} %constant.22.clone.sums) | copy-start | bytes 393220
  30.7 0.8 %copy-start.29 = (bf16[128,64]{1,0:T(8,128)(2,1)S(1)}, bf16[128,64]{1,0:T(8,128)(2,1)}, u32[]{:S(2)}) copy-start(bf16[128,64]{1,0:T(8,128)(2,1)} %constant.23.clone.sines.rest_6_) | copy-start | bytes 49156
  31.5 0.8 %copy-start.30 = (f32[8,8,128]{2,1,0:T(8,128)S(1)}, f32[8,8,128]{2,1,0:T(8,128)}, u32[]{:S(2)}) copy-start(f32[8,8,128]{2,1,0:T(8,128)} %constant.21.clone.lam_b.rest_5_) | copy-start | bytes 98308
  32.3 24.3 %copy-start.2 = (f32[8,128,512]{2,1,0:T(8,128)S(1)}, f32[8,128,512]{2,1,0:T(8,128)}, u32[]{:S(2)}) copy-start(f32[8,128,512]{2,1,0:T(8,128)} %copy-done.1) | copy-start | bytes 6291460
  32.3 24.3 %copy-start.13 = (f32[2,128,512]{2,1,0:T(8,128)S(1)}, f32[2,128,512]{2,1,0:T(8,128)}, u32[]{:S(2)}) copy-start(f32[2,128,512]{2,1,0:T(8,128)} %copy-done.12) | copy-start | bytes 1572868
  32.3 24.3 %copy-start.15 = (f32[2,128,128]{2,1,0:T(8,128)S(1)}, f32[2,128,128]{2,1,0:T(8,128)}, u32[]{:S(2)}) copy-start(f32[2,128,128]{2,1,0:T(8,128)} %constant.18.clone.east_values) | copy-start | bytes 393220
  32.3 24.3 %copy-start.17 = (bf16[2,128,256]{2,1,0:T(8,128)(2,1)S(1)}, bf16[2,128,256]{2,1,0:T(8,128)(2,1)}, u32[]{:S(2)}) copy-start(bf16[2,128,256]{2,1,0:T(8,128)(2,1)} %constant.17.clone.east_table) | copy-start | bytes 393220
  32.3 24.3 %copy-start.19 = (f32[128,512]{1,0:T(8,128)S(1)}, f32[128,512]{1,0:T(8,128)}, u32[]{:S(2)}) copy-start(f32[128,512]{1,0:T(8,128)} %copy-done.18) | copy-start | bytes 786436
  32.3 24.3 %copy-start.25 = (f32[128,512]{1,0:T(8,128)S(1)}, f32[128,512]{1,0:T(8,128)}, u32[]{:S(2)}) copy-start(f32[128,512]{1,0:T(8,128)} %copy-done.24) | copy-start | bytes 786436
  33.1 5.1 %collective-permute-start.5 = (f32[96,128]{1,0:T(8,128)S(1)}, f32[96,128]{1,0:T(8,128)S(1)}, u32[]{:S(2)}, u32[]{:S(2)}) collective-permute-start(f32[96,128]{1,0:T(8,128)S(1)} %get-tuple-element.42), channel_id=1, source_target_pairs={{3,0},{0,1},{1,2},{2,3},{7,4},{4,5},{5,6},{6,7},{11,8},{8,9},{9,10... | collective-permute-start | bytes 147464 | tf_op jit(solution)/shard_map/ppermute | solution.py:709
  33.2 3.7 %collective-permute-start.4 = (f32[64,128]{1,0:T(8,128)S(1)}, f32[64,128]{1,0:T(8,128)S(1)}, u32[]{:S(2)}, u32[]{:S(2)}) collective-permute-start(f32[64,128]{1,0:T(8,128)S(1)} %get-tuple-element.41.rest_0_), channel_id=1, source_target_pairs={{2,0},{3,1},{0,2},{1,3},{6,4},{7,5},{4,6},{5,7},{10,8},{11,9},{8,1... | collective-permute-start | bytes 98312 | tf_op jit(solution)/shard_map/ppermute | solution.py:709
  35.3 3.0 %collective-permute-start.3 = (f32[64,128]{1,0:T(8,128)S(1)}, f32[64,128]{1,0:T(8,128)S(1)}, u32[]{:S(2)}, u32[]{:S(2)}) collective-permute-start(f32[64,128]{1,0:T(8,128)S(1)} %get-tuple-element.41.rest_0_), channel_id=1, source_target_pairs={{1,0},{2,1},{3,2},{0,3},{5,4},{6,5},{7,6},{4,7},{9,8},{10,9},{11,1... | collective-permute-start | bytes 98312 | tf_op jit(solution)/shard_map/ppermute | solution.py:709
  38.2 0.8 %copy-start.31 = (f32[8,8,128]{2,1,0:T(8,128)S(1)}, f32[8,8,128]{2,1,0:T(8,128)}, u32[]{:S(2)}) copy-start(f32[8,8,128]{2,1,0:T(8,128)} %constant.21.clone.lam_b.rest_5_) | copy-start | bytes 98308
  56.6 1.6 %copy-start.4 = (f32[8,128,512]{2,1,0:T(8,128)S(1)}, f32[8,128,512]{2,1,0:T(8,128)}, u32[]{:S(2)}) copy-start(f32[8,128,512]{2,1,0:T(8,128)} %copy-done.3) | copy-start | bytes 6291460
  58.2 1.6 %copy-start.6 = (f32[128,8,512]{2,1,0:T(8,128)S(1)}, f32[128,8,512]{2,1,0:T(8,128)}, u32[]{:S(2)}) copy-start(f32[128,8,512]{2,1,0:T(8,128)} %param.13) | copy-start | bytes 6291460
  59.8 1.6 %copy-start.8 = (f32[4,1024,128]{2,1,0:T(8,128)S(1)}, f32[4,1024,128]{2,1,0:T(8,128)}, u32[]{:S(2)}) copy-start(f32[4,1024,128]{2,1,0:T(8,128)} %copy-done.7) | copy-start | bytes 6291460
  61.4 1.6 %copy-start.10 = (f32[4,1024,128]{2,1,0:T(8,128)S(1)}, f32[4,1024,128]{2,1,0:T(8,128)}, u32[]{:S(2)}) copy-start(f32[4,1024,128]{2,1,0:T(8,128)} %copy-done.9) | copy-start | bytes 6291460
  63.0 1.0 %copy-start.22 = (f32[2,128,512]{2,1,0:T(8,128)S(1)}, f32[2,128,512]{2,1,0:T(8,128)}, u32[]{:S(2)}) copy-start(f32[2,128,512]{2,1,0:T(8,128)} %copy-done.21) | copy-start | bytes 1572868
  64.0 0.8 %copy-start.27 = (f32[16,512]{1,0:T(8,128)S(1)}, f32[16,512]{1,0:T(8,128)}, u32[]{:S(2)}) copy-start(f32[16,512]{1,0:T(8,128)} %copy-done.26) | copy-start | bytes 98308

commit v7 on v6

--- a/solution.py
+++ b/solution.py
@@ -15,7 +15,7 @@
 VMEM_LIMIT = 24 * 1024 * 1024
 BACK_ROWS = 8
 BACK_LIMIT = 28 * 1024 * 1024
-LOAD_LIMIT = 48 * 1024 * 1024
+LOAD_LIMIT = 46 * 1024 * 1024
 
 
 def pair_np(table):
@@ -147,7 +147,9 @@
         ref[start + n, rows, :] = value[:, n * 128 : (n + 1) * 128]
 
 
-def load_kernel(nz, obs, up_in, east, fluid, up, high, low, side, final, raw, line, sems):
+def load_kernel(
+    nz, obs, up_in, east, fluid, up, high, low, side, final, weights, raw, line, sems
+):
     parts = raw.shape[0]
     rows = high.shape[0]
     copies = []
@@ -163,6 +165,29 @@
             copy.start()
     edge = pltpu.make_async_copy(east.at[0:nz, :], line, sems.at[2 * parts])
     edge.start()
+
+    def eigen(axis, start, half, step):
+        place = lax.broadcasted_iota(jnp.int32, (8, 128), axis) + start
+        mode = jnp.where(place < half, 2 * place, 2 * (place - half) + 1)
+        if axis == 1:
+            mode = jnp.minimum(mode, 2 * half - mode)
+        wave = jnp.sin(mode.astype(F32) * step)
+        return 4.0 * wave * wave
+
+    ny = parts * 128
+    north_eigen = [eigen(1, lane, ny // 2, float(np.pi / ny)) for lane in range(0, ny, 128)]
+
+    def coefficients(n, carry):
+        at = pl.ds(pl.multiple_of(n * 8, 8), 8)
+        east_eigen = eigen(0, n * 8, rows // 2, float(np.pi / (2 * rows)))
+        for lane in range(0, ny, 128):
+            lanes = slice(lane, lane + 128)
+            values = slab_weights(east_eigen + north_eigen[lane // 128], nz)
+            for k in range(nz):
+                weights[k, at, lanes] = values[k]
+        return carry
+
+    lax.fori_loop(0, rows // 8, coefficients, 0)
     edge.wait()
     for n, (flags, speed) in enumerate(copies):
         lanes = slice(n * 128, (n + 1) * 128)
@@ -222,8 +247,8 @@
 
 
 def interior_kernel(
-    nz, chunk, fluid, up, east, north, tables, east_table, east_values, lam_b,
-    modes, weights, bottom, top, sums,
+    nz, chunk, fluid, up, east, north, weights, tables, east_table, east_values,
+    modes, bottom, top, sums,
     src, ready, half,
 ):
     ny = src.shape[1]
@@ -266,16 +291,15 @@
         put_lanes(half, rows, even, 0)
         put_lanes(half, rows, odd, ny // 256)
 
-    stencil(0)
-    ready[...] = src[...]
+    ready[...] = jnp.zeros_like(ready)
 
     def body(step, carry):
-        transform(step - 1)
+        transform(jnp.maximum(step - 1, 0))
         stencil(step)
         ready[...] = src[...]
         return carry
 
-    lax.fori_loop(1, count, body, 0)
+    lax.fori_loop(0, count, body, 0)
     transform(count - 1)
     left = east_left(east_table[0])
     for k in range(nz):
@@ -289,9 +313,7 @@
         parity = n // (blocks // 2)
         for lane in range(0, ny, 128):
             lanes = slice(lane, lane + 128)
-            values = slab_weights(east_values[0, at, :] + lam_b[:, lanes], nz)
-            for k in range(nz):
-                weights[k, at, lanes] = values[k]
+            values = [weights[k, at, lanes] for k in range(nz)]
             local = slab_solve(values, [modes[k, at, lanes] for k in range(nz)])
             bottom[at, lanes] = local[0]
             top[at, lanes] = local[nz - 1]
@@ -623,7 +645,6 @@
     sines = np.concatenate(pair_np(sine_np), 0)
     sums = np.repeat(sines, 8, axis=1)
     east_values = np.stack([np.repeat(v[:, None], 128, 1) for v in (lam_a_np, block_np[:, 0])]).astype(np.float32)
-    lam_b = np.repeat(lam_b_np[None], 8, 0).astype(np.float32)
     part = np.tile(lam_b_np.reshape(slabs, 1, width), (1, 8, 2)).astype(np.float32)
 
     def paired(column):
@@ -643,11 +664,11 @@
         return jax.ShapeDtypeStruct(shape, F32)
 
     blocked = array(lanes, nx * nz, 128)
-    fluid, up, high, low, side, final = pl.pallas_call(
+    fluid, up, high, low, side, final, weights = pl.pallas_call(
         functools.partial(load_kernel, nz),
         in_specs=[far] * 3,
-        out_specs=[kept] * 6,
-        out_shape=[blocked, blocked, array(nx, ny), array(2, nx, ny), array(2 * nz, ny), array(nz, ny)],
+        out_specs=[kept] * 7,
+        out_shape=[blocked, blocked, array(nx, ny), array(2, nx, ny), array(2 * nz, ny), array(nz, ny), array(nz, nx, ny)],
         scratch_shapes=[
             pltpu.VMEM((lanes, nx * nz, 128), jnp.int32),
             pltpu.VMEM((nz, ny), F32),
@@ -664,11 +685,11 @@
     f_below = lax.ppermute(high, "gz", rising)
 
     cells = nx * nz * ny
-    modes, weights, bottom, top, folded = pl.pallas_call(
+    modes, bottom, top, folded = pl.pallas_call(
         functools.partial(interior_kernel, nz, chunk),
         in_specs=[kept] * 8,
-        out_specs=[kept] * 5,
-        out_shape=[array(nz, nx, ny)] * 2 + [array(nx, ny)] * 2 + [array(2, nz, 8, ny)],
+        out_specs=[kept] * 4,
+        out_shape=[array(nz, nx, ny)] + [array(nx, ny)] * 2 + [array(2, nz, 8, ny)],
         scratch_shapes=[
             pltpu.VMEM((chunk * nz, ny), F32),
             pltpu.VMEM((chunk * nz, ny), F32),
@@ -677,7 +698,7 @@
         compiler_params=params,
         cost_estimate=pl.CostEstimate(flops=cells * 2 * 3 * (ny // 2 + nx), bytes_accessed=20 * cells, transcendentals=0),
         name="interior",
-    )(fluid, up, east, north, tables, east_table, east_values, lam_b)
+    )(fluid, up, east, north, weights, tables, east_table, east_values)
     ends_shape = array(slabs, nx + nz, 2 * width)
     crown, ends = pl.pallas_call(
         functools.partial(joined_kernel, nz, slabs),

time: 74.7 us -> 75.5 us (1.011)
    ppermute x3, starting transfers between devices: 3.31 us -> 4.11 us  [project(): lax.ppermute(sent, 'xy', [((i + shift) % groups, i) for i in range(groups)])]
  transfers between devices with their start and end apart: 7 -> 7, of which waited for: 3 -> 3; matrix products, arithmetic and copies ran while one was open for 0% -> 0% of each run, Pallas kernels for 8% -> 7%
where the time goes in v7:
time: 75.5 us; the launch traced here: 74.2 us
  Pallas kernels  18.9 us (25%)
  starting transfers between devices  18.5 us (25%)
  blocking collectives  16.7 us (22%)
  local copies, waits for them, and re-layouts  14 us (19%)
  waiting for transfers between devices  5.13 us (7%)
  between operations  0.94 us (1%)
    all_to_all x1, blocking collectives, project(): lax.all_to_all(solved, 'gz', split_axis=0, concat_axis=0, tiled=True)  16.7 us
    unnamed x66, local copies, waits for them, and re-layouts  14 us
    pallas_call x1, Pallas kernels, project(): pl.pallas_call(functools.partial(backward_kernel, nz, slabs, BACK_ROWS),...  8.62 us
    ppermute x1, starting transfers between devices, project(): lax.ppermute(side, 'xy', [((i + 1) % groups, i) for i in range(groups)])  4.85 us
    pallas_call x1, Pallas kernels, project(): pl.pallas_call(functools.partial(interior_kernel, nz, chunk), in_specs=[k...  4.54 us
    ppermute x3, starting transfers between devices, project(): lax.ppermute(sent, 'xy', [((i + shift) % groups, i) for i in range(groups)])  4.11 us
    all_to_all x1, starting transfers between devices, project(): ends = lax.all_to_all(ends, 'gz', split_axis=0, concat_axis=0, tiled=True)  4 us
    ppermute x1, starting transfers between devices, project(): f_below = lax.ppermute(high, 'gz', rising)  3.53 us
  transfers between devices with their start and end apart: 7, of which 3 were waited for; matrix products, arithmetic and copies ran while one was open for 0% of the time, Pallas kernels for 7%

profile of v7, /device:TPU:1, one launch (start us, length us, event | category | flops | bytes accessed | tf_op | source)
XLA Modules:
  0.0 74.2 jit_solution(6294266567801695896)
XLA Ops:
  0.6 0.0 copy-start.5
  0.7 0.0 copy-start.11
  0.7 0.0 copy-start.14
  0.7 0.0 copy-start.16
  0.7 2.7 %load.1 = (f32[4,1024,128]{2,1,0:T(8,128)S(1)}, f32[4,1024,128]{2,1,0:T(8,128)S(1)}, f32[128,512]{1,0:T(8,128)S(1)}, f32[2,128,512]{2,1,0:T(8,128)S(1)}, f32[16,...) custom-call(s32[1024,512]{1,0:T(8,128)} %bitcast.14, f32[1024,512]{1,0:T(8,128)} %bitcast.15, ...), custom_call_target="tpu_custom_call" | custom-call | tf_op jit(solution)/shard_map/load/pallas_call | solution.py:667
  3.4 0.0 copy-start.7
  3.4 0.0 copy-start.9
  3.4 0.0 copy-start.21
  3.4 0.0 copy-start.1
  3.4 2.1 %collective-permute-start = (f32[2,128,512]{2,1,0:T(8,128)S(1)}, f32[2,128,512]{2,1,0:T(8,128)S(1)}, u32[]{:S(2)}, u32[]{:S(2)}) collective-permute-start(f32[2,128,512]{2,1,0:T(8,128)S(1)} %get-tuple-element.35.low), channel_id=1, source_target_pairs={{4,0},{8,4},{12,8},{16,12},{20,16},{24,20},{28,24},{5,1},{9,5},{13... | collective-permute-start | bytes 1572872 | tf_op jit(solution)/shard_map/ppermute | solution.py:683
  5.5 4.8 %collective-permute-start.1 = (f32[16,512]{1,0:T(8,128)S(1)}, f32[16,512]{1,0:T(8,128)S(1)}, u32[]{:S(2)}, u32[]{:S(2)}) collective-permute-start(f32[16,512]{1,0:T(8,128)S(1)} %get-tuple-element.37), channel_id=1, source_target_pairs={{1,0},{2,1},{3,2},{0,3},{5,4},{6,5},{7,6},{4,7},{9,8},{10,9},{11,1... | collective-permute-start | bytes 98312 | tf_op jit(solution)/shard_map/ppermute | solution.py:684
  10.4 0.0 copy-done.11
  10.4 4.5 %interior.1 = (f32[8,128,512]{2,1,0:T(8,128)S(1)}, f32[128,512]{1,0:T(8,128)S(1)}, f32[128,512]{1,0:T(8,128)S(1)}, f32[2,8,8,512]{3,2,1,0:T(8,128)S(1)}) custom-call(f32[4,1024,128]{2,1,0:T(8,128)S(1)} %get-tuple-element.27.fluid, f32[4,1024,128]{2,1,0:T(8,128)S(1)} %get-tuple-element.28.up, f32[1024,512]{1,0:T(8,128)S(1)} %bitcast.10, ...), custom_call_target="tpu_custom_call" | custom-call | flops 1207959552 | bytes 10485760 | tf_op jit(solution)/shard_map/interior/pallas_call | solution.py:688
  15.0 0.0 copy-start.3
  15.0 0.0 collective-permute-done.1.side_east
  15.0 0.0 collective-permute-done.low_above
  15.0 0.0 copy-start.23
  15.0 1.2 %joined.1 = (f32[128,512]{1,0:T(8,128)S(1)}, f32[8,136,128]{2,1,0:T(8,128)S(1)}) custom-call(f32[8,128,512]{2,1,0:T(8,128)S(1)} %get-tuple-element.30.modes, f32[8,128,512]{2,1,0:T(8,128)S(1)} %get-tuple-element.29.weights, f32[128,512]{1,0:T(8,128)S(1)} %get-tuple-element.31.bottom_in, f32[128,512]{1,0:T(8,128)S(1)} %get-tuple-element.32.top_in, ...), custom_call_target="tpu_custom_call" | custom-call | tf_op jit(solution)/shard_map/joined/pallas_call | solution.py:703
  16.2 0.1 copy-done.3
  16.3 0.2 copy-done.12
  16.5 0.8 %copy-done.20 = f32[8,136,128]{2,1,0:T(8,128)} copy-done((f32[8,136,128]{2,1,0:T(8,128)}, f32[8,136,128]{2,1,0:T(8,128)S(1)}, u32[]{:S(2)}) %copy-start.20) | copy-done | bytes 557080
  17.3 0.7 copy-done.24
  18.0 4.0 %all-to-all-start = ((f32[8,136,128]{2,1,0:T(8,128)}), f32[8,136,128]{2,1,0:T(8,128)S(1)}, u32[]{:S(2)}, u32[]{:S(2)}) async-start(f32[8,136,128]{2,1,0:T(8,128)} %copy-done.20), calls=%async_computation | async-start | bytes 1114112 | tf_op jit(solution)/shard_map/all_to_all | solution.py:717
  22.0 3.5 %collective-permute-start.2 = (f32[128,512]{1,0:T(8,128)}, f32[128,512]{1,0:T(8,128)}, u32[]{:S(2)}, u32[]{:S(2)}) collective-permute-start(f32[128,512]{1,0:T(8,128)} %copy-done.18), channel_id=1, source_target_pairs={{0,4},{4,8},{8,12},{12,16},{16,20},{20,24},{24,28},{1,5},{5,9},{9,... | collective-permute-start | bytes 786440 | tf_op jit(solution)/shard_map/ppermute | solution.py:685
  25.5 3.4 %all-to-all-done.ends = f32[8,136,128]{2,1,0:T(8,128)S(1)} async-done(((f32[8,136,128]{2,1,0:T(8,128)}), f32[8,136,128]{2,1,0:T(8,128)S(1)}, u32[]{:S(2)}, u32[]{:S(2)}) %all-to-all-start) | async-done | bytes 557088 | tf_op jit(solution)/shard_map/all_to_all | solution.py:717
  29.0 0.9 %copy-done.28 = bf16[128,512]{1,0:T(8,128)(2,1)S(1)} copy-done((bf16[128,512]{1,0:T(8,128)(2,1)S(1)}, bf16[128,512]{1,0:T(8,128)(2,1)}, u32[]{:S(2)}) %copy-start.28) | copy-done | bytes 131096
  29.9 0.8 %copy-done.29 = bf16[128,64]{1,0:T(8,128)(2,1)S(1)} copy-done((bf16[128,64]{1,0:T(8,128)(2,1)S(1)}, bf16[128,64]{1,0:T(8,128)(2,1)}, u32[]{:S(2)}) %copy-start.29) | copy-done | bytes 16408
  30.6 0.8 %copy-done.31 = f32[8,8,128]{2,1,0:T(8,128)S(1)} copy-done((f32[8,8,128]{2,1,0:T(8,128)S(1)}, f32[8,8,128]{2,1,0:T(8,128)}, u32[]{:S(2)}) %copy-start.31) | copy-done | bytes 32792
  31.4 0.8 %ends.1 = (f32[64,128]{1,0:T(8,128)S(1)}, f32[96,128]{1,0:T(8,128)S(1)}) custom-call(f32[8,136,128]{2,1,0:T(8,128)S(1)} %all-to-all-done.ends, f32[8,512]{1,0:T(8,128)S(1)} %get-tuple-element.36.final, f32[192,128]{1,0:T(8,128)S(1)} %copy-done.23, f32[8,8,128]{2,1,0:T(8,128)S(1)} %copy-done.31, bf16[128,512]{1,0:T(8,128)(2,1)S(1)} %copy-done.28, ...), custom_call_target="tpu_custom_call" | custom-call | tf_op jit(solution)/shard_map/ends/pallas_call | solution.py:718
  32.2 0.7 collective-permute-start.5
  33.0 2.3 %collective-permute-start.4 = (f32[64,128]{1,0:T(8,128)S(1)}, f32[64,128]{1,0:T(8,128)S(1)}, u32[]{:S(2)}, u32[]{:S(2)}) collective-permute-start(f32[64,128]{1,0:T(8,128)S(1)} %get-tuple-element.41.rest_0_), channel_id=1, source_target_pairs={{2,0},{3,1},{0,2},{1,3},{6,4},{7,5},{4,6},{5,7},{10,8},{11,9},{8,1... | collective-permute-start | bytes 98312 | tf_op jit(solution)/shard_map/ppermute | solution.py:730
  35.3 1.1 %collective-permute-start.3 = (f32[64,128]{1,0:T(8,128)S(1)}, f32[64,128]{1,0:T(8,128)S(1)}, u32[]{:S(2)}, u32[]{:S(2)}) collective-permute-start(f32[64,128]{1,0:T(8,128)S(1)} %get-tuple-element.41.rest_0_), channel_id=1, source_target_pairs={{1,0},{2,1},{3,2},{0,3},{5,4},{6,5},{7,6},{4,7},{9,8},{10,9},{11,1... | collective-permute-start | bytes 98312 | tf_op jit(solution)/shard_map/ppermute | solution.py:730
  36.3 0.0 collective-permute-done.2.f_below
  36.3 0.8 %collective-permute-done.4.rest_2_ = f32[64,128]{1,0:T(8,128)S(1)} collective-permute-done((f32[64,128]{1,0:T(8,128)S(1)}, f32[64,128]{1,0:T(8,128)S(1)}, u32[]{:S(2)}, u32[]{:S(2)}) %collective-permute-start.4) | collective-permute-done | bytes 32800 | tf_op jit(solution)/shard_map/ppermute | solution.py:730
  37.2 0.9 %collective-permute-done.3.rest_1_ = f32[64,128]{1,0:T(8,128)S(1)} collective-permute-done((f32[64,128]{1,0:T(8,128)S(1)}, f32[64,128]{1,0:T(8,128)S(1)}, u32[]{:S(2)}, u32[]{:S(2)}) %collective-permute-start.3) | collective-permute-done | bytes 32800 | tf_op jit(solution)/shard_map/ppermute | solution.py:730
  38.0 0.0 collective-permute-done.5.rest_3_.from_west
  38.0 0.8 %copy-done.30 = bf16[128,64]{1,0:T(8,128)(2,1)S(1)} copy-done((bf16[128,64]{1,0:T(8,128)(2,1)S(1)}, bf16[128,64]{1,0:T(8,128)(2,1)}, u32[]{:S(2)}) %copy-start.30) | copy-done | bytes 16408
  38.8 0.8 %copy-done.32 = f32[8,8,128]{2,1,0:T(8,128)S(1)} copy-done((f32[8,8,128]{2,1,0:T(8,128)S(1)}, f32[8,8,128]{2,1,0:T(8,128)}, u32[]{:S(2)}) %copy-start.32) | copy-done | bytes 32792
  39.6 1.1 %correct.1 = f32[8,136,128]{2,1,0:T(8,128)S(1)} custom-call(f32[8,136,128]{2,1,0:T(8,128)S(1)} %all-to-all-done.ends, f32[64,128]{1,0:T(8,128)S(1)} %get-tuple-element.41.rest_0_, f32[64,128]{1,0:T(8,128)S(1)} %collective-permute-done.3.rest_1_, f32[64,128]{1,0:T(8,128)S(1)} %collective-permute-done.4.rest_2_, ...), custom_call_target="tpu_custom_call" | custom-call | tf_op jit(solution)/shard_map/correct/pallas_call | solution.py:732
  40.6 16.7 %all_to_all.10.solved = f32[8,136,128]{2,1,0:T(8,128)S(1)} all-to-all(f32[8,136,128]{2,1,0:T(8,128)S(1)} %correct.1), channel_id=1, replica_groups=mesh['gz'=8,'xy'=4] {'gz'}, dimensions={0} | all-to-all | bytes 1114112 | tf_op jit(solution)/shard_map/all_to_all | solution.py:741
  57.4 0.0 copy-start.4
  57.4 1.6 %copy-done.4 = f32[8,128,512]{2,1,0:T(8,128)S(1)} copy-done((f32[8,128,512]{2,1,0:T(8,128)S(1)}, f32[8,128,512]{2,1,0:T(8,128)}, u32[]{:S(2)}) %copy-start.4) | copy-done | bytes 2097176
  59.0 1.6 %copy-done.6 = f32[128,8,512]{2,1,0:T(8,128)S(1)} copy-done((f32[128,8,512]{2,1,0:T(8,128)S(1)}, f32[128,8,512]{2,1,0:T(8,128)}, u32[]{:S(2)}) %copy-start.6) | copy-done | bytes 2097176
  60.5 1.6 %copy-done.8 = f32[4,1024,128]{2,1,0:T(8,128)S(1)} copy-done((f32[4,1024,128]{2,1,0:T(8,128)S(1)}, f32[4,1024,128]{2,1,0:T(8,128)}, u32[]{:S(2)}) %copy-start.8) | copy-done | bytes 2097176
  62.1 1.6 %copy-done.10 = f32[4,1024,128]{2,1,0:T(8,128)S(1)} copy-done((f32[4,1024,128]{2,1,0:T(8,128)S(1)}, f32[4,1024,128]{2,1,0:T(8,128)}, u32[]{:S(2)}) %copy-start.10) | copy-done | bytes 2097176
  63.7 1.0 %copy-done.22 = f32[2,128,512]{2,1,0:T(8,128)S(1)} copy-done((f32[2,128,512]{2,1,0:T(8,128)S(1)}, f32[2,128,512]{2,1,0:T(8,128)}, u32[]{:S(2)}) %copy-start.22) | copy-done | bytes 524312
  64.8 0.8 %copy-done.27 = f32[16,512]{1,0:T(8,128)S(1)} copy-done((f32[16,512]{1,0:T(8,128)S(1)}, f32[16,512]{1,0:T(8,128)}, u32[]{:S(2)}) %copy-start.27) | copy-done | bytes 32792
  65.5 8.6 %backward.1 = (f32[1024,512]{1,0:T(8,128)}, f32[1024,512]{1,0:T(8,128)}, f32[1024,512]{1,0:T(8,128)}, f32[1024,512]{1,0:T(8,128)}, f32[1024,512]{1,0:T(8,128)}) custom-call(f32[8,128,512]{2,1,0:T(8,128)S(1)} %copy-done.4, f32[8,128,512]{2,1,0:T(8,128)S(1)} %copy-done.2, f32[128,512]{1,0:T(8,128)S(1)} %copy-done.25, f32[8,136,128]{2,1,0:T(8,128)S(1)} %all_to_all.10.solved, ...), custom_call_target="tpu_custom_call" | custom-call | tf_op jit(solution)/shard_map/backward/pallas_call | solution.py:743
  (39 shorter events, 0.1 us)
Async XLA Ops:
  0.6 9.7 %copy-start = (f32[128,8,512]{2,1,0:T(8,128)S(1)}, f32[128,8,512]{2,1,0:T(8,128)}, u32[]{:S(2)}) copy-start(f32[128,8,512]{2,1,0:T(8,128)} %param.11) | copy-start | bytes 6291460
  0.6 9.7 %copy-start.5 = (f32[128,8,512]{2,1,0:T(8,128)S(1)}, f32[128,8,512]{2,1,0:T(8,128)}, u32[]{:S(2)}) copy-start(f32[128,8,512]{2,1,0:T(8,128)} %param.12) | copy-start | bytes 6291460
  0.7 9.7 %copy-start.11 = (bf16[1536,256]{1,0:T(8,128)(2,1)S(1)}, bf16[1536,256]{1,0:T(8,128)(2,1)}, u32[]{:S(2)}) copy-start(bf16[1536,256]{1,0:T(8,128)(2,1)} %constant.14.clone.tables) | copy-start | bytes 2359300
  0.7 9.7 %copy-start.14 = (f32[2,128,128]{2,1,0:T(8,128)S(1)}, f32[2,128,128]{2,1,0:T(8,128)}, u32[]{:S(2)}) copy-start(f32[2,128,128]{2,1,0:T(8,128)} %constant.16.clone.east_values) | copy-start | bytes 393220
  0.7 9.7 %copy-start.16 = (bf16[2,128,256]{2,1,0:T(8,128)(2,1)S(1)}, bf16[2,128,256]{2,1,0:T(8,128)(2,1)}, u32[]{:S(2)}) copy-start(bf16[2,128,256]{2,1,0:T(8,128)(2,1)} %constant.15.clone.east_table) | copy-start | bytes 393220
  3.4 11.5 %copy-start.7 = (f32[4,1024,128]{2,1,0:T(8,128)}, f32[4,1024,128]{2,1,0:T(8,128)S(1)}, u32[]{:S(2)}) copy-start(f32[4,1024,128]{2,1,0:T(8,128)S(1)} %get-tuple-element.27.fluid) | copy-start | bytes 6291460
  3.4 11.5 %copy-start.9 = (f32[4,1024,128]{2,1,0:T(8,128)}, f32[4,1024,128]{2,1,0:T(8,128)S(1)}, u32[]{:S(2)}) copy-start(f32[4,1024,128]{2,1,0:T(8,128)S(1)} %get-tuple-element.28.up) | copy-start | bytes 6291460
  3.4 11.5 %copy-start.21 = (f32[2,128,512]{2,1,0:T(8,128)}, f32[2,128,512]{2,1,0:T(8,128)S(1)}, u32[]{:S(2)}) copy-start(f32[2,128,512]{2,1,0:T(8,128)S(1)} %get-tuple-element.35.low) | copy-start | bytes 1572868
  3.4 11.6 %copy-start.1 = (f32[8,128,512]{2,1,0:T(8,128)}, f32[8,128,512]{2,1,0:T(8,128)S(1)}, u32[]{:S(2)}) copy-start(f32[8,128,512]{2,1,0:T(8,128)S(1)} %get-tuple-element.29.weights) | copy-start | bytes 6291460
  3.4 11.6 %copy-start.18 = (f32[128,512]{1,0:T(8,128)}, f32[128,512]{1,0:T(8,128)S(1)}, u32[]{:S(2)}) copy-start(f32[128,512]{1,0:T(8,128)S(1)} %get-tuple-element.34.high) | copy-start | bytes 786436
  3.4 11.6 %collective-permute-start = (f32[2,128,512]{2,1,0:T(8,128)S(1)}, f32[2,128,512]{2,1,0:T(8,128)S(1)}, u32[]{:S(2)}, u32[]{:S(2)}) collective-permute-start(f32[2,128,512]{2,1,0:T(8,128)S(1)} %get-tuple-element.35.low), channel_id=1, source_target_pairs={{4,0},{8,4},{12,8},{16,12},{20,16},{24,20},{28,24},{5,1},{9,5},{13... | collective-permute-start | bytes 1572872 | tf_op jit(solution)/shard_map/ppermute | solution.py:683
  5.5 9.5 %collective-permute-start.1 = (f32[16,512]{1,0:T(8,128)S(1)}, f32[16,512]{1,0:T(8,128)S(1)}, u32[]{:S(2)}, u32[]{:S(2)}) collective-permute-start(f32[16,512]{1,0:T(8,128)S(1)} %get-tuple-element.37), channel_id=1, source_target_pairs={{1,0},{2,1},{3,2},{0,3},{5,4},{6,5},{7,6},{4,7},{9,8},{10,9},{11,1... | collective-permute-start | bytes 98312 | tf_op jit(solution)/shard_map/ppermute | solution.py:684
  15.0 1.3 %copy-start.3 = (f32[8,128,512]{2,1,0:T(8,128)}, f32[8,128,512]{2,1,0:T(8,128)S(1)}, u32[]{:S(2)}) copy-start(f32[8,128,512]{2,1,0:T(8,128)S(1)} %get-tuple-element.30.modes) | copy-start | bytes 6291460
  15.0 1.3 %copy-start.26 = (f32[16,512]{1,0:T(8,128)}, f32[16,512]{1,0:T(8,128)S(1)}, u32[]{:S(2)}) copy-start(f32[16,512]{1,0:T(8,128)S(1)} %collective-permute-done.1.side_east) | copy-start | bytes 98308
  15.0 1.5 %copy-start.12 = (f32[2,128,512]{2,1,0:T(8,128)}, f32[2,128,512]{2,1,0:T(8,128)S(1)}, u32[]{:S(2)}) copy-start(f32[2,128,512]{2,1,0:T(8,128)S(1)} %collective-permute-done.low_above) | copy-start | bytes 1572868
  15.0 13.9 %copy-start.23 = (f32[192,128]{1,0:T(8,128)S(1)}, f32[192,128]{1,0:T(8,128)}, u32[]{:S(2)}) copy-start(f32[192,128]{1,0:T(8,128)} %constant.17.clone.pairs.rest_4_) | copy-start | bytes 294916
  16.5 0.8 %copy-start.20 = (f32[8,136,128]{2,1,0:T(8,128)}, f32[8,136,128]{2,1,0:T(8,128)S(1)}, u32[]{:S(2)}) copy-start(f32[8,136,128]{2,1,0:T(8,128)S(1)} %get-tuple-element.39) | copy-start | bytes 1671172
  17.3 0.7 copy-start.24
  18.0 11.0 %all-to-all-start = ((f32[8,136,128]{2,1,0:T(8,128)}), f32[8,136,128]{2,1,0:T(8,128)S(1)}, u32[]{:S(2)}, u32[]{:S(2)}) async-start(f32[8,136,128]{2,1,0:T(8,128)} %copy-done.20), calls=%async_computation | async-start | bytes 1114112 | tf_op jit(solution)/shard_map/all_to_all | solution.py:717
  22.0 14.4 %collective-permute-start.2 = (f32[128,512]{1,0:T(8,128)}, f32[128,512]{1,0:T(8,128)}, u32[]{:S(2)}, u32[]{:S(2)}) collective-permute-start(f32[128,512]{1,0:T(8,128)} %copy-done.18), channel_id=1, source_target_pairs={{0,4},{4,8},{8,12},{12,16},{16,20},{20,24},{24,28},{1,5},{5,9},{9,... | collective-permute-start | bytes 786440 | tf_op jit(solution)/shard_map/ppermute | solution.py:685
  29.0 0.9 %copy-start.28 = (bf16[128,512]{1,0:T(8,128)(2,1)S(1)}, bf16[128,512]{1,0:T(8,128)(2,1)}, u32[]{:S(2)}) copy-start(bf16[128,512]{1,0:T(8,128)(2,1)} %constant.19.clone.sums) | copy-start | bytes 393220
  29.9 0.8 %copy-start.29 = (bf16[128,64]{1,0:T(8,128)(2,1)S(1)}, bf16[128,64]{1,0:T(8,128)(2,1)}, u32[]{:S(2)}) copy-start(bf16[128,64]{1,0:T(8,128)(2,1)} %constant.20.clone.sines.rest_6_) | copy-start | bytes 49156
  30.6 0.8 %copy-start.31 = (f32[8,8,128]{2,1,0:T(8,128)S(1)}, f32[8,8,128]{2,1,0:T(8,128)}, u32[]{:S(2)}) copy-start(f32[8,8,128]{2,1,0:T(8,128)} %constant.18.clone.lam_b.rest_5_) | copy-start | bytes 98308
  31.4 25.9 %copy-start.2 = (f32[8,128,512]{2,1,0:T(8,128)S(1)}, f32[8,128,512]{2,1,0:T(8,128)}, u32[]{:S(2)}) copy-start(f32[8,128,512]{2,1,0:T(8,128)} %copy-done.1) | copy-start | bytes 6291460
  31.4 25.9 %copy-start.13 = (f32[2,128,512]{2,1,0:T(8,128)S(1)}, f32[2,128,512]{2,1,0:T(8,128)}, u32[]{:S(2)}) copy-start(f32[2,128,512]{2,1,0:T(8,128)} %copy-done.12) | copy-start | bytes 1572868
  31.4 25.9 %copy-start.15 = (f32[2,128,128]{2,1,0:T(8,128)S(1)}, f32[2,128,128]{2,1,0:T(8,128)}, u32[]{:S(2)}) copy-start(f32[2,128,128]{2,1,0:T(8,128)} %constant.16.clone.east_values) | copy-start | bytes 393220
  31.4 25.9 %copy-start.17 = (bf16[2,128,256]{2,1,0:T(8,128)(2,1)S(1)}, bf16[2,128,256]{2,1,0:T(8,128)(2,1)}, u32[]{:S(2)}) copy-start(bf16[2,128,256]{2,1,0:T(8,128)(2,1)} %constant.15.clone.east_table) | copy-start | bytes 393220
  31.4 25.9 %copy-start.19 = (f32[128,512]{1,0:T(8,128)S(1)}, f32[128,512]{1,0:T(8,128)}, u32[]{:S(2)}) copy-start(f32[128,512]{1,0:T(8,128)} %copy-done.18) | copy-start | bytes 786436
  31.4 25.9 %copy-start.25 = (f32[128,512]{1,0:T(8,128)S(1)}, f32[128,512]{1,0:T(8,128)}, u32[]{:S(2)}) copy-start(f32[128,512]{1,0:T(8,128)} %copy-done.24) | copy-start | bytes 786436
  32.2 5.8 %collective-permute-start.5 = (f32[96,128]{1,0:T(8,128)S(1)}, f32[96,128]{1,0:T(8,128)S(1)}, u32[]{:S(2)}, u32[]{:S(2)}) collective-permute-start(f32[96,128]{1,0:T(8,128)S(1)} %get-tuple-element.42), channel_id=1, source_target_pairs={{3,0},{0,1},{1,2},{2,3},{7,4},{4,5},{5,6},{6,7},{11,8},{8,9},{9,10... | collective-permute-start | bytes 147464 | tf_op jit(solution)/shard_map/ppermute | solution.py:730
  33.0 4.2 %collective-permute-start.4 = (f32[64,128]{1,0:T(8,128)S(1)}, f32[64,128]{1,0:T(8,128)S(1)}, u32[]{:S(2)}, u32[]{:S(2)}) collective-permute-start(f32[64,128]{1,0:T(8,128)S(1)} %get-tuple-element.41.rest_0_), channel_id=1, source_target_pairs={{2,0},{3,1},{0,2},{1,3},{6,4},{7,5},{4,6},{5,7},{10,8},{11,9},{8,1... | collective-permute-start | bytes 98312 | tf_op jit(solution)/shard_map/ppermute | solution.py:730
  35.3 2.8 %collective-permute-start.3 = (f32[64,128]{1,0:T(8,128)S(1)}, f32[64,128]{1,0:T(8,128)S(1)}, u32[]{:S(2)}, u32[]{:S(2)}) collective-permute-start(f32[64,128]{1,0:T(8,128)S(1)} %get-tuple-element.41.rest_0_), channel_id=1, source_target_pairs={{1,0},{2,1},{3,2},{0,3},{5,4},{6,5},{7,6},{4,7},{9,8},{10,9},{11,1... | collective-permute-start | bytes 98312 | tf_op jit(solution)/shard_map/ppermute | solution.py:730
  38.0 0.8 %copy-start.30 = (bf16[128,64]{1,0:T(8,128)(2,1)S(1)}, bf16[128,64]{1,0:T(8,128)(2,1)}, u32[]{:S(2)}) copy-start(bf16[128,64]{1,0:T(8,128)(2,1)} %constant.20.clone.sines.rest_6_) | copy-start | bytes 49156
  38.8 0.8 %copy-start.32 = (f32[8,8,128]{2,1,0:T(8,128)S(1)}, f32[8,8,128]{2,1,0:T(8,128)}, u32[]{:S(2)}) copy-start(f32[8,8,128]{2,1,0:T(8,128)} %constant.18.clone.lam_b.rest_5_) | copy-start | bytes 98308
  57.4 1.6 %copy-start.4 = (f32[8,128,512]{2,1,0:T(8,128)S(1)}, f32[8,128,512]{2,1,0:T(8,128)}, u32[]{:S(2)}) copy-start(f32[8,128,512]{2,1,0:T(8,128)} %copy-done.3) | copy-start | bytes 6291460
  59.0 1.6 %copy-start.6 = (f32[128,8,512]{2,1,0:T(8,128)S(1)}, f32[128,8,512]{2,1,0:T(8,128)}, u32[]{:S(2)}) copy-start(f32[128,8,512]{2,1,0:T(8,128)} %param.12) | copy-start | bytes 6291460
  60.5 1.6 %copy-start.8 = (f32[4,1024,128]{2,1,0:T(8,128)S(1)}, f32[4,1024,128]{2,1,0:T(8,128)}, u32[]{:S(2)}) copy-start(f32[4,1024,128]{2,1,0:T(8,128)} %copy-done.7) | copy-start | bytes 6291460
  62.1 1.6 %copy-start.10 = (f32[4,1024,128]{2,1,0:T(8,128)S(1)}, f32[4,1024,128]{2,1,0:T(8,128)}, u32[]{:S(2)}) copy-start(f32[4,1024,128]{2,1,0:T(8,128)} %copy-done.9) | copy-start | bytes 6291460
  63.7 1.0 %copy-start.22 = (f32[2,128,512]{2,1,0:T(8,128)S(1)}, f32[2,128,512]{2,1,0:T(8,128)}, u32[]{:S(2)}) copy-start(f32[2,128,512]{2,1,0:T(8,128)} %copy-done.21) | copy-start | bytes 1572868
  64.8 0.8 %copy-start.27 = (f32[16,512]{1,0:T(8,128)S(1)}, f32[16,512]{1,0:T(8,128)}, u32[]{:S(2)}) copy-start(f32[16,512]{1,0:T(8,128)} %copy-done.26) | copy-start | bytes 98308
